TPU v7x, 128 devices: a whole 4x4x4 slice. The times are simulated.
128 devices in a mesh: req: 8 (over y, core), hid: 16 (over x, z).
Axes of the slice: x: 4, y: 4, z: 4, core: 2. Of those that a mesh axis runs over, the one named last changes fastest.
Arguments:
- merged: bfloat16 [8, 256, 12800], P(None, 'req', 'hid')
- ln_gain: bfloat16 [12800], replicated, may hold values from 0.25 to 1.75
- ln_bias: bfloat16 [12800], replicated, may hold values from -3 to 3
- proj_weight: bfloat16 [12800, 6144], P(None, 'hid'), may hold values from -0.0546875 to 0.0546875
- proj_bias: float32 [6144], P('hid'), may hold values from -3 to 3
- text_embed: bfloat16 [16, 480, 6144], P('req', None, 'hid')
- attn_gain: bfloat16 [6144], replicated, may hold values from 0.25 to 1.75
- query_weight: bfloat16 [6144, 6144], P(None, 'hid')
- key_weight: bfloat16 [6144, 1024], P(None, 'hid')
- value_weight: bfloat16 [6144, 1024], P(None, 'hid'), may hold values from -0.078125 to 0.078125
- out_weight: bfloat16 [6144, 6144], P('hid'), may hold values from -0.078125 to 0.078125
- final_gain: bfloat16 [6144], replicated, may hold values from 0.25 to 1.75
- head_weight: bfloat16 [49152, 6144], P(('req', 'hid')), may hold values from -0.23925781 to 0.23925781
- lengths: int32 [16], P('req'), may hold values from 160 to 480, as said below
- tile_request: int32 [8], replicated, may hold values from 0 to 15, as said below
- insert_pos: int32 [8], replicated, may hold values from 0 to 224, as said below
Outputs:
- hidden: bfloat16 [16, 480, 6144], P('req', None, 'hid')
- final_norm: float32 [16], replicated
- logit_max: float32 [16], replicated
Inputs may be any that keep to these rules, and one draw needn't show every extreme that they name: For every g, the requests 2g and 2g + 1 have lengths that add up to exactly 640. `tile_request`: each pair of requests 2g, 2g + 1 holds exactly one tile, in the one of the two whose length is not smaller. insert_pos[t] + 256 is at most the length of request tile_request[t].
All inputs are finite; a program needn't handle non-finite values.
Results may differ from a plain program's by a relative error of at most 0.0095.
Values may be sent and summed in bfloat16 or wider, within the bound.
No kernel may reach another device: no remote copies, remote signals or barrier semaphores. Data moves between devices by JAX's collectives and lax.ppermute only.
A program may use at most 128 MiB of HBM per device.

v0:
```python
import math

import jax
import jax.numpy as jnp
from jax import lax
from jax.experimental import pallas as pl
from jax.experimental.pallas import tpu as pltpu
from jax.sharding import PartitionSpec as P

HEAD_DIM = 128
D = 6144
MERGED = 12800
REQ_GRP = 2
LEN_MAX = 480
LIVE = 640
TILE = 256
TEXT = LIVE - TILE
N_HID = 16
N_REQ = 8
RING = 4
FEAT = D // N_HID
MFEAT = MERGED // N_HID
MAIN = 768
MPAD = 896
BF = jnp.bfloat16
F32 = jnp.float32
VM = pltpu.VMEM


def vmem():
    return pl.BlockSpec(memory_space=pltpu.VMEM)


def params(mib):
    return pltpu.CompilerParams(vmem_limit_bytes=mib << 20)


def shift(block, dx, dz):
    route = []
    for i in range(N_HID):
        x, z = divmod(i, RING)
        route.append((((x + dx) % RING) * RING + (z + dz) % RING, i))
    return lax.ppermute(block, "hid", route)


def line_of(block, move):
    return [block, move(block, -1), move(block, 1), move(block, 2)]


def along_x(b, d):
    return shift(b, d, 0)


def along_z(b, d):
    return shift(b, 0, d)


def join(*blocks):
    total = blocks[0].astype(F32)
    for b in blocks[1:]:
        total = total + b.astype(F32)
    return total


def over_line(block, move):
    own, below, above, far = line_of(block, move)
    return (own + far) + (below + above)


def axes_of(first):
    return (along_z, along_x) if first == 0 else (along_x, along_z)


def gather_near(shard):
    half = shard.shape[0] // 2
    near = []
    for first in (0, 1):
        inner, outer = axes_of(first)
        own = lax.slice_in_dim(shard, first * half, (first + 1) * half, axis=0)
        group = jnp.concatenate(line_of(own, inner), axis=0)
        near.append((group, outer(group, -1), outer(group, 1)))
    return near


def gather_far(near):
    arrays, tables = [], []
    for first in (0, 1):
        _, outer = axes_of(first)
        group, minus, plus = near[first]
        half = group.shape[0] // RING
        far_a = outer(lax.slice_in_dim(minus, 0, 2 * half, axis=0), -1)
        far_b = outer(lax.slice_in_dim(plus, 2 * half, 4 * half, axis=0), 1)
        offs = [0, -1, 1, 2]
        table = {}
        for array, out, part in (
            (group, 0, offs),
            (minus, -1, offs),
            (plus, 1, offs),
            (far_a, 2, offs[:2]),
            (far_b, 2, offs[2:]),
        ):
            arrays.append(array)
            for j, d in enumerate(part):
                rel = (out % RING, d % RING) if first == 0 else (d % RING, out % RING)
                table[rel] = (len(arrays) - 1, j * half)
        tables.append(table)
    order = [(dx, dz) for dx in range(RING) for dz in range(RING)]
    return arrays, [(tables[0][r], tables[1][r]) for r in order]


def in_hbm(x):
    return pltpu.with_memory_space_constraint(x, pltpu.HBM)


def pack_kernel(order_ref, place_ref, x_ref, o_ref, tail):
    def step(g, carry):
        rows = x_ref[order_ref[g]]
        v = rows.astype(F32)
        here = pl.ds(pl.multiple_of(g * 32, 32), 32)
        lane = lax.broadcasted_iota(jnp.int32, (32, 128), 1)
        block = jnp.zeros((32, 128), F32)
        j = 32
        for s in (jnp.sum(v, axis=1, keepdims=True), jnp.sum(v * v, axis=1, keepdims=True)):
            for _ in range(3):
                part = s.astype(BF).astype(F32)
                block = jnp.where(lane == j, part, block)
                s = s - part
                j += 1
        o_ref[here, 0:MAIN] = rows[:, 0:MAIN]
        tail[here, :] = block
        tail[here, 0:32] = v[:, MAIN:MFEAT]
        return carry

    lax.fori_loop(0, N_REQ, step, 0)
    o_ref[:, MAIN:MPAD] = pltpu.roll(tail[...], place_ref[0] * 32, 1).astype(BF)


def pack(merged, tile_order, place):
    return pl.pallas_call(
        pack_kernel,
        out_shape=jax.ShapeDtypeStruct((TILE, MPAD), BF),
        in_specs=[pl.BlockSpec(memory_space=pltpu.SMEM)] * 2 + [vmem()],
        out_specs=vmem(),
        scratch_shapes=[VM((TILE, 128), F32)],
        compiler_params=params(16),
        name="pack",
    )(tile_order, place, merged)


def project_kernel(
    x_hbm, w_hbm, g_ref, b_ref, gl_ref, bl_ref, pb_ref, o_ref, tail, x, w, wl, acc, sem, x_sem, w_sem
):
    deep = 2 * MAIN
    tails = pltpu.make_async_copy(x_hbm.at[:, pl.ds(MAIN, 128)], tail, sem.at[0])
    lefts = pltpu.make_async_copy(w_hbm.at[:, pl.ds(MAIN, 32), :], wl, sem.at[1])

    def x_copy(k):
        here = pl.ds(pl.multiple_of(k * MAIN, MAIN), MAIN)
        there = x_hbm.at[pl.ds(k * TILE, TILE), pl.ds(0, MAIN)]
        return pltpu.make_async_copy(there, x.at[:, here], x_sem.at[k])

    def w_copy(k):
        here = pl.ds(k * MAIN, MAIN)
        return pltpu.make_async_copy(w_hbm.at[k, pl.ds(0, MAIN), :], w.at[here, :], w_sem.at[k])

    tails.start()
    for k in range(N_HID):
        x_copy(k).start()
        w_copy(k).start()
    lefts.start()
    tails.wait()
    quarter = lax.broadcasted_iota(jnp.int32, (TILE, 128), 1) // 32
    mean = jnp.zeros((TILE, 1), F32)
    square = jnp.zeros((TILE, 1), F32)
    for j in range(RING):
        total = jnp.zeros((TILE, 128), F32)
        for i in range(RING):
            k = RING * i + j
            total = total + tail[k * TILE : (k + 1) * TILE, :].astype(F32)
        at = 32 * ((j + 1) % RING)
        mean = mean + jnp.sum(total[:, at : at + 3], axis=1, keepdims=True)
        square = square + jnp.sum(total[:, at + 3 : at + 6], axis=1, keepdims=True)
    mean = mean * (1.0 / MERGED)
    rstd = lax.rsqrt(square * (1.0 / MERGED) - mean * mean + 1e-05)
    acc[...] = jnp.zeros_like(acc)

    def step(i, carry):
        for j in (0, 1):
            x_copy(2 * i + j).wait()
            w_copy(2 * i + j).wait()
        here = pl.ds(pl.multiple_of(i * deep, deep), deep)
        v = x[:, here].astype(F32)
        normed = (v - mean) * rstd * g_ref[i] + b_ref[i]
        acc[...] += jnp.dot(normed.astype(BF), w[here, :], preferred_element_type=F32)
        return carry

    lax.fori_loop(0, N_HID // 2, step, 0)
    lefts.wait()
    blocks = []
    for i in range(RING):
        v = jnp.zeros((TILE, 128), F32)
        for j in range(RING):
            k = RING * i + j
            v = jnp.where(quarter == j, tail[k * TILE : (k + 1) * TILE, :].astype(F32), v)
        blocks.append(((v - mean) * rstd * gl_ref[i] + bl_ref[i]).astype(BF))
    rest = jnp.concatenate(blocks, axis=1)
    y = acc[...] + pb_ref[...] + jnp.dot(
        rest, wl[...].reshape(N_HID * 32, FEAT), preferred_element_type=F32
    )
    y = 0.5 * y * (1.0 + lax.erf(y * math.sqrt(0.5)))
    o_ref[...] = y.astype(BF)


def project(gathered, weight, gain, bias, out_bias):
    def parts(v):
        v = v.astype(F32).reshape(N_HID, MFEAT)
        return (
            v[:, :MAIN].reshape(N_HID // 2, 1, 2 * MAIN),
            v[:, MAIN:].reshape(RING, 1, 128),
        )

    gain, gain_left = parts(gain)
    bias, bias_left = parts(bias)
    return pl.pallas_call(
        project_kernel,
        out_shape=jax.ShapeDtypeStruct((TILE, FEAT), BF),
        in_specs=[pl.BlockSpec(memory_space=pl.ANY)] * 2 + [vmem()] * 5,
        out_specs=vmem(),
        scratch_shapes=[
            VM((N_HID * TILE, 128), BF),
            VM((TILE, N_HID * MAIN), BF),
            VM((N_HID * MAIN, FEAT), BF),
            VM((N_HID, 32, FEAT), BF),
            VM((TILE, FEAT), F32),
            pltpu.SemaphoreType.DMA((2,)),
            pltpu.SemaphoreType.DMA((N_HID,)),
            pltpu.SemaphoreType.DMA((N_HID,)),
        ],
        compiler_params=params(30),
        cost_estimate=pl.CostEstimate(
            flops=2 * TILE * MERGED * FEAT, bytes_accessed=17 << 20, transcendentals=0
        ),
        name="project",
    )(
        in_hbm(gathered),
        in_hbm(weight.reshape(N_HID, MFEAT, FEAT)),
        gain,
        bias,
        gain_left,
        bias_left,
        out_bias,
    )


def turn(v, cos, sin):
    return v * cos + pltpu.roll(v, HEAD_DIM // 2, 1) * sin


def qkv(arrays, where, weight, cos, sin, sources, name):
    half = arrays[0].shape[0] // RING
    rows = 2 * half
    n = len(arrays)
    deep = 2 * FEAT
    cols = FEAT + HEAD_DIM

    def kernel(src_ref, *refs):
        ins = refs[:n]
        w_hbm, cos_ref, sin_ref, q_ref, kv_ref, xs, w, acc, sq, sem = refs[n:]

        def copy(k):
            there = pl.ds(pl.multiple_of(src_ref[k] * FEAT, FEAT), FEAT)
            here = pl.ds(k * FEAT, FEAT)
            return pltpu.make_async_copy(w_hbm.at[there, :], w.at[here, :], sem.at[k])

        for k in range(N_HID):
            copy(k).start()
        for k in range(N_HID):
            block = jnp.concatenate([ins[a][row : row + half, :] for a, row in where[k]], axis=0)
            xs[:, k * FEAT : (k + 1) * FEAT] = block
        acc[...] = jnp.zeros_like(acc)
        sq[...] = jnp.zeros_like(sq)

        def step(i, carry):
            for j in range(2):
                copy(2 * i + j).wait()
            here = pl.ds(pl.multiple_of(i * deep, deep), deep)
            acc[...] += jnp.dot(xs[:, here], w[here, :], preferred_element_type=F32)
            v = xs[:, here].astype(F32)
            v = v * v
            sq[...] += sum(v[:, c : c + 128] for c in range(0, deep, 128))
            return carry

        lax.fori_loop(0, N_HID // 2, step, 0)
        scale = lax.rsqrt(jnp.sum(sq[...], axis=1, keepdims=True) * (1.0 / D) + 1e-05)
        for h in range(FEAT // HEAD_DIM):
            part = acc[:, h * HEAD_DIM : (h + 1) * HEAD_DIM] * scale
            q_ref[:, h * HEAD_DIM : (h + 1) * HEAD_DIM] = turn(
                part, cos_ref[...], sin_ref[...]
            ).astype(BF)
        kv_ref[...] = (acc[:, FEAT:] * scale).astype(BF)

    return pl.pallas_call(
        kernel,
        out_shape=(
            jax.ShapeDtypeStruct((rows, FEAT), BF),
            jax.ShapeDtypeStruct((rows, HEAD_DIM), BF),
        ),
        in_specs=[pl.BlockSpec(memory_space=pltpu.SMEM)]
        + [vmem() for _ in arrays]
        + [pl.BlockSpec(memory_space=pl.ANY), vmem(), vmem()],
        out_specs=(vmem(), vmem()),
        scratch_shapes=[
            VM((rows, D), BF),
            VM((D, cols), BF),
            VM((rows, cols), F32),
            VM((rows, HEAD_DIM), F32),
            pltpu.SemaphoreType.DMA((N_HID,)),
        ],
        compiler_params=params(20),
        cost_estimate=pl.CostEstimate(
            flops=2 * rows * D * cols, bytes_accessed=12 << 20, transcendentals=0
        ),
        name=name,
    )(sources, *arrays, in_hbm(weight), cos, sin)


def attend_kernel(
    low_ref, qt, qi, ot, pt, oi, pi, cos_ref, sin_ref, row_ref, col_ref, o_ref, qs, keys, vals
):
    upper = low_ref[0] == 0
    lane = lax.broadcasted_iota(jnp.int32, (LIVE, HEAD_DIM), 1)
    own = jnp.concatenate([ot[...], oi[...]], axis=0).astype(F32)
    other = jnp.concatenate([pt[...], pi[...]], axis=0).astype(F32)
    low = jnp.where(upper, other, own)
    high = jnp.where(upper, own, other)
    key = jnp.where(lane < 64, low, pltpu.roll(high, 64, 1))
    val = jnp.where(lane < 64, pltpu.roll(low, 64, 1), high)
    keys[...] = turn(key, cos_ref[...], sin_ref[...]).astype(BF)
    vals[...] = val.astype(BF)
    qs[:TEXT] = qt[...]
    qs[TEXT:] = qi[...]
    code = col_ref[...]

    def block(i, carry):
        rows = pl.ds(pl.multiple_of(i * 128, 128), 128)
        mine = row_ref[rows, :]
        start = jnp.where(mine >= 1024, 1024, 0)
        live = jnp.logical_and(code <= mine, code >= start)
        for h in range(FEAT // HEAD_DIM):
            cols = slice(h * HEAD_DIM, (h + 1) * HEAD_DIM)
            s = lax.dot_general(
                qs[rows, cols], keys[...], (((1,), (1,)), ((), ())), preferred_element_type=F32
            ) * (1.0 / math.sqrt(HEAD_DIM))
            s = jnp.where(live, s, -jnp.inf)
            w = jnp.exp(s - jnp.max(s, axis=1, keepdims=True))
            total = jnp.sum(w, axis=1, keepdims=True)
            mixed = jnp.dot(w.astype(BF), vals[...], preferred_element_type=F32)
            o_ref[rows, cols] = (mixed / total).astype(BF)
        return carry

    lax.fori_loop(0, LIVE // 128, block, 0)


def attend(low, qt, qi, ot, pt, oi, pi, cos, sin, code):
    return pl.pallas_call(
        attend_kernel,
        out_shape=jax.ShapeDtypeStruct((LIVE, FEAT), BF),
        in_specs=[pl.BlockSpec(memory_space=pltpu.SMEM)] + [vmem()] * 10,
        out_specs=vmem(),
        scratch_shapes=[VM((LIVE, FEAT), BF), VM((LIVE, HEAD_DIM), BF), VM((LIVE, HEAD_DIM), BF)],
        compiler_params=params(24),
        cost_estimate=pl.CostEstimate(flops=1 << 30, bytes_accessed=2 << 20, transcendentals=0),
        name="attend",
    )(low, qt, qi, ot, pt, oi, pi, cos, sin, code[:, None], code[None, :])


def spread_kernel(a_ref, w_hbm, o_ref, w, sem):
    k = pl.program_id(0)
    two = 2 * FEAT

    def copy(i):
        cols = pl.ds(pl.multiple_of(i * two, two), two)
        return pltpu.make_async_copy(w_hbm.at[:, cols], w.at[i], sem.at[i])

    @pl.when(k == 0)
    def _():
        for i in range(N_HID // 2):
            copy(i).start()

    copy(k).wait()
    product = jnp.dot(a_ref[...], w[k], preferred_element_type=F32).astype(BF)
    o_ref[0] = product[:, :FEAT]
    o_ref[1] = product[:, FEAT:]


def spread(attended, weight):
    return pl.pallas_call(
        spread_kernel,
        out_shape=jax.ShapeDtypeStruct((N_HID, LIVE, FEAT), BF),
        grid=(N_HID // 2,),
        in_specs=[
            pl.BlockSpec(memory_space=pltpu.VMEM),
            pl.BlockSpec(memory_space=pl.ANY),
        ],
        out_specs=pl.BlockSpec((2, LIVE, FEAT), lambda k: (k, 0, 0)),
        scratch_shapes=[
            VM((N_HID // 2, FEAT, 2 * FEAT), BF),
            pltpu.SemaphoreType.DMA((N_HID // 2,)),
        ],
        compiler_params=params(58),
        cost_estimate=pl.CostEstimate(
            flops=2 * LIVE * FEAT * D, bytes_accessed=13 << 20, transcendentals=0
        ),
        name="spread",
    )(attended, in_hbm(weight))


def finish_kernel(text_ref, tile_ref, sum_ref, slot_ref, o_ref):
    def one(r, carry):
        row = slot_ref[r]
        pick = (lax.broadcasted_iota(jnp.int32, (LEN_MAX, LIVE), 1) == row).astype(BF)
        moved = jnp.dot(pick, sum_ref[...], preferred_element_type=F32)
        image = jnp.dot(pick[:, TEXT:], tile_ref[...], preferred_element_type=F32)
        base = jnp.where(row >= TEXT, image, text_ref[r].astype(F32))
        o_ref[r] = (base + moved).astype(BF)
        return carry

    lax.fori_loop(0, REQ_GRP, one, 0)


def finish(text, tile, sums, slots):
    return pl.pallas_call(
        finish_kernel,
        out_shape=jax.ShapeDtypeStruct((REQ_GRP, LEN_MAX, FEAT), BF),
        in_specs=[vmem()] * 4,
        out_specs=vmem(),
        compiler_params=params(24),
        name="finish",
    )(text, tile, sums, slots)


def shards(
    merged,
    ln_gain,
    ln_bias,
    proj_weight,
    proj_bias,
    text_embed,
    attn_gain,
    query_weight,
    key_weight,
    value_weight,
    out_weight,
    final_gain,
    head_weight,
    lengths,
    tile_request,
    insert_pos,
):
    hid = lax.axis_index("hid")
    me = lax.axis_index("req")
    owners = tile_request // REQ_GRP
    tiles = jnp.arange(N_REQ, dtype=jnp.int32)
    tile_order = jnp.sum(
        jnp.where(owners[None, :] == tiles[:, None], tiles[None, :], 0), axis=1
    ).astype(jnp.int32)
    mine = owners == me
    local_req = jnp.sum(jnp.where(mine, tile_request % REQ_GRP, 0))
    start = jnp.sum(jnp.where(mine, insert_pos, 0))
    len_a = lengths[0]
    first = local_req * len_a + start

    n = jnp.arange(LIVE, dtype=jnp.int32)
    packed = jnp.where(n < TEXT, jnp.where(n < first, n, n + TILE), n - TEXT + first)
    second = packed >= len_a
    pos = packed - jnp.where(second, len_a, 0)
    code = pos + jnp.where(second, 1024, 0)
    flat = pos + jnp.where(second, LEN_MAX, 0)
    slot = jnp.arange(LEN_MAX, dtype=jnp.int32)
    at = jnp.stack([slot, slot + len_a])
    in_tile = jnp.logical_and(at >= first, at < first + TILE)
    row_of = jnp.where(in_tile, at - first + TEXT, jnp.where(at < first, at, at - TILE))
    row_of = jnp.where(slot[None, :] < lengths[:, None], row_of, -1)

    half_dim = HEAD_DIM // 2
    inv_freq = jnp.exp(
        jnp.arange(half_dim, dtype=F32) * (-2.0 * math.log(1000000.0) / HEAD_DIM)
    )
    angles = pos.astype(F32)[:, None] * inv_freq[None, :]
    cosine, sine = jnp.cos(angles), jnp.sin(angles)
    cos = jnp.concatenate([cosine, cosine], axis=1)
    sin = jnp.concatenate([-sine, sine], axis=1)

    x, z = hid // RING, hid % RING
    rel = jnp.arange(N_HID, dtype=jnp.int32)
    sources = ((x + rel // RING) % RING) * RING + (z + rel % RING) % RING

    gathered = lax.all_gather(pack(merged, tile_order, (hid % RING)[None]), "hid", axis=0, tiled=True)

    pick = (flat[:TEXT, None] == jnp.arange(REQ_GRP * LEN_MAX)[None, :]).astype(BF)
    text_rows = jnp.dot(
        pick, text_embed.reshape(REQ_GRP * LEN_MAX, FEAT), preferred_element_type=F32
    ).astype(BF)
    weight = (
        jnp.concatenate([query_weight, key_weight, value_weight], axis=1).astype(F32)
        * attn_gain.astype(F32)[:, None]
    ).astype(BF)
    partner = [(i, i ^ 1) for i in range(N_HID)]
    text_blocks, text_where = gather_far(gather_near(text_rows))
    q_text, kv_text = qkv(
        text_blocks, text_where, weight, cos[:TEXT], sin[:TEXT], sources, "qkv_text"
    )
    gathered, q_text, kv_text = lax.optimization_barrier((gathered, q_text, kv_text))
    projected = project(
        gathered,
        proj_weight,
        ln_gain,
        ln_bias,
        proj_bias[None, :],
    )
    tile = lax.all_to_all(
        projected.reshape(N_REQ, TILE // N_REQ, FEAT), "req", split_axis=0, concat_axis=0, tiled=True
    ).reshape(TILE, FEAT)
    other_text = lax.ppermute(kv_text, "hid", partner)
    tile_blocks, tile_where = gather_far(gather_near(tile))
    q_tile, kv_tile = qkv(
        tile_blocks, tile_where, weight, cos[TEXT:], sin[TEXT:], sources, "qkv_tile"
    )
    other_tile = lax.ppermute(kv_tile, "hid", partner)

    low = (hid % 2 == 0).astype(jnp.int32)[None]
    attended = attend(
        low, q_text, q_tile, kv_text, other_text, kv_tile, other_tile, cos, sin, code
    )
    partial = spread(attended, out_weight)
    partial, attended = lax.optimization_barrier((partial, attended))
    sums = lax.psum_scatter(
        partial.reshape(N_HID * LIVE, FEAT), "hid", scatter_dimension=0, tiled=True
    )
    hidden = finish(text_embed, tile, sums, row_of[:, :, None])

    last = jnp.sum(jnp.where(slot[None, :] == lengths[:, None] - 1, row_of, 0), axis=1)
    pick_last = (last[:, None] == n[None, :]).astype(BF)
    rows_last = jnp.dot(pick_last, attended, preferred_element_type=F32).astype(BF)
    term = jnp.dot(rows_last, out_weight, preferred_element_type=F32)
    base = jnp.dot(pick_last[:, :TEXT], text_rows, preferred_element_type=F32) + jnp.dot(
        pick_last[:, TEXT:], tile, preferred_element_type=F32
    )
    spot = lax.broadcasted_iota(jnp.int32, (1, N_HID, 1), 1) == hid
    term = term + jnp.where(spot, base[:, None, :], 0.0).reshape(REQ_GRP, D)
    term = over_line(term, along_z)
    full_width = over_line(term, along_x).astype(BF)
    all_last = lax.all_gather(full_width, "req", axis=0, tiled=True)
    last_values = all_last.astype(F32)
    last_squares = jnp.sum(last_values * last_values, axis=1)
    final_norm = jnp.sqrt(last_squares)
    final_scaled = (
        last_values * lax.rsqrt(last_squares / D + 1e-05)[:, None] * final_gain.astype(F32)
    ).astype(BF)
    logits = lax.dot_general(
        final_scaled, head_weight, (((1,), (1,)), ((), ())), preferred_element_type=F32
    )
    top = jnp.max(logits, axis=1)
    for move in (along_z, along_x):
        here, below, above, far_top = line_of(top, move)
        top = jnp.maximum(jnp.maximum(here, below), jnp.maximum(above, far_top))
    logit_max = lax.pmax(top, "req")
    return (hidden, final_norm, logit_max)


def solution(mesh):
    return jax.shard_map(
        shards,
        mesh=mesh,
        in_specs=(
            P(None, "req", "hid"),
            P(),
            P(),
            P(None, "hid"),
            P("hid"),
            P("req", None, "hid"),
            P(),
            P(None, "hid"),
            P(None, "hid"),
            P(None, "hid"),
            P("hid", None),
            P(),
            P(("req", "hid"), None),
            P("req"),
            P(),
            P(),
        ),
        out_specs=(P("req", None, "hid"), P(), P()),
        check_vma=False,
    )
```

profile of v0, /device:TPU:1, one launch (start us, length us, event | category | flops | bytes accessed | tf_op | source)
XLA Modules:
  0.0 269.1 jit_solution(6741347456578336811)
XLA Ops:
  9.7 2.2 pack.1
  14.6 1.7 fusion.1
  17.1 2.1 collective-permute-start.7
  20.6 1.6 collective-permute-start.9
  22.2 1.6 collective-permute-start
  23.9 2.1 collective-permute-start.1
  26.0 1.5 collective-permute-start.2
  27.5 2.5 copy.39
  32.4 1.9 collective-permute-start.11
  34.4 1.7 collective-permute-done.2
  36.2 2.7 collective-permute-start.4
  38.9 8.7 %multiply_convert_fusion.refs_10_ = bf16[6144,512]{1,0:T(8,128)(2,1)} fusion(bf16[6144,64]{1,0:T(8,128)(2,1)} %copy.40, bf16[6144,64]{1,0:T(8,128)(2,1)} %copy.39, bf16[6144,384]{1,0:T(8,128)(2,1)} %param.23, f32[6144]{0:T(1024)S(1)} %convert_element_type.41), kind=kLoop, calls=%fused_computation | loop fusion | flops 25165824 | bytes 12607488 | tf_op jit(solution)/shard_map/convert_element_type | solution.py:507
  62.3 1.6 collective-permute-start.13
  64.1 2.9 %collective-permute-start.6 = (bf16[384,384]{1,0:T(8,128)(2,1)S(1)}, bf16[384,384]{1,0:T(8,128)(2,1)S(1)}, u32[]{:S(2)}, u32[]{:S(2)}) collective-permute-start(bf16[384,384]{1,0:T(8,128)(2,1)S(1)} %slice.106), channel_id=1, source_target_pairs={{4,0},{5,1},{6,2},{7,3},{8,4},{9,5},{10,6},{11,7},{12,8},{13,9},{1... | collective-permute-start | bytes 884744 | tf_op jit(solution)/shard_map/ppermute | solution.py:43
  67.2 7.8 %collective-permute-done.12.refs_8_ = bf16[384,384]{1,0:T(8,128)(2,1)S(1)} collective-permute-done((bf16[384,384]{1,0:T(8,128)(2,1)S(1)}, bf16[384,384]{1,0:T(8,128)(2,1)S(1)}, u32[]{:S(2)}, u32[]{:S(2)}) %collective-permute-start.12) | collective-permute-done | bytes 294944 | tf_op jit(solution)/shard_map/ppermute | solution.py:43
  75.1 2.7 collective-permute-done.5.refs_3_
  77.8 7.4 %qkv_text.1 = (bf16[384,384]{1,0:T(8,128)(2,1)S(1)}, bf16[384,128]{1,0:T(8,128)(2,1)S(1)}) custom-call(s32[16]{0:T(128)S(1)} %fusion.22.src_ref, bf16[768,384]{1,0:T(8,128)(2,1)S(1)} %pad_maximum_fusion.refs_0_, bf16[768,384]{1,0:T(8,128)(2,1)S(1)} %collective-permute-done.3.refs_1_, bf16[768,384]{1,0:T(8,128)(2,1)S(1)} %collective-permute-done.4.refs_2_, ...), custom_call_target="tpu_custom_call" | custom-call | flops 2415919104 | bytes 12582912 | tf_op jit(solution)/shard_map/qkv_text/pallas_call | solution.py:302
  86.5 6.2 %all-gather.3.cloned.1.call-done.x_hbm = bf16[4096,896]{1,0:T(8,128)(2,1)} async-done(((bf16[256,896]{1,0:T(8,128)(2,1)}), bf16[4096,896]{1,0:T(8,128)(2,1)}) %all-gather.3.cloned.1.call-update) | async-done | bytes 7340048 | tf_op jit(solution)/shard_map/all_gather | solution.py:498
  94.3 11.6 %project.1 = bf16[256,384]{1,0:T(8,128)(2,1)S(1)} custom-call(bf16[4096,896]{1,0:T(8,128)(2,1)} %all-gather.3.cloned.1.call-done.x_hbm, bf16[16,800,384]{2,1,0:T(8,128)(2,1)} %bitcast.29, f32[8,1,1536]{2,1,0:T(1,128)S(1)} %copy-done.5, f32[8,1,1536]{2,1,0:T(1,128)S(1)} %copy-done.6, f32[4,1,128]{2,1,0:T(1,128)S(1)} %reshape.333.gl_ref, ...), custom_call_target="tpu_custom_call" | custom-call | flops 2516582400 | bytes 17825792 | tf_op jit(solution)/shard_map/project/pallas_call | solution.py:224
  106.0 12.8 %all_to_all.5 = bf16[8,32,384]{2,1,0:T(8,128)(2,1)S(1)} all-to-all(bf16[8,32,384]{2,1,0:T(8,128)(2,1)S(1)} %bitcast.26), channel_id=1, replica_groups=mesh['req'=8,'hid'=16] {'req'}, dimensions={0} | all-to-all | bytes 393216 | tf_op jit(solution)/shard_map/all_to_all | solution.py:521
  118.9 3.2 %collective-permute-start.22 = (bf16[128,384]{1,0:T(8,128)(2,1)S(1)}, bf16[128,384]{1,0:T(8,128)(2,1)S(1)}, u32[]{:S(2)}, u32[]{:S(2)}) collective-permute-start(bf16[128,384]{1,0:T(8,128)(2,1)S(1)} %bitcast.35), channel_id=1, source_target_pairs={{4,0},{5,1},{6,2},{7,3},{8,4},{9,5},{10,6},{11,7},{12,8},{13,9},{1... | collective-permute-start | bytes 294920 | tf_op jit(solution)/shard_map/ppermute | solution.py:43
  123.2 2.7 collective-permute-start.15
  125.9 1.8 collective-permute-done.23
  127.8 2.7 collective-permute-start.25
  131.9 1.8 collective-permute-start.18
  136.0 3.5 %collective-permute-done.24.refs_6_ = bf16[512,384]{1,0:T(8,128)(2,1)S(1)} collective-permute-done((bf16[512,384]{1,0:T(8,128)(2,1)S(1)}, bf16[512,384]{1,0:T(8,128)(2,1)S(1)}, u32[]{:S(2)}, u32[]{:S(2)}) %collective-permute-start.24) | collective-permute-done | bytes 393248 | tf_op jit(solution)/shard_map/ppermute | solution.py:43
  139.6 2.7 %collective-permute-start.27 = (bf16[256,384]{1,0:T(8,128)(2,1)S(1)}, bf16[256,384]{1,0:T(8,128)(2,1)S(1)}, u32[]{:S(2)}, u32[]{:S(2)}) collective-permute-start(bf16[256,384]{1,0:T(8,128)(2,1)S(1)} %slice.123), channel_id=1, source_target_pairs={{1,0},{2,1},{3,2},{0,3},{5,4},{6,5},{7,6},{4,7},{9,8},{10,9},{11,1... | collective-permute-start | bytes 589832 | tf_op jit(solution)/shard_map/ppermute | solution.py:43
  143.0 2.3 collective-permute-start.20
  145.6 2.6 collective-permute-done.19.refs_3_
  148.2 5.8 %qkv_tile.1 = (bf16[256,384]{1,0:T(8,128)(2,1)S(1)}, bf16[256,128]{1,0:T(8,128)(2,1)S(1)}) custom-call(s32[16]{0:T(128)S(1)} %fusion.22.src_ref, bf16[512,384]{1,0:T(8,128)(2,1)S(1)} %pad_maximum_fusion.2.refs_0_, bf16[512,384]{1,0:T(8,128)(2,1)S(1)} %collective-permute-done.17.refs_1_, bf16[512,384]{1,0:T(8,128)(2,1)S(1)} %collective-permute-done.18.refs_2_, ...), custom_call_target="tpu_custom_call" | custom-call | flops 1610612736 | bytes 12582912 | tf_op jit(solution)/shard_map/qkv_tile/pallas_call | solution.py:302
  154.4 3.0 %collective-permute-done.29.pi = bf16[256,128]{1,0:T(8,128)(2,1)S(1)} collective-permute-done((bf16[256,128]{1,0:T(8,128)(2,1)S(1)}, bf16[256,128]{1,0:T(8,128)(2,1)S(1)}, u32[]{:S(2)}, u32[]{:S(2)}) %collective-permute-start.29) | collective-permute-done | bytes 65568 | tf_op jit(solution)/shard_map/ppermute | solution.py:529
  157.4 5.8 %attend.1.a_ref = bf16[640,384]{1,0:T(8,128)(2,1)S(1)} custom-call(s32[1]{0:T(128)} %bitcast.6.low_ref, bf16[384,384]{1,0:T(8,128)(2,1)S(1)} %copy-done.8, bf16[256,384]{1,0:T(8,128)(2,1)S(1)} %get-tuple-element.16.qi, bf16[384,128]{1,0:T(8,128)(2,1)S(1)} %copy-done.10, bf16[384,128]{1,0:T(8,128)(2,1)S(1)} %collective-permute-done.28.pt, ...), custom_call_target="tpu_custom_call" | custom-call | flops 1073741824 | bytes 2097152 | tf_op jit(solution)/shard_map/attend/pallas_call | solution.py:365
  164.1 9.5 %spread.1 = bf16[16,640,384]{2,1,0:T(8,128)(2,1)} custom-call(bf16[640,384]{1,0:T(8,128)(2,1)} %copy-done, bf16[384,6144]{1,0:T(8,128)(2,1)} %w_hbm.1), custom_call_target="tpu_custom_call" | custom-call | flops 3019898880 | bytes 13631488 | tf_op jit(solution)/shard_map/spread/pallas_call | solution.py:397
  174.9 3.2 %convolution_add_fusion = f32[2,6144]{1,0:T(2,128)S(1)} fusion(bf16[384,6144]{1,0:T(8,128)(2,1)} %w_hbm.1, bf16[640,384]{1,0:T(8,128)(2,1)S(1)} %copy-done.1, f32[2,6144]{1,0:T(2,128)S(1)} %bitcast.38, pred[6144]{0:T(1024)(128)(4,1)S(1)} %broadcast_in_dim.119, s32[2]{0:T(128)S(1)} %fusion.15), kind=kOutput, calls=%fused_computation.1 | convolution fusion | flops 10446848 | bytes 5314568 | tf_op jit(solution)/shard_map/dot_general | solution.py:545
  178.8 2.2 collective-permute-start.32
  181.1 1.6 collective-permute-done.30
  183.0 1.7 collective-permute-start.33
  184.7 1.8 collective-permute-start.34
  187.8 2.1 collective-permute-done.34
  190.4 21.1 %all-gather = bf16[8,2,6144]{2,1,0:T(2,128)(2,1)S(1)} all-gather(bf16[1,2,6144]{2,1,0:T(2,128)(2,1)S(1)} %fusion.12), channel_id=1, replica_groups=mesh['req'=8,'hid'=16] {'req'}, dimensions={0}, use_global_device_ids=true | all-gather | bytes 221184 | tf_op jit(solution)/shard_map/all_gather | solution.py:553
  212.3 3.8 %convolution_reduce_fusion = f32[16]{0:T(128)S(1)} fusion(bf16[384,6144]{1,0:T(8,128)(2,1)} %param.28, f32[16,6144]{1,0:T(8,128)S(1)} %reshape.345, f32[6144]{0:T(1024)S(1)} %convert_element_type.47, f32[16]{0:T(128)S(1)} %get-tuple-element.31), kind=kOutput, calls=%fused_computation.6 | convolution fusion | flops 75798512 | bytes 5136512 | tf_op jit(solution)/shard_map/dot_general | solution.py:560
  216.1 1.7 collective-permute-start.36
  220.5 2.3 collective-permute-done.38
  222.8 2.7 collective-permute-start.40
  226.4 3.0 %collective-permute-done.41 = f32[16]{0:T(128)S(1)} collective-permute-done((f32[16]{0:T(128)S(1)}, f32[16]{0:T(128)S(1)}, u32[]{:S(2)}, u32[]{:S(2)}) %collective-permute-start.41) | collective-permute-done | bytes 96 | tf_op jit(solution)/shard_map/ppermute | solution.py:43
  229.4 15.9 %pmax.7 = f32[16]{0:T(128)} all-reduce(f32[16]{0:T(128)S(1)} %maximum_maximum_fusion), channel_id=1, replica_groups=mesh['req'=8,'hid'=16] {'req'}, use_global_device_ids=true, to_apply=%region_7.8 | all-reduce | flops 16 | bytes 128 | tf_op jit(solution)/shard_map/pmax | solution.py:567
  245.3 13.6 %reduce-scatter.2.cloned.1.call-done.sum_ref = bf16[640,384]{1,0:T(8,128)(2,1)} async-done(((bf16[10240,384]{1,0:T(8,128)(2,1)}), bf16[640,384]{1,0:T(8,128)(2,1)}) %reduce-scatter.2.cloned.1.call-update) | async-done | bytes 491536 | tf_op jit(solution)/shard_map/reduce_scatter | solution.py:537
  260.0 2.3 finish.1
  (167 shorter events, 42.7 us)
Async XLA Ops:
  7.2 85.6 %all-gather.3.cloned.1.call-start = ((), (), s32[]{:S(2)}) async-start(), calls=%async_computation.2 | async-start | bytes 7798784 | tf_op jit(solution)/shard_map/all_gather | solution.py:498
  12.0 247.0 %reduce-scatter.2.cloned.1.call-start = ((), (), s32[]{:S(2)}) async-start(), calls=%async_computation.3 | async-start | bytes 8355840 | tf_op jit(solution)/shard_map/reduce_scatter | solution.py:537
  17.1 8.9 %collective-permute-start.7 = (bf16[192,384]{1,0:T(8,128)(2,1)S(1)}, bf16[192,384]{1,0:T(8,128)(2,1)S(1)}, u32[]{:S(2)}, u32[]{:S(2)}) collective-permute-start(bf16[192,384]{1,0:T(8,128)(2,1)S(1)} %get-tuple-element.24), channel_id=1, source_target_pairs={{12,0},{13,1},{14,2},{15,3},{0,4},{1,5},{2,6},{3,7},{4,8},{5,9},{6... | collective-permute-start | bytes 442376 | tf_op jit(solution)/shard_map/ppermute | solution.py:43
  19.2 12.3 %collective-permute-start.8 = (bf16[192,384]{1,0:T(8,128)(2,1)S(1)}, bf16[192,384]{1,0:T(8,128)(2,1)S(1)}, u32[]{:S(2)}, u32[]{:S(2)}) collective-permute-start(bf16[192,384]{1,0:T(8,128)(2,1)S(1)} %get-tuple-element.24), channel_id=1, source_target_pairs={{4,0},{5,1},{6,2},{7,3},{8,4},{9,5},{10,6},{11,7},{12,8},{13,9},{1... | collective-permute-start | bytes 442376 | tf_op jit(solution)/shard_map/ppermute | solution.py:43
  20.6 11.0 %collective-permute-start.9 = (bf16[192,384]{1,0:T(8,128)(2,1)S(1)}, bf16[192,384]{1,0:T(8,128)(2,1)S(1)}, u32[]{:S(2)}, u32[]{:S(2)}) collective-permute-start(bf16[192,384]{1,0:T(8,128)(2,1)S(1)} %get-tuple-element.24), channel_id=1, source_target_pairs={{8,0},{9,1},{10,2},{11,3},{12,4},{13,5},{14,6},{15,7},{0,8},{1,9},... | collective-permute-start | bytes 442376 | tf_op jit(solution)/shard_map/ppermute | solution.py:43
  22.2 12.2 %collective-permute-start = (bf16[192,384]{1,0:T(8,128)(2,1)S(1)}, bf16[192,384]{1,0:T(8,128)(2,1)S(1)}, u32[]{:S(2)}, u32[]{:S(2)}) collective-permute-start(bf16[192,384]{1,0:T(8,128)(2,1)S(1)} %get-tuple-element.25), channel_id=1, source_target_pairs={{3,0},{0,1},{1,2},{2,3},{7,4},{4,5},{5,6},{6,7},{11,8},{8,9},{9,10... | collective-permute-start | bytes 442376 | tf_op jit(solution)/shard_map/ppermute | solution.py:43
  23.9 10.5 %collective-permute-start.1 = (bf16[192,384]{1,0:T(8,128)(2,1)S(1)}, bf16[192,384]{1,0:T(8,128)(2,1)S(1)}, u32[]{:S(2)}, u32[]{:S(2)}) collective-permute-start(bf16[192,384]{1,0:T(8,128)(2,1)S(1)} %get-tuple-element.25), channel_id=1, source_target_pairs={{1,0},{2,1},{3,2},{0,3},{5,4},{6,5},{7,6},{4,7},{9,8},{10,9},{11,1... | collective-permute-start | bytes 442376 | tf_op jit(solution)/shard_map/ppermute | solution.py:43
  26.0 10.1 %collective-permute-start.2 = (bf16[192,384]{1,0:T(8,128)(2,1)S(1)}, bf16[192,384]{1,0:T(8,128)(2,1)S(1)}, u32[]{:S(2)}, u32[]{:S(2)}) collective-permute-start(bf16[192,384]{1,0:T(8,128)(2,1)S(1)} %get-tuple-element.25), channel_id=1, source_target_pairs={{2,0},{3,1},{0,2},{1,3},{6,4},{7,5},{4,6},{5,7},{10,8},{11,9},{8,1... | collective-permute-start | bytes 442376 | tf_op jit(solution)/shard_map/ppermute | solution.py:43
  31.6 29.4 %collective-permute-start.10 = (bf16[768,384]{1,0:T(8,128)(2,1)S(1)}, bf16[768,384]{1,0:T(8,128)(2,1)S(1)}, u32[]{:S(2)}, u32[]{:S(2)}) collective-permute-start(bf16[768,384]{1,0:T(8,128)(2,1)S(1)} %pad_maximum_fusion.1.refs_5_), channel_id=1, source_target_pairs={{3,0},{0,1},{1,2},{2,3},{7,4},{4,5},{5,6},{6,7},{11,8},{8,9},{9,10... | collective-permute-start | bytes 1769480 | tf_op jit(solution)/shard_map/ppermute | solution.py:43
  32.4 29.8 %collective-permute-start.11 = (bf16[768,384]{1,0:T(8,128)(2,1)S(1)}, bf16[768,384]{1,0:T(8,128)(2,1)S(1)}, u32[]{:S(2)}, u32[]{:S(2)}) collective-permute-start(bf16[768,384]{1,0:T(8,128)(2,1)S(1)} %pad_maximum_fusion.1.refs_5_), channel_id=1, source_target_pairs={{1,0},{2,1},{3,2},{0,3},{5,4},{6,5},{7,6},{4,7},{9,8},{10,9},{11,1... | collective-permute-start | bytes 1769480 | tf_op jit(solution)/shard_map/ppermute | solution.py:43
  36.1 27.8 %collective-permute-start.3 = (bf16[768,384]{1,0:T(8,128)(2,1)S(1)}, bf16[768,384]{1,0:T(8,128)(2,1)S(1)}, u32[]{:S(2)}, u32[]{:S(2)}) collective-permute-start(bf16[768,384]{1,0:T(8,128)(2,1)S(1)} %pad_maximum_fusion.refs_0_), channel_id=1, source_target_pairs={{12,0},{13,1},{14,2},{15,3},{0,4},{1,5},{2,6},{3,7},{4,8},{5,9},{6... | collective-permute-start | bytes 1769480 | tf_op jit(solution)/shard_map/ppermute | solution.py:43
  36.2 27.8 %collective-permute-start.4 = (bf16[768,384]{1,0:T(8,128)(2,1)S(1)}, bf16[768,384]{1,0:T(8,128)(2,1)S(1)}, u32[]{:S(2)}, u32[]{:S(2)}) collective-permute-start(bf16[768,384]{1,0:T(8,128)(2,1)S(1)} %pad_maximum_fusion.refs_0_), channel_id=1, source_target_pairs={{4,0},{5,1},{6,2},{7,3},{8,4},{9,5},{10,6},{11,7},{12,8},{13,9},{1... | collective-permute-start | bytes 1769480 | tf_op jit(solution)/shard_map/ppermute | solution.py:43
  61.1 14.0 %collective-permute-start.12 = (bf16[384,384]{1,0:T(8,128)(2,1)S(1)}, bf16[384,384]{1,0:T(8,128)(2,1)S(1)}, u32[]{:S(2)}, u32[]{:S(2)}) collective-permute-start(bf16[384,384]{1,0:T(8,128)(2,1)S(1)} %slice.108), channel_id=1, source_target_pairs={{3,0},{0,1},{1,2},{2,3},{7,4},{4,5},{5,6},{6,7},{11,8},{8,9},{9,10... | collective-permute-start | bytes 884744 | tf_op jit(solution)/shard_map/ppermute | solution.py:43
  62.3 12.8 %collective-permute-start.13 = (bf16[384,384]{1,0:T(8,128)(2,1)S(1)}, bf16[384,384]{1,0:T(8,128)(2,1)S(1)}, u32[]{:S(2)}, u32[]{:S(2)}) collective-permute-start(bf16[384,384]{1,0:T(8,128)(2,1)S(1)} %slice.109), channel_id=1, source_target_pairs={{1,0},{2,1},{3,2},{0,3},{5,4},{6,5},{7,6},{4,7},{9,8},{10,9},{11,1... | collective-permute-start | bytes 884744 | tf_op jit(solution)/shard_map/ppermute | solution.py:43
  64.0 13.8 %collective-permute-start.5 = (bf16[384,384]{1,0:T(8,128)(2,1)S(1)}, bf16[384,384]{1,0:T(8,128)(2,1)S(1)}, u32[]{:S(2)}, u32[]{:S(2)}) collective-permute-start(bf16[384,384]{1,0:T(8,128)(2,1)S(1)} %slice.105), channel_id=1, source_target_pairs={{12,0},{13,1},{14,2},{15,3},{0,4},{1,5},{2,6},{3,7},{4,8},{5,9},{6... | collective-permute-start | bytes 884744 | tf_op jit(solution)/shard_map/ppermute | solution.py:43
  64.1 13.7 %collective-permute-start.6 = (bf16[384,384]{1,0:T(8,128)(2,1)S(1)}, bf16[384,384]{1,0:T(8,128)(2,1)S(1)}, u32[]{:S(2)}, u32[]{:S(2)}) collective-permute-start(bf16[384,384]{1,0:T(8,128)(2,1)S(1)} %slice.106), channel_id=1, source_target_pairs={{4,0},{5,1},{6,2},{7,3},{8,4},{9,5},{10,6},{11,7},{12,8},{13,9},{1... | collective-permute-start | bytes 884744 | tf_op jit(solution)/shard_map/ppermute | solution.py:43
  94.3 39.4 %copy-start.14 = (f32[640,64]{1,0:T(8,128)S(1)}, f32[640,64]{1,0:T(8,128)}, u32[]{:S(2)}) copy-start(f32[640,64]{1,0:T(8,128)} %copy-done.13) | copy-start | bytes 491524
  94.3 41.5 %copy-start.12 = (f32[640,64]{1,0:T(8,128)S(1)}, f32[640,64]{1,0:T(8,128)}, u32[]{:S(2)}) copy-start(f32[640,64]{1,0:T(8,128)} %copy-done.11) | copy-start | bytes 491524
  106.0 39.5 %copy-start.10 = (bf16[384,128]{1,0:T(8,128)(2,1)S(1)}, bf16[384,128]{1,0:T(8,128)(2,1)}, u32[]{:S(2)}) copy-start(bf16[384,128]{1,0:T(8,128)(2,1)} %copy-done.9) | copy-start | bytes 294916
  118.8 7.1 %collective-permute-start.21 = (bf16[128,384]{1,0:T(8,128)(2,1)S(1)}, bf16[128,384]{1,0:T(8,128)(2,1)S(1)}, u32[]{:S(2)}, u32[]{:S(2)}) collective-permute-start(bf16[128,384]{1,0:T(8,128)(2,1)S(1)} %bitcast.34), channel_id=1, source_target_pairs={{12,0},{13,1},{14,2},{15,3},{0,4},{1,5},{2,6},{3,7},{4,8},{5,9},{6... | collective-permute-start | bytes 294920 | tf_op jit(solution)/shard_map/ppermute | solution.py:43
  118.9 7.0 %collective-permute-start.22 = (bf16[128,384]{1,0:T(8,128)(2,1)S(1)}, bf16[128,384]{1,0:T(8,128)(2,1)S(1)}, u32[]{:S(2)}, u32[]{:S(2)}) collective-permute-start(bf16[128,384]{1,0:T(8,128)(2,1)S(1)} %bitcast.35), channel_id=1, source_target_pairs={{4,0},{5,1},{6,2},{7,3},{8,4},{9,5},{10,6},{11,7},{12,8},{13,9},{1... | collective-permute-start | bytes 294920 | tf_op jit(solution)/shard_map/ppermute | solution.py:43
  122.1 5.6 %collective-permute-start.23 = (bf16[128,384]{1,0:T(8,128)(2,1)S(1)}, bf16[128,384]{1,0:T(8,128)(2,1)S(1)}, u32[]{:S(2)}, u32[]{:S(2)}) collective-permute-start(bf16[128,384]{1,0:T(8,128)(2,1)S(1)} %bitcast.36), channel_id=1, source_target_pairs={{8,0},{9,1},{10,2},{11,3},{12,4},{13,5},{14,6},{15,7},{0,8},{1,9},... | collective-permute-start | bytes 294920 | tf_op jit(solution)/shard_map/ppermute | solution.py:43
  123.2 7.3 %collective-permute-start.14 = (bf16[128,384]{1,0:T(8,128)(2,1)S(1)}, bf16[128,384]{1,0:T(8,128)(2,1)S(1)}, u32[]{:S(2)}, u32[]{:S(2)}) collective-permute-start(bf16[128,384]{1,0:T(8,128)(2,1)S(1)} %bitcast.30), channel_id=1, source_target_pairs={{3,0},{0,1},{1,2},{2,3},{7,4},{4,5},{5,6},{6,7},{11,8},{8,9},{9,10... | collective-permute-start | bytes 294920 | tf_op jit(solution)/shard_map/ppermute | solution.py:43
  123.2 7.3 %collective-permute-start.15 = (bf16[128,384]{1,0:T(8,128)(2,1)S(1)}, bf16[128,384]{1,0:T(8,128)(2,1)S(1)}, u32[]{:S(2)}, u32[]{:S(2)}) collective-permute-start(bf16[128,384]{1,0:T(8,128)(2,1)S(1)} %bitcast.31), channel_id=1, source_target_pairs={{1,0},{2,1},{3,2},{0,3},{5,4},{6,5},{7,6},{4,7},{9,8},{10,9},{11,1... | collective-permute-start | bytes 294920 | tf_op jit(solution)/shard_map/ppermute | solution.py:43
  125.9 5.0 %collective-permute-start.16 = (bf16[128,384]{1,0:T(8,128)(2,1)S(1)}, bf16[128,384]{1,0:T(8,128)(2,1)S(1)}, u32[]{:S(2)}, u32[]{:S(2)}) collective-permute-start(bf16[128,384]{1,0:T(8,128)(2,1)S(1)} %bitcast.32), channel_id=1, source_target_pairs={{2,0},{3,1},{0,2},{1,3},{6,4},{7,5},{4,6},{5,7},{10,8},{11,9},{8,1... | collective-permute-start | bytes 294920 | tf_op jit(solution)/shard_map/ppermute | solution.py:43
  127.7 11.8 %collective-permute-start.24 = (bf16[512,384]{1,0:T(8,128)(2,1)S(1)}, bf16[512,384]{1,0:T(8,128)(2,1)S(1)}, u32[]{:S(2)}, u32[]{:S(2)}) collective-permute-start(bf16[512,384]{1,0:T(8,128)(2,1)S(1)} %pad_maximum_fusion.3.refs_5_), channel_id=1, source_target_pairs={{3,0},{0,1},{1,2},{2,3},{7,4},{4,5},{5,6},{6,7},{11,8},{8,9},{9,10... | collective-permute-start | bytes 1179656 | tf_op jit(solution)/shard_map/ppermute | solution.py:43
  127.8 11.8 %collective-permute-start.25 = (bf16[512,384]{1,0:T(8,128)(2,1)S(1)}, bf16[512,384]{1,0:T(8,128)(2,1)S(1)}, u32[]{:S(2)}, u32[]{:S(2)}) collective-permute-start(bf16[512,384]{1,0:T(8,128)(2,1)S(1)} %pad_maximum_fusion.3.refs_5_), channel_id=1, source_target_pairs={{1,0},{2,1},{3,2},{0,3},{5,4},{6,5},{7,6},{4,7},{9,8},{10,9},{11,1... | collective-permute-start | bytes 1179656 | tf_op jit(solution)/shard_map/ppermute | solution.py:43
  130.9 11.4 %collective-permute-start.17 = (bf16[512,384]{1,0:T(8,128)(2,1)S(1)}, bf16[512,384]{1,0:T(8,128)(2,1)S(1)}, u32[]{:S(2)}, u32[]{:S(2)}) collective-permute-start(bf16[512,384]{1,0:T(8,128)(2,1)S(1)} %pad_maximum_fusion.2.refs_0_), channel_id=1, source_target_pairs={{12,0},{13,1},{14,2},{15,3},{0,4},{1,5},{2,6},{3,7},{4,8},{5,9},{6... | collective-permute-start | bytes 1179656 | tf_op jit(solution)/shard_map/ppermute | solution.py:43
  131.9 11.0 %collective-permute-start.18 = (bf16[512,384]{1,0:T(8,128)(2,1)S(1)}, bf16[512,384]{1,0:T(8,128)(2,1)S(1)}, u32[]{:S(2)}, u32[]{:S(2)}) collective-permute-start(bf16[512,384]{1,0:T(8,128)(2,1)S(1)} %pad_maximum_fusion.2.refs_0_), channel_id=1, source_target_pairs={{4,0},{5,1},{6,2},{7,3},{8,4},{9,5},{10,6},{11,7},{12,8},{13,9},{1... | collective-permute-start | bytes 1179656 | tf_op jit(solution)/shard_map/ppermute | solution.py:43
  139.5 6.1 %collective-permute-start.26 = (bf16[256,384]{1,0:T(8,128)(2,1)S(1)}, bf16[256,384]{1,0:T(8,128)(2,1)S(1)}, u32[]{:S(2)}, u32[]{:S(2)}) collective-permute-start(bf16[256,384]{1,0:T(8,128)(2,1)S(1)} %slice.122), channel_id=1, source_target_pairs={{3,0},{0,1},{1,2},{2,3},{7,4},{4,5},{5,6},{6,7},{11,8},{8,9},{9,10... | collective-permute-start | bytes 589832 | tf_op jit(solution)/shard_map/ppermute | solution.py:43
  139.6 6.0 %collective-permute-start.27 = (bf16[256,384]{1,0:T(8,128)(2,1)S(1)}, bf16[256,384]{1,0:T(8,128)(2,1)S(1)}, u32[]{:S(2)}, u32[]{:S(2)}) collective-permute-start(bf16[256,384]{1,0:T(8,128)(2,1)S(1)} %slice.123), channel_id=1, source_target_pairs={{1,0},{2,1},{3,2},{0,3},{5,4},{6,5},{7,6},{4,7},{9,8},{10,9},{11,1... | collective-permute-start | bytes 589832 | tf_op jit(solution)/shard_map/ppermute | solution.py:43
  142.4 5.8 %collective-permute-start.19 = (bf16[256,384]{1,0:T(8,128)(2,1)S(1)}, bf16[256,384]{1,0:T(8,128)(2,1)S(1)}, u32[]{:S(2)}, u32[]{:S(2)}) collective-permute-start(bf16[256,384]{1,0:T(8,128)(2,1)S(1)} %slice.119), channel_id=1, source_target_pairs={{12,0},{13,1},{14,2},{15,3},{0,4},{1,5},{2,6},{3,7},{4,8},{5,9},{6... | collective-permute-start | bytes 589832 | tf_op jit(solution)/shard_map/ppermute | solution.py:43
  143.0 5.2 %collective-permute-start.20 = (bf16[256,384]{1,0:T(8,128)(2,1)S(1)}, bf16[256,384]{1,0:T(8,128)(2,1)S(1)}, u32[]{:S(2)}, u32[]{:S(2)}) collective-permute-start(bf16[256,384]{1,0:T(8,128)(2,1)S(1)} %slice.120), channel_id=1, source_target_pairs={{4,0},{5,1},{6,2},{7,3},{8,4},{9,5},{10,6},{11,7},{12,8},{13,9},{1... | collective-permute-start | bytes 589832 | tf_op jit(solution)/shard_map/ppermute | solution.py:43
  145.5 8.9 %collective-permute-start.28 = (bf16[384,128]{1,0:T(8,128)(2,1)S(1)}, bf16[384,128]{1,0:T(8,128)(2,1)S(1)}, u32[]{:S(2)}, u32[]{:S(2)}) collective-permute-start(bf16[384,128]{1,0:T(8,128)(2,1)S(1)} %copy-done.10), channel_id=1, source_target_pairs={{0,1},{1,0},{2,3},{3,2},{4,5},{5,4},{6,7},{7,6},{8,9},{9,8},{10,11... | collective-permute-start | bytes 294920 | tf_op jit(solution)/shard_map/ppermute | solution.py:524
  154.0 3.4 %collective-permute-start.29 = (bf16[256,128]{1,0:T(8,128)(2,1)S(1)}, bf16[256,128]{1,0:T(8,128)(2,1)S(1)}, u32[]{:S(2)}, u32[]{:S(2)}) collective-permute-start(bf16[256,128]{1,0:T(8,128)(2,1)S(1)} %get-tuple-element.18.oi), channel_id=1, source_target_pairs={{0,1},{1,0},{2,3},{3,2},{4,5},{5,4},{6,7},{7,6},{8,9},{9,8},{10,11... | collective-permute-start | bytes 196616 | tf_op jit(solution)/shard_map/ppermute | solution.py:529
  178.2 80.8 %copy-start.2 = (bf16[2,480,384]{2,1,0:T(8,128)(2,1)S(1)}, bf16[2,480,384]{2,1,0:T(8,128)(2,1)}, u32[]{:S(2)}) copy-start(bf16[2,480,384]{2,1,0:T(8,128)(2,1)} %text_ref.1) | copy-start | bytes 2211844
  178.2 4.6 %collective-permute-start.30 = (f32[2,6144]{1,0:T(2,128)S(1)}, f32[2,6144]{1,0:T(2,128)S(1)}, u32[]{:S(2)}, u32[]{:S(2)}) collective-permute-start(f32[2,6144]{1,0:T(2,128)S(1)} %convolution_add_fusion), channel_id=1, source_target_pairs={{2,0},{3,1},{0,2},{1,3},{6,4},{7,5},{4,6},{5,7},{10,8},{11,9},{8,1... | collective-permute-start | bytes 147464 | tf_op jit(solution)/shard_map/ppermute | solution.py:43
  178.2 4.7 %collective-permute-start.31 = (f32[2,6144]{1,0:T(2,128)S(1)}, f32[2,6144]{1,0:T(2,128)S(1)}, u32[]{:S(2)}, u32[]{:S(2)}) collective-permute-start(f32[2,6144]{1,0:T(2,128)S(1)} %convolution_add_fusion), channel_id=1, source_target_pairs={{3,0},{0,1},{1,2},{2,3},{7,4},{4,5},{5,6},{6,7},{11,8},{8,9},{9,10... | collective-permute-start | bytes 147464 | tf_op jit(solution)/shard_map/ppermute | solution.py:43
  178.8 4.2 %collective-permute-start.32 = (f32[2,6144]{1,0:T(2,128)S(1)}, f32[2,6144]{1,0:T(2,128)S(1)}, u32[]{:S(2)}, u32[]{:S(2)}) collective-permute-start(f32[2,6144]{1,0:T(2,128)S(1)} %convolution_add_fusion), channel_id=1, source_target_pairs={{1,0},{2,1},{3,2},{0,3},{5,4},{6,5},{7,6},{4,7},{9,8},{10,9},{11,1... | collective-permute-start | bytes 147464 | tf_op jit(solution)/shard_map/ppermute | solution.py:43
  183.0 4.8 %collective-permute-start.33 = (f32[2,6144]{1,0:T(2,128)S(1)}, f32[2,6144]{1,0:T(2,128)S(1)}, u32[]{:S(2)}, u32[]{:S(2)}) collective-permute-start(f32[2,6144]{1,0:T(2,128)S(1)} %add_add_fusion), channel_id=1, source_target_pairs={{8,0},{9,1},{10,2},{11,3},{12,4},{13,5},{14,6},{15,7},{0,8},{1,9},... | collective-permute-start | bytes 147464 | tf_op jit(solution)/shard_map/ppermute | solution.py:43
  184.7 5.2 %collective-permute-start.34 = (f32[2,6144]{1,0:T(2,128)S(1)}, f32[2,6144]{1,0:T(2,128)S(1)}, u32[]{:S(2)}, u32[]{:S(2)}) collective-permute-start(f32[2,6144]{1,0:T(2,128)S(1)} %add_add_fusion), channel_id=1, source_target_pairs={{12,0},{13,1},{14,2},{15,3},{0,4},{1,5},{2,6},{3,7},{4,8},{5,9},{6... | collective-permute-start | bytes 147464 | tf_op jit(solution)/shard_map/ppermute | solution.py:43
  186.4 4.0 %collective-permute-start.35 = (f32[2,6144]{1,0:T(2,128)S(1)}, f32[2,6144]{1,0:T(2,128)S(1)}, u32[]{:S(2)}, u32[]{:S(2)}) collective-permute-start(f32[2,6144]{1,0:T(2,128)S(1)} %add_add_fusion), channel_id=1, source_target_pairs={{4,0},{5,1},{6,2},{7,3},{8,4},{9,5},{10,6},{11,7},{12,8},{13,9},{1... | collective-permute-start | bytes 147464 | tf_op jit(solution)/shard_map/ppermute | solution.py:43
  216.1 4.1 %collective-permute-start.36 = (f32[16]{0:T(128)S(1)}, f32[16]{0:T(128)S(1)}, u32[]{:S(2)}, u32[]{:S(2)}) collective-permute-start(f32[16]{0:T(128)S(1)} %convolution_reduce_fusion), channel_id=1, source_target_pairs={{3,0},{0,1},{1,2},{2,3},{7,4},{4,5},{5,6},{6,7},{11,8},{8,9},{9,10... | collective-permute-start | bytes 200 | tf_op jit(solution)/shard_map/ppermute | solution.py:43
  217.9 2.6 collective-permute-start.37
  218.9 3.9 %collective-permute-start.38 = (f32[16]{0:T(128)S(1)}, f32[16]{0:T(128)S(1)}, u32[]{:S(2)}, u32[]{:S(2)}) collective-permute-start(f32[16]{0:T(128)S(1)} %convolution_reduce_fusion), channel_id=1, source_target_pairs={{2,0},{3,1},{0,2},{1,3},{6,4},{7,5},{4,6},{5,7},{10,8},{11,9},{8,1... | collective-permute-start | bytes 200 | tf_op jit(solution)/shard_map/ppermute | solution.py:43
  222.8 3.6 %collective-permute-start.39 = (f32[16]{0:T(128)S(1)}, f32[16]{0:T(128)S(1)}, u32[]{:S(2)}, u32[]{:S(2)}) collective-permute-start(f32[16]{0:T(128)S(1)} %maximum_maximum_fusion.1), channel_id=1, source_target_pairs={{12,0},{13,1},{14,2},{15,3},{0,4},{1,5},{2,6},{3,7},{4,8},{5,9},{6... | collective-permute-start | bytes 200 | tf_op jit(solution)/shard_map/ppermute | solution.py:43
  222.8 3.6 %collective-permute-start.40 = (f32[16]{0:T(128)S(1)}, f32[16]{0:T(128)S(1)}, u32[]{:S(2)}, u32[]{:S(2)}) collective-permute-start(f32[16]{0:T(128)S(1)} %maximum_maximum_fusion.1), channel_id=1, source_target_pairs={{4,0},{5,1},{6,2},{7,3},{8,4},{9,5},{10,6},{11,7},{12,8},{13,9},{1... | collective-permute-start | bytes 200 | tf_op jit(solution)/shard_map/ppermute | solution.py:43
  225.5 4.0 %collective-permute-start.41 = (f32[16]{0:T(128)S(1)}, f32[16]{0:T(128)S(1)}, u32[]{:S(2)}, u32[]{:S(2)}) collective-permute-start(f32[16]{0:T(128)S(1)} %maximum_maximum_fusion.1), channel_id=1, source_target_pairs={{8,0},{9,1},{10,2},{11,3},{12,4},{13,5},{14,6},{15,7},{0,8},{1,9},... | collective-permute-start | bytes 200 | tf_op jit(solution)/shard_map/ppermute | solution.py:43
  (18 other events, 169.1 us)
Sparse Core Ops, SparseCore 0:
  12.1 80.6 all-gather.2
  173.8 85.1 reduce-scatter.1
where the time goes:
time: 271 us; the launch traced here: 269 us
  waiting for transfers between devices  54.6 us (20%)
  starting transfers between devices  54.1 us (20%)
  blocking collectives  49.8 us (18%)
  Pallas kernels  44.7 us (16%)
  local copies, waits for them, and re-layouts  23.8 us (9%)
  between operations  16.6 us (6%)
  other arithmetic  16.4 us (6%)
  matrix products  9.1 us (3%)
    ppermute x40, starting transfers between devices, shift(): return lax.ppermute(block, 'hid', route)  53.7 us
    ppermute x40, waiting for transfers between devices, shift(): return lax.ppermute(block, 'hid', route)  31.7 us
    all_gather x1, blocking collectives, shards(): all_last = lax.all_gather(full_width, 'req', axis=0, tiled=True)  21.1 us
    pmax x1, blocking collectives, shards(): logit_max = lax.pmax(top, 'req')  15.9 us
    reduce_scatter x1, waiting for transfers between devices, shards(): lax.psum_scatter(partial.reshape(N_HID * LIVE, FEAT), 'hid', scatter_dime...  13.6 us
    pallas_call x2, Pallas kernels, qkv(): pl.pallas_call(kernel, out_shape=(jax.ShapeDtypeStruct((rows, FEAT), BF),...  13.2 us
    all_to_all x1, blocking collectives, shards(): lax.all_to_all(projected.reshape(N_REQ, TILE // N_REQ, FEAT), 'req', spli...  12.8 us
    pallas_call x1, Pallas kernels, project(): pl.pallas_call(project_kernel, out_shape=jax.ShapeDtypeStruct((TILE, FEAT...  11.6 us
  transfers between devices with their start and end apart: 44, of which 19 were waited for; matrix products, arithmetic and copies ran while one was open for 15% of the time, Pallas kernels for 5%

commit v1 on v0

--- a/solution.py
+++ b/solution.py
@@ -148,7 +148,7 @@
 
 
 def project_kernel(
-    x_hbm, w_hbm, g_ref, b_ref, gl_ref, bl_ref, pb_ref, o_ref, tail, x, w, wl, acc, sem, x_sem, w_sem
+    x_hbm, w_hbm, gb_ref, left_ref, pb_ref, o_ref, tail, x, w, wl, acc, sem, x_sem, w_sem
 ):
     deep = 2 * MAIN
     tails = pltpu.make_async_copy(x_hbm.at[:, pl.ds(MAIN, 128)], tail, sem.at[0])
@@ -158,6 +158,9 @@
         here = pl.ds(pl.multiple_of(k * MAIN, MAIN), MAIN)
         there = x_hbm.at[pl.ds(k * TILE, TILE), pl.ds(0, MAIN)]
         return pltpu.make_async_copy(there, x.at[:, here], x_sem.at[k])
+
+    def pair(part, i):
+        return jnp.concatenate([gb_ref[part, pl.ds(2 * i + j, 1), :] for j in (0, 1)], axis=1)
 
     def w_copy(k):
         here = pl.ds(k * MAIN, MAIN)
@@ -190,7 +193,7 @@
             w_copy(2 * i + j).wait()
         here = pl.ds(pl.multiple_of(i * deep, deep), deep)
         v = x[:, here].astype(F32)
-        normed = (v - mean) * rstd * g_ref[i] + b_ref[i]
+        normed = (v - mean) * rstd * pair(0, i) + pair(1, i)
         acc[...] += jnp.dot(normed.astype(BF), w[here, :], preferred_element_type=F32)
         return carry
 
@@ -202,7 +205,7 @@
         for j in range(RING):
             k = RING * i + j
             v = jnp.where(quarter == j, tail[k * TILE : (k + 1) * TILE, :].astype(F32), v)
-        blocks.append(((v - mean) * rstd * gl_ref[i] + bl_ref[i]).astype(BF))
+        blocks.append(((v - mean) * rstd * left_ref[0, i] + left_ref[1, i]).astype(BF))
     rest = jnp.concatenate(blocks, axis=1)
     y = acc[...] + pb_ref[...] + jnp.dot(
         rest, wl[...].reshape(N_HID * 32, FEAT), preferred_element_type=F32
@@ -212,19 +215,11 @@
 
 
 def project(gathered, weight, gain, bias, out_bias):
-    def parts(v):
-        v = v.astype(F32).reshape(N_HID, MFEAT)
-        return (
-            v[:, :MAIN].reshape(N_HID // 2, 1, 2 * MAIN),
-            v[:, MAIN:].reshape(RING, 1, 128),
-        )
-
-    gain, gain_left = parts(gain)
-    bias, bias_left = parts(bias)
+    both = jnp.stack([gain, bias]).astype(F32).reshape(2, N_HID, MFEAT)
     return pl.pallas_call(
         project_kernel,
         out_shape=jax.ShapeDtypeStruct((TILE, FEAT), BF),
-        in_specs=[pl.BlockSpec(memory_space=pl.ANY)] * 2 + [vmem()] * 5,
+        in_specs=[pl.BlockSpec(memory_space=pl.ANY)] * 2 + [vmem()] * 3,
         out_specs=vmem(),
         scratch_shapes=[
             VM((N_HID * TILE, 128), BF),
@@ -244,10 +239,8 @@
     )(
         in_hbm(gathered),
         in_hbm(weight.reshape(N_HID, MFEAT, FEAT)),
-        gain,
-        bias,
-        gain_left,
-        bias_left,
+        both[:, :, :MAIN],
+        both[:, :, MAIN:].reshape(2, RING, 1, 128),
         out_bias,
     )
 
@@ -260,7 +253,7 @@
     half = arrays[0].shape[0] // RING
     rows = 2 * half
     n = len(arrays)
-    deep = 2 * FEAT
+    deep = 4 * FEAT
     cols = FEAT + HEAD_DIM
 
     def kernel(src_ref, *refs):
@@ -281,8 +274,8 @@
         sq[...] = jnp.zeros_like(sq)
 
         def step(i, carry):
-            for j in range(2):
-                copy(2 * i + j).wait()
+            for j in range(4):
+                copy(4 * i + j).wait()
             here = pl.ds(pl.multiple_of(i * deep, deep), deep)
             acc[...] += jnp.dot(xs[:, here], w[here, :], preferred_element_type=F32)
             v = xs[:, here].astype(F32)
@@ -290,7 +283,7 @@
             sq[...] += sum(v[:, c : c + 128] for c in range(0, deep, 128))
             return carry
 
-        lax.fori_loop(0, N_HID // 2, step, 0)
+        lax.fori_loop(0, RING, step, 0)
         scale = lax.rsqrt(jnp.sum(sq[...], axis=1, keepdims=True) * (1.0 / D) + 1e-05)
         for h in range(FEAT // HEAD_DIM):
             part = acc[:, h * HEAD_DIM : (h + 1) * HEAD_DIM] * scale
@@ -374,52 +367,39 @@
     )(low, qt, qi, ot, pt, oi, pi, cos, sin, code[:, None], code[None, :])
 
 
-def spread_kernel(a_ref, w_hbm, o_ref, w, sem):
-    k = pl.program_id(0)
+def finish_kernel(
+    text_ref, tile_ref, a_hbm, w_hbm, slot_ref, o_ref, a, w, acc, sums, a_sem, w_sem
+):
     two = 2 * FEAT
 
-    def copy(i):
-        cols = pl.ds(pl.multiple_of(i * two, two), two)
-        return pltpu.make_async_copy(w_hbm.at[:, cols], w.at[i], sem.at[i])
-
-    @pl.when(k == 0)
-    def _():
-        for i in range(N_HID // 2):
-            copy(i).start()
-
-    copy(k).wait()
-    product = jnp.dot(a_ref[...], w[k], preferred_element_type=F32).astype(BF)
-    o_ref[0] = product[:, :FEAT]
-    o_ref[1] = product[:, FEAT:]
-
-
-def spread(attended, weight):
-    return pl.pallas_call(
-        spread_kernel,
-        out_shape=jax.ShapeDtypeStruct((N_HID, LIVE, FEAT), BF),
-        grid=(N_HID // 2,),
-        in_specs=[
-            pl.BlockSpec(memory_space=pltpu.VMEM),
-            pl.BlockSpec(memory_space=pl.ANY),
-        ],
-        out_specs=pl.BlockSpec((2, LIVE, FEAT), lambda k: (k, 0, 0)),
-        scratch_shapes=[
-            VM((N_HID // 2, FEAT, 2 * FEAT), BF),
-            pltpu.SemaphoreType.DMA((N_HID // 2,)),
-        ],
-        compiler_params=params(58),
-        cost_estimate=pl.CostEstimate(
-            flops=2 * LIVE * FEAT * D, bytes_accessed=13 << 20, transcendentals=0
-        ),
-        name="spread",
-    )(attended, in_hbm(weight))
-
-
-def finish_kernel(text_ref, tile_ref, sum_ref, slot_ref, o_ref):
+    def a_copy(k):
+        here = pl.ds(pl.multiple_of(k * FEAT, FEAT), FEAT)
+        return pltpu.make_async_copy(a_hbm.at[pl.ds(k * LIVE, LIVE), :], a.at[:, here], a_sem.at[k])
+
+    def w_copy(k):
+        here = pl.ds(k * FEAT, FEAT)
+        return pltpu.make_async_copy(w_hbm.at[here, :], w.at[here, :], w_sem.at[k])
+
+    for k in range(N_HID):
+        a_copy(k).start()
+        w_copy(k).start()
+    acc[...] = jnp.zeros_like(acc)
+
+    def step(i, carry):
+        for j in (0, 1):
+            a_copy(2 * i + j).wait()
+            w_copy(2 * i + j).wait()
+        here = pl.ds(pl.multiple_of(i * two, two), two)
+        acc[...] += jnp.dot(a[:, here], w[here, :], preferred_element_type=F32)
+        return carry
+
+    lax.fori_loop(0, N_HID // 2, step, 0)
+    sums[...] = acc[...].astype(BF)
+
     def one(r, carry):
         row = slot_ref[r]
         pick = (lax.broadcasted_iota(jnp.int32, (LEN_MAX, LIVE), 1) == row).astype(BF)
-        moved = jnp.dot(pick, sum_ref[...], preferred_element_type=F32)
+        moved = jnp.dot(pick, sums[...], preferred_element_type=F32)
         image = jnp.dot(pick[:, TEXT:], tile_ref[...], preferred_element_type=F32)
         base = jnp.where(row >= TEXT, image, text_ref[r].astype(F32))
         o_ref[r] = (base + moved).astype(BF)
@@ -428,15 +408,26 @@
     lax.fori_loop(0, REQ_GRP, one, 0)
 
 
-def finish(text, tile, sums, slots):
+def finish(text, tile, heads, weight, slots):
     return pl.pallas_call(
         finish_kernel,
         out_shape=jax.ShapeDtypeStruct((REQ_GRP, LEN_MAX, FEAT), BF),
-        in_specs=[vmem()] * 4,
+        in_specs=[vmem()] * 2 + [pl.BlockSpec(memory_space=pl.ANY)] * 2 + [vmem()],
         out_specs=vmem(),
-        compiler_params=params(24),
+        scratch_shapes=[
+            VM((LIVE, D), BF),
+            VM((D, FEAT), BF),
+            VM((LIVE, FEAT), F32),
+            VM((LIVE, FEAT), BF),
+            pltpu.SemaphoreType.DMA((N_HID,)),
+            pltpu.SemaphoreType.DMA((N_HID,)),
+        ],
+        compiler_params=params(32),
+        cost_estimate=pl.CostEstimate(
+            flops=2 * LIVE * FEAT * D, bytes_accessed=14 << 20, transcendentals=0
+        ),
         name="finish",
-    )(text, tile, sums, slots)
+    )(text, tile, in_hbm(heads), in_hbm(weight), slots)
 
 
 def shards(
@@ -522,7 +513,13 @@
         projected.reshape(N_REQ, TILE // N_REQ, FEAT), "req", split_axis=0, concat_axis=0, tiled=True
     ).reshape(TILE, FEAT)
     other_text = lax.ppermute(kv_text, "hid", partner)
+    strip = FEAT // N_REQ
+    piece = lax.dynamic_slice_in_dim(out_weight, me * strip, strip, axis=0)
+    piece = piece.reshape(strip, N_HID, FEAT).transpose(1, 0, 2)
+    piece = lax.all_to_all(piece, "hid", split_axis=0, concat_axis=0, tiled=True)
+    piece, tile = lax.optimization_barrier((piece, tile))
     tile_blocks, tile_where = gather_far(gather_near(tile))
+    columns = lax.all_gather(piece, "req", axis=1, tiled=True).reshape(D, FEAT)
     q_tile, kv_tile = qkv(
         tile_blocks, tile_where, weight, cos[TEXT:], sin[TEXT:], sources, "qkv_tile"
     )
@@ -532,12 +529,8 @@
     attended = attend(
         low, q_text, q_tile, kv_text, other_text, kv_tile, other_tile, cos, sin, code
     )
-    partial = spread(attended, out_weight)
-    partial, attended = lax.optimization_barrier((partial, attended))
-    sums = lax.psum_scatter(
-        partial.reshape(N_HID * LIVE, FEAT), "hid", scatter_dimension=0, tiled=True
-    )
-    hidden = finish(text_embed, tile, sums, row_of[:, :, None])
+    heads = lax.all_gather(attended, "hid", axis=0, tiled=True)
+    hidden = finish(text_embed, tile, heads, columns, row_of[:, :, None])
 
     last = jnp.sum(jnp.where(slot[None, :] == lengths[:, None] - 1, row_of, 0), axis=1)
     pick_last = (last[:, None] == n[None, :]).astype(BF)

time: 271 us -> 267 us (0.985)
  starting transfers between devices: 54.1 us -> 61.5 us
  waiting for transfers between devices: 54.6 us -> 48.8 us
  blocking collectives: 49.8 us -> 46.8 us
    reduce_scatter x1 -> x0, waiting for transfers between devices: 13.6 us -> none  [shards(): lax.psum_scatter(partial.reshape(N_HID * LIVE, FEAT), 'hid', scatter_dime...]
    pallas_call x1 -> x0, Pallas kernels: 9.52 us -> none  [spread(): pl.pallas_call(spread_kernel, out_shape=jax.ShapeDtypeStruct((N_HID, LIVE...]
    pallas_call x1, Pallas kernels: 2.31 us -> 9.5 us  [finish(): pl.pallas_call(finish_kernel, out_shape=jax.ShapeDtypeStruct((REQ_GRP, LE...]
    reshape x6 -> x1, local copies, waits for them, and re-layouts: 6.68 us -> 0.81 us  [project(): both[:, :, MAIN:].reshape(2, RING, 1, 128)]
    all_gather x1, waiting for transfers between devices: 6.19 us -> 12 us  [shards(): lax.all_gather(pack(merged, tile_order, (hid % RING)[None]), 'hid', axis=...]
    all_gather x0 -> x1, local copies, waits for them, and re-layouts: none -> 5.73 us  [shards(): columns = lax.all_gather(piece, 'req', axis=1, tiled=True).reshape(D, FEAT)]
    all_to_all x0 -> x1, starting transfers between devices: none -> 4.27 us  [shards(): lax.all_to_all(piece, 'hid', split_axis=0, concat_axis=0, tiled=True)]
    slice x4 -> x1, local copies, waits for them, and re-layouts: 4.82 us -> 0.65 us  [project(): both[:, :, :MAIN]]
  transfers between devices with their start and end apart: 44 -> 46, of which waited for: 19 -> 20; matrix products, arithmetic and copies ran while one was open for 15% -> 16% of each run, Pallas kernels for 5% -> 12%
where the time goes in v1:
time: 267 us; the launch traced here: 266 us
  starting transfers between devices  61.5 us (23%)
  waiting for transfers between devices  48.8 us (18%)
  blocking collectives  46.8 us (18%)
  Pallas kernels  42.7 us (16%)
  local copies, waits for them, and re-layouts  21.9 us (8%)
  other arithmetic  18.5 us (7%)
  between operations  16.3 us (6%)
  matrix products  9.28 us (3%)
    ppermute x40, starting transfers between devices, shift(): return lax.ppermute(block, 'hid', route)  56.7 us
    ppermute x40, waiting for transfers between devices, shift(): return lax.ppermute(block, 'hid', route)  33.7 us
    all_gather x1, blocking collectives, shards(): all_last = lax.all_gather(full_width, 'req', axis=0, tiled=True)  20.2 us
    pmax x1, blocking collectives, shards(): logit_max = lax.pmax(top, 'req')  15.8 us
    pallas_call x2, Pallas kernels, qkv(): pl.pallas_call(kernel, out_shape=(jax.ShapeDtypeStruct((rows, FEAT), BF),...  12.8 us
    all_gather x1, waiting for transfers between devices, shards(): lax.all_gather(pack(merged, tile_order, (hid % RING)[None]), 'hid', axis=...  12 us
    pallas_call x1, Pallas kernels, project(): pl.pallas_call(project_kernel, out_shape=jax.ShapeDtypeStruct((TILE, FEAT...  11.5 us
    all_to_all x1, blocking collectives, shards(): lax.all_to_all(projected.reshape(N_REQ, TILE // N_REQ, FEAT), 'req', spli...  10.8 us
  transfers between devices with their start and end apart: 46, of which 20 were waited for; matrix products, arithmetic and copies ran while one was open for 16% of the time, Pallas kernels for 12%

profile of v1, /device:TPU:1, one launch (start us, length us, event | category | flops | bytes accessed | tf_op | source)
XLA Modules:
  0.0 265.9 jit_solution(13341092703183931899)
XLA Ops:
  9.7 2.3 pack.1
  14.6 1.8 fusion.1
  17.2 2.1 collective-permute-start.7
  20.6 1.6 collective-permute-start.9
  22.3 1.6 collective-permute-start
  23.9 2.1 collective-permute-start.1
  26.1 1.5 collective-permute-start.2
  29.7 4.3 %all-to-all-start = ((bf16[16,48,384]{2,1,0:T(8,128)(2,1)}), bf16[16,48,384]{2,1,0:T(8,128)(2,1)}, u32[]{:S(2)}, u32[]{:S(2)}) async-start(bf16[16,48,384]{2,1,0:T(8,128)(2,1)} %copy.43), calls=%async_computation | async-start | bytes 1179648 | tf_op jit(solution)/shard_map/all_to_all | solution.py:519
  34.1 1.5 copy.44
  35.6 1.5 copy.45
  38.5 1.5 collective-permute-start.11
  41.3 8.7 %multiply_convert_fusion.refs_10_ = bf16[6144,512]{1,0:T(8,128)(2,1)} fusion(bf16[6144,64]{1,0:T(8,128)(2,1)} %copy.45, bf16[6144,64]{1,0:T(8,128)(2,1)} %copy.44, bf16[6144,384]{1,0:T(8,128)(2,1)} %param.23, f32[6144]{0:T(1024)S(1)} %convert_element_type.43), kind=kLoop, calls=%fused_computation | loop fusion | flops 25165824 | bytes 12607488 | tf_op jit(solution)/shard_map/convert_element_type | solution.py:498
  50.0 1.5 collective-permute-start.4
  51.5 1.5 stack.18
  59.2 1.9 collective-permute-done.10.refs_6_
  61.3 3.3 %collective-permute-start.13 = (bf16[384,384]{1,0:T(8,128)(2,1)S(1)}, bf16[384,384]{1,0:T(8,128)(2,1)S(1)}, u32[]{:S(2)}, u32[]{:S(2)}) collective-permute-start(bf16[384,384]{1,0:T(8,128)(2,1)S(1)} %slice.93), channel_id=1, source_target_pairs={{1,0},{2,1},{3,2},{0,3},{5,4},{6,5},{7,6},{4,7},{9,8},{10,9},{11,1... | collective-permute-start | bytes 884744 | tf_op jit(solution)/shard_map/ppermute | solution.py:43
  64.7 3.7 %collective-permute-start.6 = (bf16[384,384]{1,0:T(8,128)(2,1)S(1)}, bf16[384,384]{1,0:T(8,128)(2,1)S(1)}, u32[]{:S(2)}, u32[]{:S(2)}) collective-permute-start(bf16[384,384]{1,0:T(8,128)(2,1)S(1)} %slice.90), channel_id=1, source_target_pairs={{4,0},{5,1},{6,2},{7,3},{8,4},{9,5},{10,6},{11,7},{12,8},{13,9},{1... | collective-permute-start | bytes 884744 | tf_op jit(solution)/shard_map/ppermute | solution.py:43
  68.6 8.4 %collective-permute-done.12.refs_8_ = bf16[384,384]{1,0:T(8,128)(2,1)S(1)} collective-permute-done((bf16[384,384]{1,0:T(8,128)(2,1)S(1)}, bf16[384,384]{1,0:T(8,128)(2,1)S(1)}, u32[]{:S(2)}, u32[]{:S(2)}) %collective-permute-start.12) | collective-permute-done | bytes 294944 | tf_op jit(solution)/shard_map/ppermute | solution.py:43
  77.1 3.4 %collective-permute-done.5.refs_3_ = bf16[384,384]{1,0:T(8,128)(2,1)S(1)} collective-permute-done((bf16[384,384]{1,0:T(8,128)(2,1)S(1)}, bf16[384,384]{1,0:T(8,128)(2,1)S(1)}, u32[]{:S(2)}, u32[]{:S(2)}) %collective-permute-start.5) | collective-permute-done | bytes 294944 | tf_op jit(solution)/shard_map/ppermute | solution.py:43
  80.9 7.2 %qkv_text.1 = (bf16[384,384]{1,0:T(8,128)(2,1)S(1)}, bf16[384,128]{1,0:T(8,128)(2,1)S(1)}) custom-call(s32[16]{0:T(128)S(1)} %fusion.22.src_ref, bf16[768,384]{1,0:T(8,128)(2,1)S(1)} %pad_maximum_fusion.refs_0_, bf16[768,384]{1,0:T(8,128)(2,1)S(1)} %collective-permute-done.3.refs_1_, bf16[768,384]{1,0:T(8,128)(2,1)S(1)} %collective-permute-done.4.refs_2_, ...), custom_call_target="tpu_custom_call" | custom-call | flops 2415919104 | bytes 12582912 | tf_op jit(solution)/shard_map/qkv_text/pallas_call | solution.py:295
  89.5 12.0 %all-gather.5.cloned.1.call-done.x_hbm = bf16[4096,896]{1,0:T(8,128)(2,1)} async-done(((bf16[256,896]{1,0:T(8,128)(2,1)}), bf16[4096,896]{1,0:T(8,128)(2,1)}) %all-gather.5.cloned.1.call-update) | async-done | bytes 7340048 | tf_op jit(solution)/shard_map/all_gather | solution.py:489
  102.5 11.5 %project.1 = bf16[256,384]{1,0:T(8,128)(2,1)S(1)} custom-call(bf16[4096,896]{1,0:T(8,128)(2,1)} %all-gather.5.cloned.1.call-done.x_hbm, bf16[16,800,384]{2,1,0:T(8,128)(2,1)} %bitcast.32, f32[2,16,768]{2,1,0:T(8,128)S(1)} %copy-done.2, f32[2,4,1,128]{3,2,1,0:T(1,128)S(1)} %reshape.313.left_ref, f32[1,384]{1,0:T(1,128)S(1)} %broadcast_in_dim.108.pb_ref), custom_call_target="tpu_custom_call" | custom-call | flops 2516582400 | bytes 17825792 | tf_op jit(solution)/shard_map/project/pallas_call | solution.py:219
  114.1 10.8 %all_to_all.10 = bf16[8,32,384]{2,1,0:T(8,128)(2,1)S(1)} all-to-all(bf16[8,32,384]{2,1,0:T(8,128)(2,1)S(1)} %bitcast.29), channel_id=1, replica_groups=mesh['req'=8,'hid'=16] {'req'}, dimensions={0} | all-to-all | bytes 393216 | tf_op jit(solution)/shard_map/all_to_all | solution.py:512
  124.8 2.0 copy.46
  128.2 2.3 collective-permute-start.22
  131.6 1.8 collective-permute-start.14
  136.1 1.9 collective-permute-start.24
  140.3 1.8 collective-permute-start.18
  144.4 3.6 %collective-permute-done.24.refs_6_ = bf16[512,384]{1,0:T(8,128)(2,1)S(1)} collective-permute-done((bf16[512,384]{1,0:T(8,128)(2,1)S(1)}, bf16[512,384]{1,0:T(8,128)(2,1)S(1)}, u32[]{:S(2)}, u32[]{:S(2)}) %collective-permute-start.24) | collective-permute-done | bytes 393248 | tf_op jit(solution)/shard_map/ppermute | solution.py:43
  148.2 2.7 %collective-permute-start.27 = (bf16[256,384]{1,0:T(8,128)(2,1)S(1)}, bf16[256,384]{1,0:T(8,128)(2,1)S(1)}, u32[]{:S(2)}, u32[]{:S(2)}) collective-permute-start(bf16[256,384]{1,0:T(8,128)(2,1)S(1)} %slice.102), channel_id=1, source_target_pairs={{1,0},{2,1},{3,2},{0,3},{5,4},{6,5},{7,6},{4,7},{9,8},{10,9},{11,1... | collective-permute-start | bytes 589832 | tf_op jit(solution)/shard_map/ppermute | solution.py:43
  151.4 2.3 collective-permute-start.20
  154.2 2.9 %collective-permute-done.19.refs_3_ = bf16[256,384]{1,0:T(8,128)(2,1)S(1)} collective-permute-done((bf16[256,384]{1,0:T(8,128)(2,1)S(1)}, bf16[256,384]{1,0:T(8,128)(2,1)S(1)}, u32[]{:S(2)}, u32[]{:S(2)}) %collective-permute-start.19) | collective-permute-done | bytes 196640 | tf_op jit(solution)/shard_map/ppermute | solution.py:43
  157.1 5.6 %qkv_tile.1 = (bf16[256,384]{1,0:T(8,128)(2,1)S(1)}, bf16[256,128]{1,0:T(8,128)(2,1)S(1)}) custom-call(s32[16]{0:T(128)S(1)} %fusion.22.src_ref, bf16[512,384]{1,0:T(8,128)(2,1)S(1)} %pad_maximum_fusion.2.refs_0_, bf16[512,384]{1,0:T(8,128)(2,1)S(1)} %collective-permute-done.17.refs_1_, bf16[512,384]{1,0:T(8,128)(2,1)S(1)} %collective-permute-done.18.refs_2_, ...), custom_call_target="tpu_custom_call" | custom-call | flops 1610612736 | bytes 12582912 | tf_op jit(solution)/shard_map/qkv_tile/pallas_call | solution.py:295
  163.0 3.0 %collective-permute-done.29.pi = bf16[256,128]{1,0:T(8,128)(2,1)S(1)} collective-permute-done((bf16[256,128]{1,0:T(8,128)(2,1)S(1)}, bf16[256,128]{1,0:T(8,128)(2,1)S(1)}, u32[]{:S(2)}, u32[]{:S(2)}) %collective-permute-start.29) | collective-permute-done | bytes 65568 | tf_op jit(solution)/shard_map/ppermute | solution.py:526
  166.1 6.6 %attend.1 = bf16[640,384]{1,0:T(8,128)(2,1)} custom-call(s32[1]{0:T(128)} %bitcast.7.low_ref, bf16[384,384]{1,0:T(8,128)(2,1)S(1)} %copy-done.4, bf16[256,384]{1,0:T(8,128)(2,1)S(1)} %get-tuple-element.17.qi, bf16[384,128]{1,0:T(8,128)(2,1)S(1)} %copy-done.6, bf16[384,128]{1,0:T(8,128)(2,1)S(1)} %collective-permute-done.28.pt, ...), custom_call_target="tpu_custom_call" | custom-call | flops 1073741824 | bytes 2097152 | tf_op jit(solution)/shard_map/attend/pallas_call | solution.py:358
  173.6 3.4 %convolution_add_fusion = f32[2,6144]{1,0:T(2,128)S(1)} fusion(bf16[384,6144]{1,0:T(8,128)(2,1)} %param.26, bf16[640,384]{1,0:T(8,128)(2,1)} %attend.1, f32[2,6144]{1,0:T(2,128)S(1)} %bitcast.35, pred[6144]{0:T(1024)(128)(4,1)S(1)} %broadcast_in_dim.119, s32[2]{0:T(128)S(1)} %fusion.15), kind=kOutput, calls=%fused_computation.1 | convolution fusion | flops 10446848 | bytes 5314568 | tf_op jit(solution)/shard_map/dot_general | solution.py:538
  177.5 2.6 collective-permute-start.32
  183.4 2.0 collective-permute-start.34
  187.5 1.9 collective-permute-done.35
  189.5 20.2 %all-gather = bf16[8,2,6144]{2,1,0:T(2,128)(2,1)S(1)} all-gather(bf16[1,2,6144]{2,1,0:T(2,128)(2,1)S(1)} %fusion.12), channel_id=1, replica_groups=mesh['req'=8,'hid'=16] {'req'}, dimensions={0}, use_global_device_ids=true | all-gather | bytes 221184 | tf_op jit(solution)/shard_map/all_gather | solution.py:546
  210.4 3.8 %convolution_reduce_fusion = f32[16]{0:T(128)S(1)} fusion(bf16[384,6144]{1,0:T(8,128)(2,1)} %param.28, f32[16,6144]{1,0:T(8,128)S(1)} %reshape.320, f32[6144]{0:T(1024)S(1)} %convert_element_type.50, f32[16]{0:T(128)S(1)} %get-tuple-element.31), kind=kOutput, calls=%fused_computation.6 | convolution fusion | flops 75798512 | bytes 5136512 | tf_op jit(solution)/shard_map/dot_general | solution.py:553
  215.5 2.1 collective-permute-start.37
  218.9 2.7 %collective-permute-done.38 = f32[16]{0:T(128)S(1)} collective-permute-done((f32[16]{0:T(128)S(1)}, f32[16]{0:T(128)S(1)}, u32[]{:S(2)}, u32[]{:S(2)}) %collective-permute-start.38) | collective-permute-done | bytes 96 | tf_op jit(solution)/shard_map/ppermute | solution.py:43
  221.6 2.7 %collective-permute-start.40 = (f32[16]{0:T(128)S(1)}, f32[16]{0:T(128)S(1)}, u32[]{:S(2)}, u32[]{:S(2)}) collective-permute-start(f32[16]{0:T(128)S(1)} %maximum_maximum_fusion.1), channel_id=1, source_target_pairs={{4,0},{5,1},{6,2},{7,3},{8,4},{9,5},{10,6},{11,7},{12,8},{13,9},{1... | collective-permute-start | bytes 200 | tf_op jit(solution)/shard_map/ppermute | solution.py:43
  225.6 2.6 collective-permute-done.41
  228.2 15.8 %pmax.7 = f32[16]{0:T(128)} all-reduce(f32[16]{0:T(128)S(1)} %maximum_maximum_fusion), channel_id=1, replica_groups=mesh['req'=8,'hid'=16] {'req'}, use_global_device_ids=true, to_apply=%region_6.7 | all-reduce | flops 16 | bytes 128 | tf_op jit(solution)/shard_map/pmax | solution.py:560
  244.1 5.7 %copy.47 = bf16[16,384,384]{2,1,0:T(8,128)(2,1)} copy(bf16[16,384,384]{2,0,1:T(8,128)(2,1)} %all-gather.9.cloned.1.call-done) | data formatting | bytes 9437184 | tf_op jit(solution)/shard_map/all_gather | solution.py:522
  249.8 9.5 %finish.1 = bf16[2,480,384]{2,1,0:T(8,128)(2,1)} custom-call(bf16[2,480,384]{2,1,0:T(8,128)(2,1)S(1)} %copy-done, bf16[256,384]{1,0:T(8,128)(2,1)S(1)} %bitcast.28, bf16[10240,384]{1,0:T(8,128)(2,1)} %all-gather.7.cloned.1.call-done.a_hbm, bf16[6144,384]{1,0:T(8,128)(2,1)} %bitcast.31, s32[2,480,1]{2,1,0:T(8,128)S(1)} %fusion.4.slot_ref), custom_call_target="tpu_custom_call" | custom-call | flops 3019898880 | bytes 14680064 | tf_op jit(solution)/shard_map/finish/pallas_call | solution.py:412
  (168 shorter events, 42.0 us)
Async XLA Ops:
  7.2 94.4 %all-gather.5.cloned.1.call-start = ((), (), s32[]{:S(2)}) async-start(), calls=%async_computation.2 | async-start | bytes 7798784 | tf_op jit(solution)/shard_map/all_gather | solution.py:489
  17.2 8.9 %collective-permute-start.7 = (bf16[192,384]{1,0:T(8,128)(2,1)S(1)}, bf16[192,384]{1,0:T(8,128)(2,1)S(1)}, u32[]{:S(2)}, u32[]{:S(2)}) collective-permute-start(bf16[192,384]{1,0:T(8,128)(2,1)S(1)} %get-tuple-element.24), channel_id=1, source_target_pairs={{12,0},{13,1},{14,2},{15,3},{0,4},{1,5},{2,6},{3,7},{4,8},{5,9},{6... | collective-permute-start | bytes 442376 | tf_op jit(solution)/shard_map/ppermute | solution.py:43
  19.3 17.8 %collective-permute-start.8 = (bf16[192,384]{1,0:T(8,128)(2,1)S(1)}, bf16[192,384]{1,0:T(8,128)(2,1)S(1)}, u32[]{:S(2)}, u32[]{:S(2)}) collective-permute-start(bf16[192,384]{1,0:T(8,128)(2,1)S(1)} %get-tuple-element.24), channel_id=1, source_target_pairs={{4,0},{5,1},{6,2},{7,3},{8,4},{9,5},{10,6},{11,7},{12,8},{13,9},{1... | collective-permute-start | bytes 442376 | tf_op jit(solution)/shard_map/ppermute | solution.py:43
  20.6 16.5 %collective-permute-start.9 = (bf16[192,384]{1,0:T(8,128)(2,1)S(1)}, bf16[192,384]{1,0:T(8,128)(2,1)S(1)}, u32[]{:S(2)}, u32[]{:S(2)}) collective-permute-start(bf16[192,384]{1,0:T(8,128)(2,1)S(1)} %get-tuple-element.24), channel_id=1, source_target_pairs={{8,0},{9,1},{10,2},{11,3},{12,4},{13,5},{14,6},{15,7},{0,8},{1,9},... | collective-permute-start | bytes 442376 | tf_op jit(solution)/shard_map/ppermute | solution.py:43
  22.3 17.7 %collective-permute-start = (bf16[192,384]{1,0:T(8,128)(2,1)S(1)}, bf16[192,384]{1,0:T(8,128)(2,1)S(1)}, u32[]{:S(2)}, u32[]{:S(2)}) collective-permute-start(bf16[192,384]{1,0:T(8,128)(2,1)S(1)} %get-tuple-element.25), channel_id=1, source_target_pairs={{3,0},{0,1},{1,2},{2,3},{7,4},{4,5},{5,6},{6,7},{11,8},{8,9},{9,10... | collective-permute-start | bytes 442376 | tf_op jit(solution)/shard_map/ppermute | solution.py:43
  23.9 16.0 %collective-permute-start.1 = (bf16[192,384]{1,0:T(8,128)(2,1)S(1)}, bf16[192,384]{1,0:T(8,128)(2,1)S(1)}, u32[]{:S(2)}, u32[]{:S(2)}) collective-permute-start(bf16[192,384]{1,0:T(8,128)(2,1)S(1)} %get-tuple-element.25), channel_id=1, source_target_pairs={{1,0},{2,1},{3,2},{0,3},{5,4},{6,5},{7,6},{4,7},{9,8},{10,9},{11,1... | collective-permute-start | bytes 442376 | tf_op jit(solution)/shard_map/ppermute | solution.py:43
  26.1 13.9 %collective-permute-start.2 = (bf16[192,384]{1,0:T(8,128)(2,1)S(1)}, bf16[192,384]{1,0:T(8,128)(2,1)S(1)}, u32[]{:S(2)}, u32[]{:S(2)}) collective-permute-start(bf16[192,384]{1,0:T(8,128)(2,1)S(1)} %get-tuple-element.25), channel_id=1, source_target_pairs={{2,0},{3,1},{0,2},{1,3},{6,4},{7,5},{4,6},{5,7},{10,8},{11,9},{8,1... | collective-permute-start | bytes 442376 | tf_op jit(solution)/shard_map/ppermute | solution.py:43
  29.7 84.3 %all-to-all-start = ((bf16[16,48,384]{2,1,0:T(8,128)(2,1)}), bf16[16,48,384]{2,1,0:T(8,128)(2,1)}, u32[]{:S(2)}, u32[]{:S(2)}) async-start(bf16[16,48,384]{2,1,0:T(8,128)(2,1)} %copy.43), calls=%async_computation | async-start | bytes 1179648 | tf_op jit(solution)/shard_map/all_to_all | solution.py:519
  34.0 210.1 %all-gather.9.cloned.1.call-start = ((), (), s32[]{:S(2)}) async-start(), calls=%async_computation.4 | async-start | bytes 5308416 | tf_op jit(solution)/shard_map/all_gather | solution.py:522
  37.2 23.9 %collective-permute-start.10 = (bf16[768,384]{1,0:T(8,128)(2,1)S(1)}, bf16[768,384]{1,0:T(8,128)(2,1)S(1)}, u32[]{:S(2)}, u32[]{:S(2)}) collective-permute-start(bf16[768,384]{1,0:T(8,128)(2,1)S(1)} %pad_maximum_fusion.1.refs_5_), channel_id=1, source_target_pairs={{3,0},{0,1},{1,2},{2,3},{7,4},{4,5},{5,6},{6,7},{11,8},{8,9},{9,10... | collective-permute-start | bytes 1769480 | tf_op jit(solution)/shard_map/ppermute | solution.py:43
  38.5 22.8 %collective-permute-start.11 = (bf16[768,384]{1,0:T(8,128)(2,1)S(1)}, bf16[768,384]{1,0:T(8,128)(2,1)S(1)}, u32[]{:S(2)}, u32[]{:S(2)}) collective-permute-start(bf16[768,384]{1,0:T(8,128)(2,1)S(1)} %pad_maximum_fusion.1.refs_5_), channel_id=1, source_target_pairs={{1,0},{2,1},{3,2},{0,3},{5,4},{6,5},{7,6},{4,7},{9,8},{10,9},{11,1... | collective-permute-start | bytes 1769480 | tf_op jit(solution)/shard_map/ppermute | solution.py:43
  40.0 24.5 %collective-permute-start.3 = (bf16[768,384]{1,0:T(8,128)(2,1)S(1)}, bf16[768,384]{1,0:T(8,128)(2,1)S(1)}, u32[]{:S(2)}, u32[]{:S(2)}) collective-permute-start(bf16[768,384]{1,0:T(8,128)(2,1)S(1)} %pad_maximum_fusion.refs_0_), channel_id=1, source_target_pairs={{12,0},{13,1},{14,2},{15,3},{0,4},{1,5},{2,6},{3,7},{4,8},{5,9},{6... | collective-permute-start | bytes 1769480 | tf_op jit(solution)/shard_map/ppermute | solution.py:43
  50.0 14.7 %collective-permute-start.4 = (bf16[768,384]{1,0:T(8,128)(2,1)S(1)}, bf16[768,384]{1,0:T(8,128)(2,1)S(1)}, u32[]{:S(2)}, u32[]{:S(2)}) collective-permute-start(bf16[768,384]{1,0:T(8,128)(2,1)S(1)} %pad_maximum_fusion.refs_0_), channel_id=1, source_target_pairs={{4,0},{5,1},{6,2},{7,3},{8,4},{9,5},{10,6},{11,7},{12,8},{13,9},{1... | collective-permute-start | bytes 1769480 | tf_op jit(solution)/shard_map/ppermute | solution.py:43
  61.1 15.9 %collective-permute-start.12 = (bf16[384,384]{1,0:T(8,128)(2,1)S(1)}, bf16[384,384]{1,0:T(8,128)(2,1)S(1)}, u32[]{:S(2)}, u32[]{:S(2)}) collective-permute-start(bf16[384,384]{1,0:T(8,128)(2,1)S(1)} %slice.92), channel_id=1, source_target_pairs={{3,0},{0,1},{1,2},{2,3},{7,4},{4,5},{5,6},{6,7},{11,8},{8,9},{9,10... | collective-permute-start | bytes 884744 | tf_op jit(solution)/shard_map/ppermute | solution.py:43
  61.3 15.8 %collective-permute-start.13 = (bf16[384,384]{1,0:T(8,128)(2,1)S(1)}, bf16[384,384]{1,0:T(8,128)(2,1)S(1)}, u32[]{:S(2)}, u32[]{:S(2)}) collective-permute-start(bf16[384,384]{1,0:T(8,128)(2,1)S(1)} %slice.93), channel_id=1, source_target_pairs={{1,0},{2,1},{3,2},{0,3},{5,4},{6,5},{7,6},{4,7},{9,8},{10,9},{11,1... | collective-permute-start | bytes 884744 | tf_op jit(solution)/shard_map/ppermute | solution.py:43
  64.6 15.9 %collective-permute-start.5 = (bf16[384,384]{1,0:T(8,128)(2,1)S(1)}, bf16[384,384]{1,0:T(8,128)(2,1)S(1)}, u32[]{:S(2)}, u32[]{:S(2)}) collective-permute-start(bf16[384,384]{1,0:T(8,128)(2,1)S(1)} %slice.89), channel_id=1, source_target_pairs={{12,0},{13,1},{14,2},{15,3},{0,4},{1,5},{2,6},{3,7},{4,8},{5,9},{6... | collective-permute-start | bytes 884744 | tf_op jit(solution)/shard_map/ppermute | solution.py:43
  64.7 16.2 %collective-permute-start.6 = (bf16[384,384]{1,0:T(8,128)(2,1)S(1)}, bf16[384,384]{1,0:T(8,128)(2,1)S(1)}, u32[]{:S(2)}, u32[]{:S(2)}) collective-permute-start(bf16[384,384]{1,0:T(8,128)(2,1)S(1)} %slice.90), channel_id=1, source_target_pairs={{4,0},{5,1},{6,2},{7,3},{8,4},{9,5},{10,6},{11,7},{12,8},{13,9},{1... | collective-permute-start | bytes 884744 | tf_op jit(solution)/shard_map/ppermute | solution.py:43
  114.0 39.8 %copy-start.16 = (s32[2]{0:T(128)S(1)}, s32[2]{0:T(128)}, u32[]{:S(2)}) copy-start(s32[2]{0:T(128)} %param.29) | copy-start | bytes 28
  114.0 40.0 %copy-start.6 = (bf16[384,128]{1,0:T(8,128)(2,1)S(1)}, bf16[384,128]{1,0:T(8,128)(2,1)}, u32[]{:S(2)}) copy-start(bf16[384,128]{1,0:T(8,128)(2,1)} %copy-done.5) | copy-start | bytes 294916
  126.8 123.0 %all-gather.7.cloned.1.call-start = ((), (), s32[]{:S(2)}) async-start(), calls=%async_computation.3 | async-start | bytes 8355840 | tf_op jit(solution)/shard_map/all_gather | solution.py:532
  126.9 7.3 %collective-permute-start.21 = (bf16[128,384]{1,0:T(8,128)(2,1)S(1)}, bf16[128,384]{1,0:T(8,128)(2,1)S(1)}, u32[]{:S(2)}, u32[]{:S(2)}) collective-permute-start(bf16[128,384]{1,0:T(8,128)(2,1)S(1)} %get-tuple-element.26), channel_id=1, source_target_pairs={{12,0},{13,1},{14,2},{15,3},{0,4},{1,5},{2,6},{3,7},{4,8},{5,9},{6... | collective-permute-start | bytes 294920 | tf_op jit(solution)/shard_map/ppermute | solution.py:43
  128.2 7.0 %collective-permute-start.22 = (bf16[128,384]{1,0:T(8,128)(2,1)S(1)}, bf16[128,384]{1,0:T(8,128)(2,1)S(1)}, u32[]{:S(2)}, u32[]{:S(2)}) collective-permute-start(bf16[128,384]{1,0:T(8,128)(2,1)S(1)} %get-tuple-element.26), channel_id=1, source_target_pairs={{4,0},{5,1},{6,2},{7,3},{8,4},{9,5},{10,6},{11,7},{12,8},{13,9},{1... | collective-permute-start | bytes 294920 | tf_op jit(solution)/shard_map/ppermute | solution.py:43
  130.5 5.6 %collective-permute-start.23 = (bf16[128,384]{1,0:T(8,128)(2,1)S(1)}, bf16[128,384]{1,0:T(8,128)(2,1)S(1)}, u32[]{:S(2)}, u32[]{:S(2)}) collective-permute-start(bf16[128,384]{1,0:T(8,128)(2,1)S(1)} %get-tuple-element.26), channel_id=1, source_target_pairs={{8,0},{9,1},{10,2},{11,3},{12,4},{13,5},{14,6},{15,7},{0,8},{1,9},... | collective-permute-start | bytes 294920 | tf_op jit(solution)/shard_map/ppermute | solution.py:43
  131.6 7.3 %collective-permute-start.14 = (bf16[128,384]{1,0:T(8,128)(2,1)S(1)}, bf16[128,384]{1,0:T(8,128)(2,1)S(1)}, u32[]{:S(2)}, u32[]{:S(2)}) collective-permute-start(bf16[128,384]{1,0:T(8,128)(2,1)S(1)} %get-tuple-element.27), channel_id=1, source_target_pairs={{3,0},{0,1},{1,2},{2,3},{7,4},{4,5},{5,6},{6,7},{11,8},{8,9},{9,10... | collective-permute-start | bytes 294920 | tf_op jit(solution)/shard_map/ppermute | solution.py:43
  133.4 5.5 %collective-permute-start.15 = (bf16[128,384]{1,0:T(8,128)(2,1)S(1)}, bf16[128,384]{1,0:T(8,128)(2,1)S(1)}, u32[]{:S(2)}, u32[]{:S(2)}) collective-permute-start(bf16[128,384]{1,0:T(8,128)(2,1)S(1)} %get-tuple-element.27), channel_id=1, source_target_pairs={{1,0},{2,1},{3,2},{0,3},{5,4},{6,5},{7,6},{4,7},{9,8},{10,9},{11,1... | collective-permute-start | bytes 294920 | tf_op jit(solution)/shard_map/ppermute | solution.py:43
  134.3 5.0 %collective-permute-start.16 = (bf16[128,384]{1,0:T(8,128)(2,1)S(1)}, bf16[128,384]{1,0:T(8,128)(2,1)S(1)}, u32[]{:S(2)}, u32[]{:S(2)}) collective-permute-start(bf16[128,384]{1,0:T(8,128)(2,1)S(1)} %get-tuple-element.27), channel_id=1, source_target_pairs={{2,0},{3,1},{0,2},{1,3},{6,4},{7,5},{4,6},{5,7},{10,8},{11,9},{8,1... | collective-permute-start | bytes 294920 | tf_op jit(solution)/shard_map/ppermute | solution.py:43
  136.1 11.9 %collective-permute-start.24 = (bf16[512,384]{1,0:T(8,128)(2,1)S(1)}, bf16[512,384]{1,0:T(8,128)(2,1)S(1)}, u32[]{:S(2)}, u32[]{:S(2)}) collective-permute-start(bf16[512,384]{1,0:T(8,128)(2,1)S(1)} %pad_maximum_fusion.3.refs_5_), channel_id=1, source_target_pairs={{3,0},{0,1},{1,2},{2,3},{7,4},{4,5},{5,6},{6,7},{11,8},{8,9},{9,10... | collective-permute-start | bytes 1179656 | tf_op jit(solution)/shard_map/ppermute | solution.py:43
  138.0 10.1 %collective-permute-start.25 = (bf16[512,384]{1,0:T(8,128)(2,1)S(1)}, bf16[512,384]{1,0:T(8,128)(2,1)S(1)}, u32[]{:S(2)}, u32[]{:S(2)}) collective-permute-start(bf16[512,384]{1,0:T(8,128)(2,1)S(1)} %pad_maximum_fusion.3.refs_5_), channel_id=1, source_target_pairs={{1,0},{2,1},{3,2},{0,3},{5,4},{6,5},{7,6},{4,7},{9,8},{10,9},{11,1... | collective-permute-start | bytes 1179656 | tf_op jit(solution)/shard_map/ppermute | solution.py:43
  139.3 11.5 %collective-permute-start.17 = (bf16[512,384]{1,0:T(8,128)(2,1)S(1)}, bf16[512,384]{1,0:T(8,128)(2,1)S(1)}, u32[]{:S(2)}, u32[]{:S(2)}) collective-permute-start(bf16[512,384]{1,0:T(8,128)(2,1)S(1)} %pad_maximum_fusion.2.refs_0_), channel_id=1, source_target_pairs={{12,0},{13,1},{14,2},{15,3},{0,4},{1,5},{2,6},{3,7},{4,8},{5,9},{6... | collective-permute-start | bytes 1179656 | tf_op jit(solution)/shard_map/ppermute | solution.py:43
  140.3 11.1 %collective-permute-start.18 = (bf16[512,384]{1,0:T(8,128)(2,1)S(1)}, bf16[512,384]{1,0:T(8,128)(2,1)S(1)}, u32[]{:S(2)}, u32[]{:S(2)}) collective-permute-start(bf16[512,384]{1,0:T(8,128)(2,1)S(1)} %pad_maximum_fusion.2.refs_0_), channel_id=1, source_target_pairs={{4,0},{5,1},{6,2},{7,3},{8,4},{9,5},{10,6},{11,7},{12,8},{13,9},{1... | collective-permute-start | bytes 1179656 | tf_op jit(solution)/shard_map/ppermute | solution.py:43
  148.0 6.2 %collective-permute-start.26 = (bf16[256,384]{1,0:T(8,128)(2,1)S(1)}, bf16[256,384]{1,0:T(8,128)(2,1)S(1)}, u32[]{:S(2)}, u32[]{:S(2)}) collective-permute-start(bf16[256,384]{1,0:T(8,128)(2,1)S(1)} %slice.101), channel_id=1, source_target_pairs={{3,0},{0,1},{1,2},{2,3},{7,4},{4,5},{5,6},{6,7},{11,8},{8,9},{9,10... | collective-permute-start | bytes 589832 | tf_op jit(solution)/shard_map/ppermute | solution.py:43
  148.2 6.1 %collective-permute-start.27 = (bf16[256,384]{1,0:T(8,128)(2,1)S(1)}, bf16[256,384]{1,0:T(8,128)(2,1)S(1)}, u32[]{:S(2)}, u32[]{:S(2)}) collective-permute-start(bf16[256,384]{1,0:T(8,128)(2,1)S(1)} %slice.102), channel_id=1, source_target_pairs={{1,0},{2,1},{3,2},{0,3},{5,4},{6,5},{7,6},{4,7},{9,8},{10,9},{11,1... | collective-permute-start | bytes 589832 | tf_op jit(solution)/shard_map/ppermute | solution.py:43
  150.9 6.2 %collective-permute-start.19 = (bf16[256,384]{1,0:T(8,128)(2,1)S(1)}, bf16[256,384]{1,0:T(8,128)(2,1)S(1)}, u32[]{:S(2)}, u32[]{:S(2)}) collective-permute-start(bf16[256,384]{1,0:T(8,128)(2,1)S(1)} %slice.99), channel_id=1, source_target_pairs={{12,0},{13,1},{14,2},{15,3},{0,4},{1,5},{2,6},{3,7},{4,8},{5,9},{6... | collective-permute-start | bytes 589832 | tf_op jit(solution)/shard_map/ppermute | solution.py:43
  151.4 5.7 %collective-permute-start.20 = (bf16[256,384]{1,0:T(8,128)(2,1)S(1)}, bf16[256,384]{1,0:T(8,128)(2,1)S(1)}, u32[]{:S(2)}, u32[]{:S(2)}) collective-permute-start(bf16[256,384]{1,0:T(8,128)(2,1)S(1)} %slice.100), channel_id=1, source_target_pairs={{4,0},{5,1},{6,2},{7,3},{8,4},{9,5},{10,6},{11,7},{12,8},{13,9},{1... | collective-permute-start | bytes 589832 | tf_op jit(solution)/shard_map/ppermute | solution.py:43
  154.0 9.0 %collective-permute-start.28 = (bf16[384,128]{1,0:T(8,128)(2,1)S(1)}, bf16[384,128]{1,0:T(8,128)(2,1)S(1)}, u32[]{:S(2)}, u32[]{:S(2)}) collective-permute-start(bf16[384,128]{1,0:T(8,128)(2,1)S(1)} %copy-done.6), channel_id=1, source_target_pairs={{0,1},{1,0},{2,3},{3,2},{4,5},{5,4},{6,7},{7,6},{8,9},{9,8},{10,11... | collective-permute-start | bytes 294920 | tf_op jit(solution)/shard_map/ppermute | solution.py:515
  162.7 3.4 %collective-permute-start.29 = (bf16[256,128]{1,0:T(8,128)(2,1)S(1)}, bf16[256,128]{1,0:T(8,128)(2,1)S(1)}, u32[]{:S(2)}, u32[]{:S(2)}) collective-permute-start(bf16[256,128]{1,0:T(8,128)(2,1)S(1)} %get-tuple-element.19.oi), channel_id=1, source_target_pairs={{0,1},{1,0},{2,3},{3,2},{4,5},{5,4},{6,7},{7,6},{8,9},{9,8},{10,11... | collective-permute-start | bytes 196616 | tf_op jit(solution)/shard_map/ppermute | solution.py:526
  177.0 4.5 %collective-permute-start.30 = (f32[2,6144]{1,0:T(2,128)S(1)}, f32[2,6144]{1,0:T(2,128)S(1)}, u32[]{:S(2)}, u32[]{:S(2)}) collective-permute-start(f32[2,6144]{1,0:T(2,128)S(1)} %convolution_add_fusion), channel_id=1, source_target_pairs={{2,0},{3,1},{0,2},{1,3},{6,4},{7,5},{4,6},{5,7},{10,8},{11,9},{8,1... | collective-permute-start | bytes 147464 | tf_op jit(solution)/shard_map/ppermute | solution.py:43
  177.5 4.5 %collective-permute-start.31 = (f32[2,6144]{1,0:T(2,128)S(1)}, f32[2,6144]{1,0:T(2,128)S(1)}, u32[]{:S(2)}, u32[]{:S(2)}) collective-permute-start(f32[2,6144]{1,0:T(2,128)S(1)} %convolution_add_fusion), channel_id=1, source_target_pairs={{3,0},{0,1},{1,2},{2,3},{7,4},{4,5},{5,6},{6,7},{11,8},{8,9},{9,10... | collective-permute-start | bytes 147464 | tf_op jit(solution)/shard_map/ppermute | solution.py:43
  177.5 4.4 %collective-permute-start.32 = (f32[2,6144]{1,0:T(2,128)S(1)}, f32[2,6144]{1,0:T(2,128)S(1)}, u32[]{:S(2)}, u32[]{:S(2)}) collective-permute-start(f32[2,6144]{1,0:T(2,128)S(1)} %convolution_add_fusion), channel_id=1, source_target_pairs={{1,0},{2,1},{3,2},{0,3},{5,4},{6,5},{7,6},{4,7},{9,8},{10,9},{11,1... | collective-permute-start | bytes 147464 | tf_op jit(solution)/shard_map/ppermute | solution.py:43
  182.0 4.5 %collective-permute-start.33 = (f32[2,6144]{1,0:T(2,128)S(1)}, f32[2,6144]{1,0:T(2,128)S(1)}, u32[]{:S(2)}, u32[]{:S(2)}) collective-permute-start(f32[2,6144]{1,0:T(2,128)S(1)} %add_add_fusion), channel_id=1, source_target_pairs={{8,0},{9,1},{10,2},{11,3},{12,4},{13,5},{14,6},{15,7},{0,8},{1,9},... | collective-permute-start | bytes 147464 | tf_op jit(solution)/shard_map/ppermute | solution.py:43
  183.4 4.2 %collective-permute-start.34 = (f32[2,6144]{1,0:T(2,128)S(1)}, f32[2,6144]{1,0:T(2,128)S(1)}, u32[]{:S(2)}, u32[]{:S(2)}) collective-permute-start(f32[2,6144]{1,0:T(2,128)S(1)} %add_add_fusion), channel_id=1, source_target_pairs={{12,0},{13,1},{14,2},{15,3},{0,4},{1,5},{2,6},{3,7},{4,8},{5,9},{6... | collective-permute-start | bytes 147464 | tf_op jit(solution)/shard_map/ppermute | solution.py:43
  185.4 4.1 %collective-permute-start.35 = (f32[2,6144]{1,0:T(2,128)S(1)}, f32[2,6144]{1,0:T(2,128)S(1)}, u32[]{:S(2)}, u32[]{:S(2)}) collective-permute-start(f32[2,6144]{1,0:T(2,128)S(1)} %add_add_fusion), channel_id=1, source_target_pairs={{4,0},{5,1},{6,2},{7,3},{8,4},{9,5},{10,6},{11,7},{12,8},{13,9},{1... | collective-permute-start | bytes 147464 | tf_op jit(solution)/shard_map/ppermute | solution.py:43
  214.2 4.6 %collective-permute-start.36 = (f32[16]{0:T(128)S(1)}, f32[16]{0:T(128)S(1)}, u32[]{:S(2)}, u32[]{:S(2)}) collective-permute-start(f32[16]{0:T(128)S(1)} %convolution_reduce_fusion), channel_id=1, source_target_pairs={{3,0},{0,1},{1,2},{2,3},{7,4},{4,5},{5,6},{6,7},{11,8},{8,9},{9,10... | collective-permute-start | bytes 200 | tf_op jit(solution)/shard_map/ppermute | solution.py:43
  215.5 3.4 %collective-permute-start.37 = (f32[16]{0:T(128)S(1)}, f32[16]{0:T(128)S(1)}, u32[]{:S(2)}, u32[]{:S(2)}) collective-permute-start(f32[16]{0:T(128)S(1)} %convolution_reduce_fusion), channel_id=1, source_target_pairs={{1,0},{2,1},{3,2},{0,3},{5,4},{6,5},{7,6},{4,7},{9,8},{10,9},{11,1... | collective-permute-start | bytes 200 | tf_op jit(solution)/shard_map/ppermute | solution.py:43
  217.6 4.0 %collective-permute-start.38 = (f32[16]{0:T(128)S(1)}, f32[16]{0:T(128)S(1)}, u32[]{:S(2)}, u32[]{:S(2)}) collective-permute-start(f32[16]{0:T(128)S(1)} %convolution_reduce_fusion), channel_id=1, source_target_pairs={{2,0},{3,1},{0,2},{1,3},{6,4},{7,5},{4,6},{5,7},{10,8},{11,9},{8,1... | collective-permute-start | bytes 200 | tf_op jit(solution)/shard_map/ppermute | solution.py:43
  221.6 4.0 %collective-permute-start.39 = (f32[16]{0:T(128)S(1)}, f32[16]{0:T(128)S(1)}, u32[]{:S(2)}, u32[]{:S(2)}) collective-permute-start(f32[16]{0:T(128)S(1)} %maximum_maximum_fusion.1), channel_id=1, source_target_pairs={{12,0},{13,1},{14,2},{15,3},{0,4},{1,5},{2,6},{3,7},{4,8},{5,9},{6... | collective-permute-start | bytes 200 | tf_op jit(solution)/shard_map/ppermute | solution.py:43
  221.6 4.0 %collective-permute-start.40 = (f32[16]{0:T(128)S(1)}, f32[16]{0:T(128)S(1)}, u32[]{:S(2)}, u32[]{:S(2)}) collective-permute-start(f32[16]{0:T(128)S(1)} %maximum_maximum_fusion.1), channel_id=1, source_target_pairs={{4,0},{5,1},{6,2},{7,3},{8,4},{9,5},{10,6},{11,7},{12,8},{13,9},{1... | collective-permute-start | bytes 200 | tf_op jit(solution)/shard_map/ppermute | solution.py:43
  224.3 4.0 %collective-permute-start.41 = (f32[16]{0:T(128)S(1)}, f32[16]{0:T(128)S(1)}, u32[]{:S(2)}, u32[]{:S(2)}) collective-permute-start(f32[16]{0:T(128)S(1)} %maximum_maximum_fusion.1), channel_id=1, source_target_pairs={{8,0},{9,1},{10,2},{11,3},{12,4},{13,5},{14,6},{15,7},{0,8},{1,9},... | collective-permute-start | bytes 200 | tf_op jit(solution)/shard_map/ppermute | solution.py:43
  (18 other events, 263.6 us)
Sparse Core Ops, SparseCore 0:
  12.1 89.4 all-gather.4
  127.0 34.0 all-gather.8
  172.9 70.7 all-gather.6

commit v2 on v1

--- a/solution.py
+++ b/solution.py
@@ -258,7 +258,7 @@
 
     def kernel(src_ref, *refs):
         ins = refs[:n]
-        w_hbm, cos_ref, sin_ref, q_ref, kv_ref, xs, w, acc, sq, sem = refs[n:]
+        w_hbm, cos_ref, sin_ref, q_ref, kv_ref, xs, w, acc, sem = refs[n:]
 
         def copy(k):
             there = pl.ds(pl.multiple_of(src_ref[k] * FEAT, FEAT), FEAT)
@@ -267,24 +267,24 @@
 
         for k in range(N_HID):
             copy(k).start()
+        square = jnp.zeros((rows, HEAD_DIM), F32)
         for k in range(N_HID):
             block = jnp.concatenate([ins[a][row : row + half, :] for a, row in where[k]], axis=0)
             xs[:, k * FEAT : (k + 1) * FEAT] = block
+            v = block.astype(F32)
+            v = v * v
+            square = square + (v[:, 0:128] + v[:, 128:256] + v[:, 256:384])
         acc[...] = jnp.zeros_like(acc)
-        sq[...] = jnp.zeros_like(sq)
 
         def step(i, carry):
             for j in range(4):
                 copy(4 * i + j).wait()
             here = pl.ds(pl.multiple_of(i * deep, deep), deep)
             acc[...] += jnp.dot(xs[:, here], w[here, :], preferred_element_type=F32)
-            v = xs[:, here].astype(F32)
-            v = v * v
-            sq[...] += sum(v[:, c : c + 128] for c in range(0, deep, 128))
             return carry
 
         lax.fori_loop(0, RING, step, 0)
-        scale = lax.rsqrt(jnp.sum(sq[...], axis=1, keepdims=True) * (1.0 / D) + 1e-05)
+        scale = lax.rsqrt(jnp.sum(square, axis=1, keepdims=True) * (1.0 / D) + 1e-05)
         for h in range(FEAT // HEAD_DIM):
             part = acc[:, h * HEAD_DIM : (h + 1) * HEAD_DIM] * scale
             q_ref[:, h * HEAD_DIM : (h + 1) * HEAD_DIM] = turn(
@@ -306,7 +306,6 @@
             VM((rows, D), BF),
             VM((D, cols), BF),
             VM((rows, cols), F32),
-            VM((rows, HEAD_DIM), F32),
             pltpu.SemaphoreType.DMA((N_HID,)),
         ],
         compiler_params=params(20),
@@ -374,23 +373,28 @@
 
     def a_copy(k):
         here = pl.ds(pl.multiple_of(k * FEAT, FEAT), FEAT)
-        return pltpu.make_async_copy(a_hbm.at[pl.ds(k * LIVE, LIVE), :], a.at[:, here], a_sem.at[k])
-
-    def w_copy(k):
-        here = pl.ds(k * FEAT, FEAT)
-        return pltpu.make_async_copy(w_hbm.at[here, :], w.at[here, :], w_sem.at[k])
-
-    for k in range(N_HID):
+        return pltpu.make_async_copy(a_hbm.at[pl.ds(pl.multiple_of(k * LIVE, LIVE), LIVE), :], a.at[:, here], a_sem.at[k])
+
+    def w_copy(k, r):
+        return pltpu.make_async_copy(w_hbm.at[r, k], w.at[k, r], w_sem.at[k, r])
+
+    def begin(k, carry):
         a_copy(k).start()
-        w_copy(k).start()
+        for r in range(N_REQ):
+            w_copy(k, r).start()
+        return carry
+
+    lax.fori_loop(0, N_HID, begin, 0)
     acc[...] = jnp.zeros_like(acc)
 
     def step(i, carry):
         for j in (0, 1):
             a_copy(2 * i + j).wait()
-            w_copy(2 * i + j).wait()
+            for r in range(N_REQ):
+                w_copy(2 * i + j, r).wait()
         here = pl.ds(pl.multiple_of(i * two, two), two)
-        acc[...] += jnp.dot(a[:, here], w[here, :], preferred_element_type=F32)
+        block = w[pl.ds(2 * i, 2)].reshape(two, FEAT)
+        acc[...] += jnp.dot(a[:, here], block, preferred_element_type=F32)
         return carry
 
     lax.fori_loop(0, N_HID // 2, step, 0)
@@ -416,11 +420,11 @@
         out_specs=vmem(),
         scratch_shapes=[
             VM((LIVE, D), BF),
-            VM((D, FEAT), BF),
+            VM((N_HID, N_REQ, FEAT // N_REQ, FEAT), BF),
             VM((LIVE, FEAT), F32),
             VM((LIVE, FEAT), BF),
             pltpu.SemaphoreType.DMA((N_HID,)),
-            pltpu.SemaphoreType.DMA((N_HID,)),
+            pltpu.SemaphoreType.DMA((N_HID, N_REQ)),
         ],
         compiler_params=params(32),
         cost_estimate=pl.CostEstimate(
@@ -498,6 +502,11 @@
     ).astype(BF)
     partner = [(i, i ^ 1) for i in range(N_HID)]
     text_blocks, text_where = gather_far(gather_near(text_rows))
+    strip = FEAT // N_REQ
+    piece = lax.dynamic_slice_in_dim(out_weight, me * strip, strip, axis=0)
+    piece = piece.reshape(strip, N_HID, FEAT).transpose(1, 0, 2)
+    piece, *text_blocks[3:5] = lax.optimization_barrier((piece, *text_blocks[3:5]))
+    piece = lax.all_to_all(piece, "hid", split_axis=0, concat_axis=0, tiled=True)
     q_text, kv_text = qkv(
         text_blocks, text_where, weight, cos[:TEXT], sin[:TEXT], sources, "qkv_text"
     )
@@ -513,13 +522,9 @@
         projected.reshape(N_REQ, TILE // N_REQ, FEAT), "req", split_axis=0, concat_axis=0, tiled=True
     ).reshape(TILE, FEAT)
     other_text = lax.ppermute(kv_text, "hid", partner)
-    strip = FEAT // N_REQ
-    piece = lax.dynamic_slice_in_dim(out_weight, me * strip, strip, axis=0)
-    piece = piece.reshape(strip, N_HID, FEAT).transpose(1, 0, 2)
-    piece = lax.all_to_all(piece, "hid", split_axis=0, concat_axis=0, tiled=True)
     piece, tile = lax.optimization_barrier((piece, tile))
     tile_blocks, tile_where = gather_far(gather_near(tile))
-    columns = lax.all_gather(piece, "req", axis=1, tiled=True).reshape(D, FEAT)
+    columns = lax.all_gather(piece, "req", axis=0, tiled=False)
     q_tile, kv_tile = qkv(
         tile_blocks, tile_where, weight, cos[TEXT:], sin[TEXT:], sources, "qkv_tile"
     )

time: 267 us -> 262 us (0.981)
  waiting for transfers between devices: 48.8 us -> 37.5 us
  other arithmetic: 18.5 us -> 23.8 us
    ppermute x40, waiting for transfers between devices: 33.7 us -> 24.9 us  [shift(): return lax.ppermute(block, 'hid', route)]
    all_gather x1 -> x0, local copies, waits for them, and re-layouts: 5.73 us -> none  [shards(): columns = lax.all_gather(piece, 'req', axis=1, tiled=True).reshape(D, FEAT)]
    unnamed x45 -> x39, local copies, waits for them, and re-layouts: 7.2 us -> 10.7 us
    all_gather x1, waiting for transfers between devices: 12 us -> 9.32 us  [shards(): lax.all_gather(pack(merged, tile_order, (hid % RING)[None]), 'hid', axis=...]
  transfers between devices with their start and end apart: 46 -> 46, of which waited for: 20 -> 19; matrix products, arithmetic and copies ran while one was open for 16% -> 19% of each run, Pallas kernels for 12% -> 11%
where the time goes in v2:
time: 262 us; the launch traced here: 261 us
  starting transfers between devices  62.6 us (24%)
  blocking collectives  47 us (18%)
  Pallas kernels  41.9 us (16%)
  waiting for transfers between devices  37.5 us (14%)
  other arithmetic  23.8 us (9%)
  local copies, waits for them, and re-layouts  22.5 us (9%)
  between operations  16.2 us (6%)
  matrix products  9.21 us (4%)
    ppermute x40, starting transfers between devices, shift(): return lax.ppermute(block, 'hid', route)  57.6 us
    ppermute x40, waiting for transfers between devices, shift(): return lax.ppermute(block, 'hid', route)  24.9 us
    all_gather x1, blocking collectives, shards(): all_last = lax.all_gather(full_width, 'req', axis=0, tiled=True)  20.3 us
    pmax x1, blocking collectives, shards(): logit_max = lax.pmax(top, 'req')  15.8 us
    pallas_call x1, Pallas kernels, project(): pl.pallas_call(project_kernel, out_shape=jax.ShapeDtypeStruct((TILE, FEAT...  11.6 us
    all_to_all x1, blocking collectives, shards(): lax.all_to_all(projected.reshape(N_REQ, TILE // N_REQ, FEAT), 'req', spli...  10.8 us
    pallas_call x1, Pallas kernels, finish(): pl.pallas_call(finish_kernel, out_shape=jax.ShapeDtypeStruct((REQ_GRP, LE...  10.7 us
    unnamed x39, local copies, waits for them, and re-layouts  10.7 us
  transfers between devices with their start and end apart: 46, of which 19 were waited for; matrix products, arithmetic and copies ran while one was open for 19% of the time, Pallas kernels for 11%

profile of v2, /device:TPU:1, one launch (start us, length us, event | category | flops | bytes accessed | tf_op | source)
XLA Modules:
  0.0 260.6 jit_solution(6089589008103886404)
XLA Ops:
  9.7 2.3 pack.1
  14.6 1.7 fusion.1
  16.4 2.5 collective-permute-start
  18.9 2.2 collective-permute-start.1
  25.0 1.8 copy.58
  26.8 1.8 copy.59
  28.6 7.7 %multiply_convert_fusion.refs_10_ = bf16[6144,512]{1,0:T(8,128)(2,1)} fusion(bf16[6144,64]{1,0:T(8,128)(2,1)S(1)} %copy.59, bf16[6144,64]{1,0:T(8,128)(2,1)S(1)} %copy.58, bf16[6144,384]{1,0:T(8,128)(2,1)} %param.23, f32[6144]{0:T(1024)S(1)} %convert_element_type.43), kind=kLoop, calls=%fused_computation | loop fusion | flops 25165824 | bytes 12607488 | tf_op jit(solution)/shard_map/convert_element_type | solution.py:502
  37.9 1.9 constant_dynamic-slice_fusion
  41.3 2.4 collective-permute-start.5
  45.5 1.9 collective-permute-start.11
  47.5 2.0 copy.61
  53.8 2.1 multiply_sine_fusion
  58.0 2.0 collective-permute-start.4
  60.8 1.8 collective-permute-start.6
  65.7 4.0 %collective-permute-done.11.refs_7_ = bf16[768,384]{1,0:T(8,128)(2,1)S(1)} collective-permute-done((bf16[768,384]{1,0:T(8,128)(2,1)S(1)}, bf16[768,384]{1,0:T(8,128)(2,1)S(1)}, u32[]{:S(2)}, u32[]{:S(2)}) %collective-permute-start.11) | collective-permute-done | bytes 589856 | tf_op jit(solution)/shard_map/ppermute | solution.py:43
  70.5 3.5 %collective-permute-start.13 = (bf16[384,384]{1,0:T(8,128)(2,1)}, bf16[384,384]{1,0:T(8,128)(2,1)}, u32[]{:S(2)}, u32[]{:S(2)}) collective-permute-start(bf16[384,384]{1,0:T(8,128)(2,1)} %slice.93), channel_id=1, source_target_pairs={{1,0},{2,1},{3,2},{0,3},{5,4},{6,5},{7,6},{4,7},{9,8},{10,9},{11,1... | collective-permute-start | bytes 884744 | tf_op jit(solution)/shard_map/ppermute | solution.py:43
  74.0 1.8 fusion.6.refs_11_
  75.8 1.8 fusion.5.refs_12_
  77.7 2.0 copy.57
  79.7 4.3 %all-to-all-start = ((bf16[16,48,384]{2,1,0:T(8,128)(2,1)}), bf16[16,48,384]{2,1,0:T(8,128)(2,1)}, u32[]{:S(2)}, u32[]{:S(2)}) async-start(bf16[16,48,384]{2,1,0:T(8,128)(2,1)} %copy.57), calls=%async_computation | async-start | bytes 1179648 | tf_op jit(solution)/shard_map/all_to_all | solution.py:509
  87.1 6.2 %qkv_text.1 = (bf16[384,384]{1,0:T(8,128)(2,1)S(1)}, bf16[384,128]{1,0:T(8,128)(2,1)S(1)}) custom-call(s32[16]{0:T(128)S(1)} %fusion.22.src_ref, bf16[768,384]{1,0:T(8,128)(2,1)S(1)} %pad_maximum_fusion.refs_0_, bf16[768,384]{1,0:T(8,128)(2,1)S(1)} %collective-permute-done.3.refs_1_, bf16[768,384]{1,0:T(8,128)(2,1)S(1)} %collective-permute-done.5.refs_2_, ...), custom_call_target="tpu_custom_call" | custom-call | flops 2415919104 | bytes 12582912 | tf_op jit(solution)/shard_map/qkv_text/pallas_call | solution.py:295
  94.6 9.3 %all-gather.6.cloned.1.call-done.x_hbm = bf16[4096,896]{1,0:T(8,128)(2,1)} async-done(((bf16[256,896]{1,0:T(8,128)(2,1)}), bf16[4096,896]{1,0:T(8,128)(2,1)}) %all-gather.6.cloned.1.call-update) | async-done | bytes 7340048 | tf_op jit(solution)/shard_map/all_gather | solution.py:493
  104.8 11.6 %project.1 = bf16[256,384]{1,0:T(8,128)(2,1)S(1)} custom-call(bf16[4096,896]{1,0:T(8,128)(2,1)} %all-gather.6.cloned.1.call-done.x_hbm, bf16[16,800,384]{2,1,0:T(8,128)(2,1)} %bitcast.31, f32[2,16,768]{2,1,0:T(8,128)S(1)} %copy-done.4, f32[2,4,1,128]{3,2,1,0:T(1,128)S(1)} %reshape.310.left_ref, f32[1,384]{1,0:T(1,128)S(1)} %broadcast_in_dim.108.pb_ref), custom_call_target="tpu_custom_call" | custom-call | flops 2516582400 | bytes 17825792 | tf_op jit(solution)/shard_map/project/pallas_call | solution.py:219
  116.4 10.8 %all_to_all.10 = bf16[8,32,384]{2,1,0:T(8,128)(2,1)S(1)} all-to-all(bf16[8,32,384]{2,1,0:T(8,128)(2,1)S(1)} %bitcast.29), channel_id=1, replica_groups=mesh['req'=8,'hid'=16] {'req'}, dimensions={0} | all-to-all | bytes 393216 | tf_op jit(solution)/shard_map/all_to_all | solution.py:521
  127.4 2.7 %collective-permute-start.22 = (bf16[128,384]{1,0:T(8,128)(2,1)S(1)}, bf16[128,384]{1,0:T(8,128)(2,1)S(1)}, u32[]{:S(2)}, u32[]{:S(2)}) collective-permute-start(bf16[128,384]{1,0:T(8,128)(2,1)S(1)} %get-tuple-element.32), channel_id=1, source_target_pairs={{4,0},{5,1},{6,2},{7,3},{8,4},{9,5},{10,6},{11,7},{12,8},{13,9},{1... | collective-permute-start | bytes 294920 | tf_op jit(solution)/shard_map/ppermute | solution.py:43
  130.5 3.7 %collective-permute-start.15 = (bf16[128,384]{1,0:T(8,128)(2,1)S(1)}, bf16[128,384]{1,0:T(8,128)(2,1)S(1)}, u32[]{:S(2)}, u32[]{:S(2)}) collective-permute-start(bf16[128,384]{1,0:T(8,128)(2,1)S(1)} %get-tuple-element.33), channel_id=1, source_target_pairs={{1,0},{2,1},{3,2},{0,3},{5,4},{6,5},{7,6},{4,7},{9,8},{10,9},{11,1... | collective-permute-start | bytes 294920 | tf_op jit(solution)/shard_map/ppermute | solution.py:43
  136.9 2.5 collective-permute-start.25
  140.7 2.1 collective-permute-start.18
  145.1 3.1 %collective-permute-done.24.refs_6_ = bf16[512,384]{1,0:T(8,128)(2,1)S(1)} collective-permute-done((bf16[512,384]{1,0:T(8,128)(2,1)S(1)}, bf16[512,384]{1,0:T(8,128)(2,1)S(1)}, u32[]{:S(2)}, u32[]{:S(2)}) %collective-permute-start.24) | collective-permute-done | bytes 393248 | tf_op jit(solution)/shard_map/ppermute | solution.py:43
  148.4 2.7 %collective-permute-start.27 = (bf16[256,384]{1,0:T(8,128)(2,1)S(1)}, bf16[256,384]{1,0:T(8,128)(2,1)S(1)}, u32[]{:S(2)}, u32[]{:S(2)}) collective-permute-start(bf16[256,384]{1,0:T(8,128)(2,1)S(1)} %slice.102), channel_id=1, source_target_pairs={{1,0},{2,1},{3,2},{0,3},{5,4},{6,5},{7,6},{4,7},{9,8},{10,9},{11,1... | collective-permute-start | bytes 589832 | tf_op jit(solution)/shard_map/ppermute | solution.py:43
  151.9 2.0 collective-permute-start.20
  154.5 2.9 %collective-permute-done.19.refs_3_ = bf16[256,384]{1,0:T(8,128)(2,1)S(1)} collective-permute-done((bf16[256,384]{1,0:T(8,128)(2,1)S(1)}, bf16[256,384]{1,0:T(8,128)(2,1)S(1)}, u32[]{:S(2)}, u32[]{:S(2)}) %collective-permute-start.19) | collective-permute-done | bytes 196640 | tf_op jit(solution)/shard_map/ppermute | solution.py:43
  157.3 4.5 %qkv_tile.1 = (bf16[256,384]{1,0:T(8,128)(2,1)S(1)}, bf16[256,128]{1,0:T(8,128)(2,1)S(1)}) custom-call(s32[16]{0:T(128)S(1)} %fusion.22.src_ref, bf16[512,384]{1,0:T(8,128)(2,1)S(1)} %pad_maximum_fusion.2.refs_0_, bf16[512,384]{1,0:T(8,128)(2,1)S(1)} %collective-permute-done.17.refs_1_, bf16[512,384]{1,0:T(8,128)(2,1)S(1)} %collective-permute-done.18.refs_2_, ...), custom_call_target="tpu_custom_call" | custom-call | flops 1610612736 | bytes 12582912 | tf_op jit(solution)/shard_map/qkv_tile/pallas_call | solution.py:295
  162.3 3.0 %collective-permute-done.29.pi = bf16[256,128]{1,0:T(8,128)(2,1)S(1)} collective-permute-done((bf16[256,128]{1,0:T(8,128)(2,1)S(1)}, bf16[256,128]{1,0:T(8,128)(2,1)S(1)}, u32[]{:S(2)}, u32[]{:S(2)}) %collective-permute-start.29) | collective-permute-done | bytes 65568 | tf_op jit(solution)/shard_map/ppermute | solution.py:531
  165.3 6.6 %attend.1 = bf16[640,384]{1,0:T(8,128)(2,1)} custom-call(s32[1]{0:T(128)} %bitcast.7.low_ref, bf16[384,384]{1,0:T(8,128)(2,1)S(1)} %copy-done.6, bf16[256,384]{1,0:T(8,128)(2,1)S(1)} %get-tuple-element.23.qi, bf16[384,128]{1,0:T(8,128)(2,1)S(1)} %copy-done.8, bf16[384,128]{1,0:T(8,128)(2,1)S(1)} %collective-permute-done.28.pt, ...), custom_call_target="tpu_custom_call" | custom-call | flops 1073741824 | bytes 2097152 | tf_op jit(solution)/shard_map/attend/pallas_call | solution.py:357
  172.8 3.4 %convolution_add_fusion = f32[2,6144]{1,0:T(2,128)S(1)} fusion(bf16[384,6144]{1,0:T(8,128)(2,1)} %param.26, bf16[640,384]{1,0:T(8,128)(2,1)} %attend.1, f32[2,6144]{1,0:T(2,128)S(1)} %bitcast.35, pred[6144]{0:T(1024)(128)(4,1)S(1)} %broadcast_in_dim.119, s32[2]{0:T(128)S(1)} %fusion.15), kind=kOutput, calls=%fused_computation.1 | convolution fusion | flops 10446848 | bytes 5314568 | tf_op jit(solution)/shard_map/dot_general | solution.py:543
  176.8 2.2 collective-permute-start.32
  181.0 1.7 collective-permute-start.33
  182.7 1.8 collective-permute-start.34
  186.8 1.8 collective-permute-done.35
  188.7 20.3 %all-gather.1 = bf16[8,2,6144]{2,1,0:T(2,128)(2,1)S(1)} all-gather(bf16[1,2,6144]{2,1,0:T(2,128)(2,1)S(1)} %fusion.12), channel_id=1, replica_groups=mesh['req'=8,'hid'=16] {'req'}, dimensions={0}, use_global_device_ids=true | all-gather | bytes 221184 | tf_op jit(solution)/shard_map/all_gather | solution.py:551
  209.8 3.8 %convolution_reduce_fusion = f32[16]{0:T(128)S(1)} fusion(bf16[384,6144]{1,0:T(8,128)(2,1)} %param.28, f32[16,6144]{1,0:T(8,128)S(1)} %reshape.317, f32[6144]{0:T(1024)S(1)} %convert_element_type.50, f32[16]{0:T(128)S(1)} %get-tuple-element.37), kind=kOutput, calls=%fused_computation.6 | convolution fusion | flops 75798512 | bytes 5136512 | tf_op jit(solution)/shard_map/dot_general | solution.py:558
  214.1 2.6 %collective-permute-start.37 = (f32[16]{0:T(128)S(1)}, f32[16]{0:T(128)S(1)}, u32[]{:S(2)}, u32[]{:S(2)}) collective-permute-start(f32[16]{0:T(128)S(1)} %convolution_reduce_fusion), channel_id=1, source_target_pairs={{1,0},{2,1},{3,2},{0,3},{5,4},{6,5},{7,6},{4,7},{9,8},{10,9},{11,1... | collective-permute-start | bytes 200 | tf_op jit(solution)/shard_map/ppermute | solution.py:43
  218.0 2.7 %collective-permute-done.38 = f32[16]{0:T(128)S(1)} collective-permute-done((f32[16]{0:T(128)S(1)}, f32[16]{0:T(128)S(1)}, u32[]{:S(2)}, u32[]{:S(2)}) %collective-permute-start.38) | collective-permute-done | bytes 96 | tf_op jit(solution)/shard_map/ppermute | solution.py:43
  220.7 2.7 %collective-permute-start.40 = (f32[16]{0:T(128)S(1)}, f32[16]{0:T(128)S(1)}, u32[]{:S(2)}, u32[]{:S(2)}) collective-permute-start(f32[16]{0:T(128)S(1)} %maximum_maximum_fusion.1), channel_id=1, source_target_pairs={{4,0},{5,1},{6,2},{7,3},{8,4},{9,5},{10,6},{11,7},{12,8},{13,9},{1... | collective-permute-start | bytes 200 | tf_op jit(solution)/shard_map/ppermute | solution.py:43
  224.7 2.6 %collective-permute-done.41 = f32[16]{0:T(128)S(1)} collective-permute-done((f32[16]{0:T(128)S(1)}, f32[16]{0:T(128)S(1)}, u32[]{:S(2)}, u32[]{:S(2)}) %collective-permute-start.41) | collective-permute-done | bytes 96 | tf_op jit(solution)/shard_map/ppermute | solution.py:43
  227.4 15.8 %pmax.7 = f32[16]{0:T(128)} all-reduce(f32[16]{0:T(128)S(1)} %maximum_maximum_fusion), channel_id=1, replica_groups=mesh['req'=8,'hid'=16] {'req'}, use_global_device_ids=true, to_apply=%region_6.7 | all-reduce | flops 16 | bytes 128 | tf_op jit(solution)/shard_map/pmax | solution.py:565
  243.4 10.7 %finish.1 = bf16[2,480,384]{2,1,0:T(8,128)(2,1)} custom-call(bf16[2,480,384]{2,1,0:T(8,128)(2,1)S(1)} %copy-done.2, bf16[256,384]{1,0:T(8,128)(2,1)S(1)} %bitcast.28, bf16[10240,384]{1,0:T(8,128)(2,1)} %all-gather.8.cloned.1.call-done.a_hbm, bf16[8,16,48,384]{3,2,1,0:T(8,128)(2,1)} %bitcast.32, s32[2,480,1]{2,1,0:T(8,128)S(1)} %fusion.4.slot_ref), custom_call_target="tpu_custom_call" | custom-call | flops 3019898880 | bytes 14680064 | tf_op jit(solution)/shard_map/finish/pallas_call | solution.py:416
  (160 shorter events, 47.0 us)
Async XLA Ops:
  7.2 96.7 %all-gather.6.cloned.1.call-start = ((), (), s32[]{:S(2)}) async-start(), calls=%async_computation.2 | async-start | bytes 7798784 | tf_op jit(solution)/shard_map/all_gather | solution.py:493
  16.4 20.0 %collective-permute-start = (bf16[192,384]{1,0:T(8,128)(2,1)S(1)}, bf16[192,384]{1,0:T(8,128)(2,1)}, u32[]{:S(2)}, u32[]{:S(2)}) collective-permute-start(bf16[192,384]{1,0:T(8,128)(2,1)S(1)} %get-tuple-element.31), channel_id=1, source_target_pairs={{3,0},{0,1},{1,2},{2,3},{7,4},{4,5},{5,6},{6,7},{11,8},{8,9},{9,10... | collective-permute-start | bytes 442376 | tf_op jit(solution)/shard_map/ppermute | solution.py:43
  18.9 20.9 %collective-permute-start.1 = (bf16[192,384]{1,0:T(8,128)(2,1)S(1)}, bf16[192,384]{1,0:T(8,128)(2,1)}, u32[]{:S(2)}, u32[]{:S(2)}) collective-permute-start(bf16[192,384]{1,0:T(8,128)(2,1)S(1)} %get-tuple-element.31), channel_id=1, source_target_pairs={{1,0},{2,1},{3,2},{0,3},{5,4},{6,5},{7,6},{4,7},{9,8},{10,9},{11,1... | collective-permute-start | bytes 442376 | tf_op jit(solution)/shard_map/ppermute | solution.py:43
  21.1 18.7 %collective-permute-start.2 = (bf16[192,384]{1,0:T(8,128)(2,1)S(1)}, bf16[192,384]{1,0:T(8,128)(2,1)}, u32[]{:S(2)}, u32[]{:S(2)}) collective-permute-start(bf16[192,384]{1,0:T(8,128)(2,1)S(1)} %get-tuple-element.31), channel_id=1, source_target_pairs={{2,0},{3,1},{0,2},{1,3},{6,4},{7,5},{4,6},{5,7},{10,8},{11,9},{8,1... | collective-permute-start | bytes 442376 | tf_op jit(solution)/shard_map/ppermute | solution.py:43
  22.3 21.3 %collective-permute-start.7 = (bf16[192,384]{1,0:T(8,128)(2,1)S(1)}, bf16[192,384]{1,0:T(8,128)(2,1)}, u32[]{:S(2)}, u32[]{:S(2)}) collective-permute-start(bf16[192,384]{1,0:T(8,128)(2,1)S(1)} %get-tuple-element.30), channel_id=1, source_target_pairs={{12,0},{13,1},{14,2},{15,3},{0,4},{1,5},{2,6},{3,7},{4,8},{5,9},{6... | collective-permute-start | bytes 442376 | tf_op jit(solution)/shard_map/ppermute | solution.py:43
  23.5 20.1 %collective-permute-start.8 = (bf16[192,384]{1,0:T(8,128)(2,1)S(1)}, bf16[192,384]{1,0:T(8,128)(2,1)}, u32[]{:S(2)}, u32[]{:S(2)}) collective-permute-start(bf16[192,384]{1,0:T(8,128)(2,1)S(1)} %get-tuple-element.30), channel_id=1, source_target_pairs={{4,0},{5,1},{6,2},{7,3},{8,4},{9,5},{10,6},{11,7},{12,8},{13,9},{1... | collective-permute-start | bytes 442376 | tf_op jit(solution)/shard_map/ppermute | solution.py:43
  36.3 7.3 %collective-permute-start.9 = (bf16[192,384]{1,0:T(8,128)(2,1)S(1)}, bf16[192,384]{1,0:T(8,128)(2,1)S(1)}, u32[]{:S(2)}, u32[]{:S(2)}) collective-permute-start(bf16[192,384]{1,0:T(8,128)(2,1)S(1)} %get-tuple-element.30), channel_id=1, source_target_pairs={{8,0},{9,1},{10,2},{11,3},{12,4},{13,5},{14,6},{15,7},{0,8},{1,9},... | collective-permute-start | bytes 442376 | tf_op jit(solution)/shard_map/ppermute | solution.py:43
  40.9 16.4 %collective-permute-start.3 = (bf16[768,384]{1,0:T(8,128)(2,1)S(1)}, bf16[768,384]{1,0:T(8,128)(2,1)S(1)}, u32[]{:S(2)}, u32[]{:S(2)}) collective-permute-start(bf16[768,384]{1,0:T(8,128)(2,1)S(1)} %pad_maximum_fusion.refs_0_), channel_id=1, source_target_pairs={{12,0},{13,1},{14,2},{15,3},{0,4},{1,5},{2,6},{3,7},{4,8},{5,9},{6... | collective-permute-start | bytes 1769480 | tf_op jit(solution)/shard_map/ppermute | solution.py:43
  41.3 18.7 %collective-permute-start.5 = (bf16[768,384]{1,0:T(8,128)(2,1)S(1)}, bf16[768,384]{1,0:T(8,128)(2,1)S(1)}, u32[]{:S(2)}, u32[]{:S(2)}) collective-permute-start(bf16[768,384]{1,0:T(8,128)(2,1)S(1)} %pad_maximum_fusion.refs_0_), channel_id=1, source_target_pairs={{4,0},{5,1},{6,2},{7,3},{8,4},{9,5},{10,6},{11,7},{12,8},{13,9},{1... | collective-permute-start | bytes 1769480 | tf_op jit(solution)/shard_map/ppermute | solution.py:43
  44.7 20.0 %collective-permute-start.10 = (bf16[768,384]{1,0:T(8,128)(2,1)S(1)}, bf16[768,384]{1,0:T(8,128)(2,1)S(1)}, u32[]{:S(2)}, u32[]{:S(2)}) collective-permute-start(bf16[768,384]{1,0:T(8,128)(2,1)S(1)} %pad_maximum_fusion.1.refs_5_), channel_id=1, source_target_pairs={{3,0},{0,1},{1,2},{2,3},{7,4},{4,5},{5,6},{6,7},{11,8},{8,9},{9,10... | collective-permute-start | bytes 1769480 | tf_op jit(solution)/shard_map/ppermute | solution.py:43
  45.5 24.2 %collective-permute-start.11 = (bf16[768,384]{1,0:T(8,128)(2,1)S(1)}, bf16[768,384]{1,0:T(8,128)(2,1)S(1)}, u32[]{:S(2)}, u32[]{:S(2)}) collective-permute-start(bf16[768,384]{1,0:T(8,128)(2,1)S(1)} %pad_maximum_fusion.1.refs_5_), channel_id=1, source_target_pairs={{1,0},{2,1},{3,2},{0,3},{5,4},{6,5},{7,6},{4,7},{9,8},{10,9},{11,1... | collective-permute-start | bytes 1769480 | tf_op jit(solution)/shard_map/ppermute | solution.py:43
  58.0 19.6 %collective-permute-start.4 = (bf16[384,384]{1,0:T(8,128)(2,1)}, bf16[384,384]{1,0:T(8,128)(2,1)}, u32[]{:S(2)}, u32[]{:S(2)}) collective-permute-start(bf16[384,384]{1,0:T(8,128)(2,1)} %slice.89), channel_id=1, source_target_pairs={{12,0},{13,1},{14,2},{15,3},{0,4},{1,5},{2,6},{3,7},{4,8},{5,9},{6... | collective-permute-start | bytes 884744 | tf_op jit(solution)/shard_map/ppermute | solution.py:43
  60.8 16.9 %collective-permute-start.6 = (bf16[384,384]{1,0:T(8,128)(2,1)}, bf16[384,384]{1,0:T(8,128)(2,1)}, u32[]{:S(2)}, u32[]{:S(2)}) collective-permute-start(bf16[384,384]{1,0:T(8,128)(2,1)} %slice.90), channel_id=1, source_target_pairs={{4,0},{5,1},{6,2},{7,3},{8,4},{9,5},{10,6},{11,7},{12,8},{13,9},{1... | collective-permute-start | bytes 884744 | tf_op jit(solution)/shard_map/ppermute | solution.py:43
  65.4 18.8 %collective-permute-start.12 = (bf16[384,384]{1,0:T(8,128)(2,1)}, bf16[384,384]{1,0:T(8,128)(2,1)}, u32[]{:S(2)}, u32[]{:S(2)}) collective-permute-start(bf16[384,384]{1,0:T(8,128)(2,1)} %slice.92), channel_id=1, source_target_pairs={{3,0},{0,1},{1,2},{2,3},{7,4},{4,5},{5,6},{6,7},{11,8},{8,9},{9,10... | collective-permute-start | bytes 884744 | tf_op jit(solution)/shard_map/ppermute | solution.py:43
  70.5 14.7 %collective-permute-start.13 = (bf16[384,384]{1,0:T(8,128)(2,1)}, bf16[384,384]{1,0:T(8,128)(2,1)}, u32[]{:S(2)}, u32[]{:S(2)}) collective-permute-start(bf16[384,384]{1,0:T(8,128)(2,1)} %slice.93), channel_id=1, source_target_pairs={{1,0},{2,1},{3,2},{0,3},{5,4},{6,5},{7,6},{4,7},{9,8},{10,9},{11,1... | collective-permute-start | bytes 884744 | tf_op jit(solution)/shard_map/ppermute | solution.py:43
  79.7 36.7 %all-to-all-start = ((bf16[16,48,384]{2,1,0:T(8,128)(2,1)}), bf16[16,48,384]{2,1,0:T(8,128)(2,1)}, u32[]{:S(2)}, u32[]{:S(2)}) async-start(bf16[16,48,384]{2,1,0:T(8,128)(2,1)} %copy.57), calls=%async_computation | async-start | bytes 1179648 | tf_op jit(solution)/shard_map/all_to_all | solution.py:509
  83.9 159.3 %all-gather.10.cloned.1.call-start = ((), (), s32[]{:S(2)}) async-start(), calls=%async_computation.4 | async-start | bytes 5308416 | tf_op jit(solution)/shard_map/all_gather | solution.py:527
  104.8 38.0 %copy-start.10 = (f32[640,64]{1,0:T(8,128)S(1)}, f32[640,64]{1,0:T(8,128)}, u32[]{:S(2)}) copy-start(f32[640,64]{1,0:T(8,128)} %get-tuple-element.34) | copy-start | bytes 491524
  127.2 116.1 %all-gather.8.cloned.1.call-start = ((), (), s32[]{:S(2)}) async-start(), calls=%async_computation.3 | async-start | bytes 8355840 | tf_op jit(solution)/shard_map/all_gather | solution.py:537
  127.3 6.9 %collective-permute-start.21 = (bf16[128,384]{1,0:T(8,128)(2,1)S(1)}, bf16[128,384]{1,0:T(8,128)(2,1)S(1)}, u32[]{:S(2)}, u32[]{:S(2)}) collective-permute-start(bf16[128,384]{1,0:T(8,128)(2,1)S(1)} %get-tuple-element.32), channel_id=1, source_target_pairs={{12,0},{13,1},{14,2},{15,3},{0,4},{1,5},{2,6},{3,7},{4,8},{5,9},{6... | collective-permute-start | bytes 294920 | tf_op jit(solution)/shard_map/ppermute | solution.py:43
  127.4 8.0 %collective-permute-start.22 = (bf16[128,384]{1,0:T(8,128)(2,1)S(1)}, bf16[128,384]{1,0:T(8,128)(2,1)S(1)}, u32[]{:S(2)}, u32[]{:S(2)}) collective-permute-start(bf16[128,384]{1,0:T(8,128)(2,1)S(1)} %get-tuple-element.32), channel_id=1, source_target_pairs={{4,0},{5,1},{6,2},{7,3},{8,4},{9,5},{10,6},{11,7},{12,8},{13,9},{1... | collective-permute-start | bytes 294920 | tf_op jit(solution)/shard_map/ppermute | solution.py:43
  130.1 5.3 %collective-permute-start.23 = (bf16[128,384]{1,0:T(8,128)(2,1)S(1)}, bf16[128,384]{1,0:T(8,128)(2,1)S(1)}, u32[]{:S(2)}, u32[]{:S(2)}) collective-permute-start(bf16[128,384]{1,0:T(8,128)(2,1)S(1)} %get-tuple-element.32), channel_id=1, source_target_pairs={{8,0},{9,1},{10,2},{11,3},{12,4},{13,5},{14,6},{15,7},{0,8},{1,9},... | collective-permute-start | bytes 294920 | tf_op jit(solution)/shard_map/ppermute | solution.py:43
  130.1 9.3 %collective-permute-start.14 = (bf16[128,384]{1,0:T(8,128)(2,1)S(1)}, bf16[128,384]{1,0:T(8,128)(2,1)S(1)}, u32[]{:S(2)}, u32[]{:S(2)}) collective-permute-start(bf16[128,384]{1,0:T(8,128)(2,1)S(1)} %get-tuple-element.33), channel_id=1, source_target_pairs={{3,0},{0,1},{1,2},{2,3},{7,4},{4,5},{5,6},{6,7},{11,8},{8,9},{9,10... | collective-permute-start | bytes 294920 | tf_op jit(solution)/shard_map/ppermute | solution.py:43
  130.5 8.9 %collective-permute-start.15 = (bf16[128,384]{1,0:T(8,128)(2,1)S(1)}, bf16[128,384]{1,0:T(8,128)(2,1)S(1)}, u32[]{:S(2)}, u32[]{:S(2)}) collective-permute-start(bf16[128,384]{1,0:T(8,128)(2,1)S(1)} %get-tuple-element.33), channel_id=1, source_target_pairs={{1,0},{2,1},{3,2},{0,3},{5,4},{6,5},{7,6},{4,7},{9,8},{10,9},{11,1... | collective-permute-start | bytes 294920 | tf_op jit(solution)/shard_map/ppermute | solution.py:43
  134.2 5.8 %collective-permute-start.16 = (bf16[128,384]{1,0:T(8,128)(2,1)S(1)}, bf16[128,384]{1,0:T(8,128)(2,1)S(1)}, u32[]{:S(2)}, u32[]{:S(2)}) collective-permute-start(bf16[128,384]{1,0:T(8,128)(2,1)S(1)} %get-tuple-element.33), channel_id=1, source_target_pairs={{2,0},{3,1},{0,2},{1,3},{6,4},{7,5},{4,6},{5,7},{10,8},{11,9},{8,1... | collective-permute-start | bytes 294920 | tf_op jit(solution)/shard_map/ppermute | solution.py:43
  135.4 12.8 %collective-permute-start.24 = (bf16[512,384]{1,0:T(8,128)(2,1)S(1)}, bf16[512,384]{1,0:T(8,128)(2,1)S(1)}, u32[]{:S(2)}, u32[]{:S(2)}) collective-permute-start(bf16[512,384]{1,0:T(8,128)(2,1)S(1)} %pad_maximum_fusion.3.refs_5_), channel_id=1, source_target_pairs={{3,0},{0,1},{1,2},{2,3},{7,4},{4,5},{5,6},{6,7},{11,8},{8,9},{9,10... | collective-permute-start | bytes 1179656 | tf_op jit(solution)/shard_map/ppermute | solution.py:43
  136.9 11.5 %collective-permute-start.25 = (bf16[512,384]{1,0:T(8,128)(2,1)S(1)}, bf16[512,384]{1,0:T(8,128)(2,1)S(1)}, u32[]{:S(2)}, u32[]{:S(2)}) collective-permute-start(bf16[512,384]{1,0:T(8,128)(2,1)S(1)} %pad_maximum_fusion.3.refs_5_), channel_id=1, source_target_pairs={{1,0},{2,1},{3,2},{0,3},{5,4},{6,5},{7,6},{4,7},{9,8},{10,9},{11,1... | collective-permute-start | bytes 1179656 | tf_op jit(solution)/shard_map/ppermute | solution.py:43
  140.1 11.0 %collective-permute-start.17 = (bf16[512,384]{1,0:T(8,128)(2,1)S(1)}, bf16[512,384]{1,0:T(8,128)(2,1)S(1)}, u32[]{:S(2)}, u32[]{:S(2)}) collective-permute-start(bf16[512,384]{1,0:T(8,128)(2,1)S(1)} %pad_maximum_fusion.2.refs_0_), channel_id=1, source_target_pairs={{12,0},{13,1},{14,2},{15,3},{0,4},{1,5},{2,6},{3,7},{4,8},{5,9},{6... | collective-permute-start | bytes 1179656 | tf_op jit(solution)/shard_map/ppermute | solution.py:43
  140.7 11.2 %collective-permute-start.18 = (bf16[512,384]{1,0:T(8,128)(2,1)S(1)}, bf16[512,384]{1,0:T(8,128)(2,1)S(1)}, u32[]{:S(2)}, u32[]{:S(2)}) collective-permute-start(bf16[512,384]{1,0:T(8,128)(2,1)S(1)} %pad_maximum_fusion.2.refs_0_), channel_id=1, source_target_pairs={{4,0},{5,1},{6,2},{7,3},{8,4},{9,5},{10,6},{11,7},{12,8},{13,9},{1... | collective-permute-start | bytes 1179656 | tf_op jit(solution)/shard_map/ppermute | solution.py:43
  148.3 6.2 %collective-permute-start.26 = (bf16[256,384]{1,0:T(8,128)(2,1)S(1)}, bf16[256,384]{1,0:T(8,128)(2,1)S(1)}, u32[]{:S(2)}, u32[]{:S(2)}) collective-permute-start(bf16[256,384]{1,0:T(8,128)(2,1)S(1)} %slice.101), channel_id=1, source_target_pairs={{3,0},{0,1},{1,2},{2,3},{7,4},{4,5},{5,6},{6,7},{11,8},{8,9},{9,10... | collective-permute-start | bytes 589832 | tf_op jit(solution)/shard_map/ppermute | solution.py:43
  148.4 6.1 %collective-permute-start.27 = (bf16[256,384]{1,0:T(8,128)(2,1)S(1)}, bf16[256,384]{1,0:T(8,128)(2,1)S(1)}, u32[]{:S(2)}, u32[]{:S(2)}) collective-permute-start(bf16[256,384]{1,0:T(8,128)(2,1)S(1)} %slice.102), channel_id=1, source_target_pairs={{1,0},{2,1},{3,2},{0,3},{5,4},{6,5},{7,6},{4,7},{9,8},{10,9},{11,1... | collective-permute-start | bytes 589832 | tf_op jit(solution)/shard_map/ppermute | solution.py:43
  151.1 6.2 %collective-permute-start.19 = (bf16[256,384]{1,0:T(8,128)(2,1)S(1)}, bf16[256,384]{1,0:T(8,128)(2,1)S(1)}, u32[]{:S(2)}, u32[]{:S(2)}) collective-permute-start(bf16[256,384]{1,0:T(8,128)(2,1)S(1)} %slice.99), channel_id=1, source_target_pairs={{12,0},{13,1},{14,2},{15,3},{0,4},{1,5},{2,6},{3,7},{4,8},{5,9},{6... | collective-permute-start | bytes 589832 | tf_op jit(solution)/shard_map/ppermute | solution.py:43
  151.9 5.4 %collective-permute-start.20 = (bf16[256,384]{1,0:T(8,128)(2,1)S(1)}, bf16[256,384]{1,0:T(8,128)(2,1)S(1)}, u32[]{:S(2)}, u32[]{:S(2)}) collective-permute-start(bf16[256,384]{1,0:T(8,128)(2,1)S(1)} %slice.100), channel_id=1, source_target_pairs={{4,0},{5,1},{6,2},{7,3},{8,4},{9,5},{10,6},{11,7},{12,8},{13,9},{1... | collective-permute-start | bytes 589832 | tf_op jit(solution)/shard_map/ppermute | solution.py:43
  154.2 8.0 %collective-permute-start.28 = (bf16[384,128]{1,0:T(8,128)(2,1)S(1)}, bf16[384,128]{1,0:T(8,128)(2,1)S(1)}, u32[]{:S(2)}, u32[]{:S(2)}) collective-permute-start(bf16[384,128]{1,0:T(8,128)(2,1)S(1)} %copy-done.8), channel_id=1, source_target_pairs={{0,1},{1,0},{2,3},{3,2},{4,5},{5,4},{6,7},{7,6},{8,9},{9,8},{10,11... | collective-permute-start | bytes 294920 | tf_op jit(solution)/shard_map/ppermute | solution.py:524
  161.9 3.4 %collective-permute-start.29 = (bf16[256,128]{1,0:T(8,128)(2,1)S(1)}, bf16[256,128]{1,0:T(8,128)(2,1)S(1)}, u32[]{:S(2)}, u32[]{:S(2)}) collective-permute-start(bf16[256,128]{1,0:T(8,128)(2,1)S(1)} %get-tuple-element.25.oi), channel_id=1, source_target_pairs={{0,1},{1,0},{2,3},{3,2},{4,5},{5,4},{6,7},{7,6},{8,9},{9,8},{10,11... | collective-permute-start | bytes 196616 | tf_op jit(solution)/shard_map/ppermute | solution.py:531
  176.2 67.2 %copy-start.2 = (bf16[2,480,384]{2,1,0:T(8,128)(2,1)S(1)}, bf16[2,480,384]{2,1,0:T(8,128)(2,1)}, u32[]{:S(2)}) copy-start(bf16[2,480,384]{2,1,0:T(8,128)(2,1)} %text_ref.1) | copy-start | bytes 2211844
  176.2 4.6 %collective-permute-start.30 = (f32[2,6144]{1,0:T(2,128)S(1)}, f32[2,6144]{1,0:T(2,128)S(1)}, u32[]{:S(2)}, u32[]{:S(2)}) collective-permute-start(f32[2,6144]{1,0:T(2,128)S(1)} %convolution_add_fusion), channel_id=1, source_target_pairs={{2,0},{3,1},{0,2},{1,3},{6,4},{7,5},{4,6},{5,7},{10,8},{11,9},{8,1... | collective-permute-start | bytes 147464 | tf_op jit(solution)/shard_map/ppermute | solution.py:43
  176.2 4.7 %collective-permute-start.31 = (f32[2,6144]{1,0:T(2,128)S(1)}, f32[2,6144]{1,0:T(2,128)S(1)}, u32[]{:S(2)}, u32[]{:S(2)}) collective-permute-start(f32[2,6144]{1,0:T(2,128)S(1)} %convolution_add_fusion), channel_id=1, source_target_pairs={{3,0},{0,1},{1,2},{2,3},{7,4},{4,5},{5,6},{6,7},{11,8},{8,9},{9,10... | collective-permute-start | bytes 147464 | tf_op jit(solution)/shard_map/ppermute | solution.py:43
  176.8 4.2 %collective-permute-start.32 = (f32[2,6144]{1,0:T(2,128)S(1)}, f32[2,6144]{1,0:T(2,128)S(1)}, u32[]{:S(2)}, u32[]{:S(2)}) collective-permute-start(f32[2,6144]{1,0:T(2,128)S(1)} %convolution_add_fusion), channel_id=1, source_target_pairs={{1,0},{2,1},{3,2},{0,3},{5,4},{6,5},{7,6},{4,7},{9,8},{10,9},{11,1... | collective-permute-start | bytes 147464 | tf_op jit(solution)/shard_map/ppermute | solution.py:43
  181.0 4.8 %collective-permute-start.33 = (f32[2,6144]{1,0:T(2,128)S(1)}, f32[2,6144]{1,0:T(2,128)S(1)}, u32[]{:S(2)}, u32[]{:S(2)}) collective-permute-start(f32[2,6144]{1,0:T(2,128)S(1)} %add_add_fusion), channel_id=1, source_target_pairs={{8,0},{9,1},{10,2},{11,3},{12,4},{13,5},{14,6},{15,7},{0,8},{1,9},... | collective-permute-start | bytes 147464 | tf_op jit(solution)/shard_map/ppermute | solution.py:43
  182.7 4.2 %collective-permute-start.34 = (f32[2,6144]{1,0:T(2,128)S(1)}, f32[2,6144]{1,0:T(2,128)S(1)}, u32[]{:S(2)}, u32[]{:S(2)}) collective-permute-start(f32[2,6144]{1,0:T(2,128)S(1)} %add_add_fusion), channel_id=1, source_target_pairs={{12,0},{13,1},{14,2},{15,3},{0,4},{1,5},{2,6},{3,7},{4,8},{5,9},{6... | collective-permute-start | bytes 147464 | tf_op jit(solution)/shard_map/ppermute | solution.py:43
  184.4 4.2 %collective-permute-start.35 = (f32[2,6144]{1,0:T(2,128)S(1)}, f32[2,6144]{1,0:T(2,128)S(1)}, u32[]{:S(2)}, u32[]{:S(2)}) collective-permute-start(f32[2,6144]{1,0:T(2,128)S(1)} %add_add_fusion), channel_id=1, source_target_pairs={{4,0},{5,1},{6,2},{7,3},{8,4},{9,5},{10,6},{11,7},{12,8},{13,9},{1... | collective-permute-start | bytes 147464 | tf_op jit(solution)/shard_map/ppermute | solution.py:43
  213.5 4.4 %collective-permute-start.36 = (f32[16]{0:T(128)S(1)}, f32[16]{0:T(128)S(1)}, u32[]{:S(2)}, u32[]{:S(2)}) collective-permute-start(f32[16]{0:T(128)S(1)} %convolution_reduce_fusion), channel_id=1, source_target_pairs={{3,0},{0,1},{1,2},{2,3},{7,4},{4,5},{5,6},{6,7},{11,8},{8,9},{9,10... | collective-permute-start | bytes 200 | tf_op jit(solution)/shard_map/ppermute | solution.py:43
  214.1 3.9 %collective-permute-start.37 = (f32[16]{0:T(128)S(1)}, f32[16]{0:T(128)S(1)}, u32[]{:S(2)}, u32[]{:S(2)}) collective-permute-start(f32[16]{0:T(128)S(1)} %convolution_reduce_fusion), channel_id=1, source_target_pairs={{1,0},{2,1},{3,2},{0,3},{5,4},{6,5},{7,6},{4,7},{9,8},{10,9},{11,1... | collective-permute-start | bytes 200 | tf_op jit(solution)/shard_map/ppermute | solution.py:43
  216.7 4.0 %collective-permute-start.38 = (f32[16]{0:T(128)S(1)}, f32[16]{0:T(128)S(1)}, u32[]{:S(2)}, u32[]{:S(2)}) collective-permute-start(f32[16]{0:T(128)S(1)} %convolution_reduce_fusion), channel_id=1, source_target_pairs={{2,0},{3,1},{0,2},{1,3},{6,4},{7,5},{4,6},{5,7},{10,8},{11,9},{8,1... | collective-permute-start | bytes 200 | tf_op jit(solution)/shard_map/ppermute | solution.py:43
  220.7 4.0 %collective-permute-start.39 = (f32[16]{0:T(128)S(1)}, f32[16]{0:T(128)S(1)}, u32[]{:S(2)}, u32[]{:S(2)}) collective-permute-start(f32[16]{0:T(128)S(1)} %maximum_maximum_fusion.1), channel_id=1, source_target_pairs={{12,0},{13,1},{14,2},{15,3},{0,4},{1,5},{2,6},{3,7},{4,8},{5,9},{6... | collective-permute-start | bytes 200 | tf_op jit(solution)/shard_map/ppermute | solution.py:43
  220.7 4.0 %collective-permute-start.40 = (f32[16]{0:T(128)S(1)}, f32[16]{0:T(128)S(1)}, u32[]{:S(2)}, u32[]{:S(2)}) collective-permute-start(f32[16]{0:T(128)S(1)} %maximum_maximum_fusion.1), channel_id=1, source_target_pairs={{4,0},{5,1},{6,2},{7,3},{8,4},{9,5},{10,6},{11,7},{12,8},{13,9},{1... | collective-permute-start | bytes 200 | tf_op jit(solution)/shard_map/ppermute | solution.py:43
  223.4 4.0 %collective-permute-start.41 = (f32[16]{0:T(128)S(1)}, f32[16]{0:T(128)S(1)}, u32[]{:S(2)}, u32[]{:S(2)}) collective-permute-start(f32[16]{0:T(128)S(1)} %maximum_maximum_fusion.1), channel_id=1, source_target_pairs={{8,0},{9,1},{10,2},{11,3},{12,4},{13,5},{14,6},{15,7},{0,8},{1,9},... | collective-permute-start | bytes 200 | tf_op jit(solution)/shard_map/ppermute | solution.py:43
  (15 other events, 209.2 us)
Sparse Core Ops, SparseCore 0:
  12.1 91.7 all-gather.5
  127.3 33.2 all-gather.9
  172.1 71.2 all-gather.7

commit v3 on v2

--- a/solution.py
+++ b/solution.py
@@ -131,7 +131,7 @@
         tail[here, 0:32] = v[:, MAIN:MFEAT]
         return carry
 
-    lax.fori_loop(0, N_REQ, step, 0)
+    lax.fori_loop(0, N_REQ, step, 0, unroll=True)
     o_ref[:, MAIN:MPAD] = pltpu.roll(tail[...], place_ref[0] * 32, 1).astype(BF)
 
 
@@ -505,12 +505,11 @@
     strip = FEAT // N_REQ
     piece = lax.dynamic_slice_in_dim(out_weight, me * strip, strip, axis=0)
     piece = piece.reshape(strip, N_HID, FEAT).transpose(1, 0, 2)
-    piece, *text_blocks[3:5] = lax.optimization_barrier((piece, *text_blocks[3:5]))
-    piece = lax.all_to_all(piece, "hid", split_axis=0, concat_axis=0, tiled=True)
     q_text, kv_text = qkv(
         text_blocks, text_where, weight, cos[:TEXT], sin[:TEXT], sources, "qkv_text"
     )
-    gathered, q_text, kv_text = lax.optimization_barrier((gathered, q_text, kv_text))
+    gathered, piece, q_text, kv_text = lax.optimization_barrier((gathered, piece, q_text, kv_text))
+    piece = lax.all_to_all(piece, "hid", split_axis=0, concat_axis=0, tiled=True)
     projected = project(
         gathered,
         proj_weight,
@@ -518,6 +517,7 @@
         ln_bias,
         proj_bias[None, :],
     )
+    projected, piece = lax.optimization_barrier((projected, piece))
     tile = lax.all_to_all(
         projected.reshape(N_REQ, TILE // N_REQ, FEAT), "req", split_axis=0, concat_axis=0, tiled=True
     ).reshape(TILE, FEAT)

time: 262 us -> 261 us (level)
  waiting for transfers between devices: 37.5 us -> 51.4 us
  local copies, waits for them, and re-layouts: 22.5 us -> 14.3 us
  other arithmetic: 23.8 us -> 17.5 us
    ppermute x40, waiting for transfers between devices: 24.9 us -> 35.2 us  [shift(): return lax.ppermute(block, 'hid', route)]
    all_gather x1, waiting for transfers between devices: 9.32 us -> 13.1 us  [shards(): lax.all_gather(pack(merged, tile_order, (hid % RING)[None]), 'hid', axis=...]
    unnamed x39 -> x41, local copies, waits for them, and re-layouts: 10.7 us -> 7.99 us
  transfers between devices with their start and end apart: 46 -> 46, of which waited for: 19 -> 20; matrix products, arithmetic and copies ran while one was open for 19% -> 14% of each run, Pallas kernels for 11% -> 11%
where the time goes in v3:
time: 261 us; the launch traced here: 260 us
  starting transfers between devices  62.6 us (24%)
  waiting for transfers between devices  51.4 us (20%)
  blocking collectives  47.9 us (18%)
  Pallas kernels  40.6 us (16%)
  other arithmetic  17.5 us (7%)
  between operations  16.3 us (6%)
  local copies, waits for them, and re-layouts  14.3 us (5%)
  matrix products  9.21 us (4%)
    ppermute x40, starting transfers between devices, shift(): return lax.ppermute(block, 'hid', route)  57.9 us
    ppermute x40, waiting for transfers between devices, shift(): return lax.ppermute(block, 'hid', route)  35.2 us
    all_gather x1, blocking collectives, shards(): all_last = lax.all_gather(full_width, 'req', axis=0, tiled=True)  21.1 us
    pmax x1, blocking collectives, shards(): logit_max = lax.pmax(top, 'req')  15.8 us
    all_gather x1, waiting for transfers between devices, shards(): lax.all_gather(pack(merged, tile_order, (hid % RING)[None]), 'hid', axis=...  13.1 us
    pallas_call x1, Pallas kernels, project(): pl.pallas_call(project_kernel, out_shape=jax.ShapeDtypeStruct((TILE, FEAT...  11.6 us
    all_to_all x1, blocking collectives, shards(): lax.all_to_all(projected.reshape(N_REQ, TILE // N_REQ, FEAT), 'req', spli...  11 us
    pallas_call x1, Pallas kernels, finish(): pl.pallas_call(finish_kernel, out_shape=jax.ShapeDtypeStruct((REQ_GRP, LE...  10.7 us
  transfers between devices with their start and end apart: 46, of which 20 were waited for; matrix products, arithmetic and copies ran while one was open for 14% of the time, Pallas kernels for 11%

profile of v3, /device:TPU:1, one launch (start us, length us, event | category | flops | bytes accessed | tf_op | source)
XLA Modules:
  0.0 260.0 jit_solution(15141519039584143076)
XLA Ops:
  9.7 1.6 pack.1
  14.0 1.7 fusion.1
  15.8 2.1 collective-permute-start.7
  19.2 1.6 collective-permute-start.9
  20.9 1.6 collective-permute-start
  22.5 2.1 collective-permute-start.1
  24.6 1.8 copy.57
  26.5 1.8 copy.58
  29.7 7.7 %multiply_convert_fusion.refs_10_ = bf16[6144,512]{1,0:T(8,128)(2,1)} fusion(bf16[6144,64]{1,0:T(8,128)(2,1)S(1)} %copy.58, bf16[6144,64]{1,0:T(8,128)(2,1)S(1)} %copy.57, bf16[6144,384]{1,0:T(8,128)(2,1)} %param.23, f32[6144]{0:T(1024)S(1)} %convert_element_type.43), kind=kLoop, calls=%fused_computation | loop fusion | flops 25165824 | bytes 12607488 | tf_op jit(solution)/shard_map/convert_element_type | solution.py:502
  39.3 1.9 collective-permute-start.11
  42.7 2.4 collective-permute-start.4
  45.1 1.9 constant_dynamic-slice_fusion
  47.0 2.0 copy.61
  50.3 2.0 collective-permute-done.10.refs_6_
  53.0 3.1 %collective-permute-start.13 = (bf16[384,384]{1,0:T(8,128)(2,1)S(1)}, bf16[384,384]{1,0:T(8,128)(2,1)S(1)}, u32[]{:S(2)}, u32[]{:S(2)}) collective-permute-start(bf16[384,384]{1,0:T(8,128)(2,1)S(1)} %slice.93), channel_id=1, source_target_pairs={{1,0},{2,1},{3,2},{0,3},{5,4},{6,5},{7,6},{4,7},{9,8},{10,9},{11,1... | collective-permute-start | bytes 884744 | tf_op jit(solution)/shard_map/ppermute | solution.py:43
  56.2 1.8 collective-permute-done.3.refs_1_
  59.3 3.8 %collective-permute-start.6 = (bf16[384,384]{1,0:T(8,128)(2,1)S(1)}, bf16[384,384]{1,0:T(8,128)(2,1)S(1)}, u32[]{:S(2)}, u32[]{:S(2)}) collective-permute-start(bf16[384,384]{1,0:T(8,128)(2,1)S(1)} %slice.90), channel_id=1, source_target_pairs={{4,0},{5,1},{6,2},{7,3},{8,4},{9,5},{10,6},{11,7},{12,8},{13,9},{1... | collective-permute-start | bytes 884744 | tf_op jit(solution)/shard_map/ppermute | solution.py:43
  63.4 3.8 %collective-permute-done.12.refs_8_ = bf16[384,384]{1,0:T(8,128)(2,1)S(1)} collective-permute-done((bf16[384,384]{1,0:T(8,128)(2,1)S(1)}, bf16[384,384]{1,0:T(8,128)(2,1)S(1)}, u32[]{:S(2)}, u32[]{:S(2)}) %collective-permute-start.12) | collective-permute-done | bytes 294944 | tf_op jit(solution)/shard_map/ppermute | solution.py:43
  67.9 5.7 %collective-permute-done.5.refs_3_ = bf16[384,384]{1,0:T(8,128)(2,1)S(1)} collective-permute-done((bf16[384,384]{1,0:T(8,128)(2,1)S(1)}, bf16[384,384]{1,0:T(8,128)(2,1)S(1)}, u32[]{:S(2)}, u32[]{:S(2)}) %collective-permute-start.5) | collective-permute-done | bytes 294944 | tf_op jit(solution)/shard_map/ppermute | solution.py:43
  73.6 1.8 collective-permute-done.6.refs_4_
  75.4 5.5 %qkv_text.1 = (bf16[384,384]{1,0:T(8,128)(2,1)S(1)}, bf16[384,128]{1,0:T(8,128)(2,1)S(1)}) custom-call(s32[16]{0:T(128)S(1)} %fusion.22.src_ref, bf16[768,384]{1,0:T(8,128)(2,1)S(1)} %pad_maximum_fusion.refs_0_, bf16[768,384]{1,0:T(8,128)(2,1)S(1)} %collective-permute-done.3.refs_1_, bf16[768,384]{1,0:T(8,128)(2,1)S(1)} %collective-permute-done.4.refs_2_, ...), custom_call_target="tpu_custom_call" | custom-call | flops 2415919104 | bytes 12582912 | tf_op jit(solution)/shard_map/qkv_text/pallas_call | solution.py:295
  82.2 13.1 %all-gather.6.cloned.1.call-done.x_hbm = bf16[4096,896]{1,0:T(8,128)(2,1)} async-done(((bf16[256,896]{1,0:T(8,128)(2,1)}), bf16[4096,896]{1,0:T(8,128)(2,1)}) %all-gather.6.cloned.1.call-update) | async-done | bytes 7340048 | tf_op jit(solution)/shard_map/all_gather | solution.py:493
  95.3 2.0 copy.59
  97.3 4.2 %all-to-all-start = ((bf16[16,48,384]{2,1,0:T(8,128)(2,1)}), bf16[16,48,384]{2,1,0:T(8,128)(2,1)S(1)}, u32[]{:S(2)}, u32[]{:S(2)}) async-start(bf16[16,48,384]{2,1,0:T(8,128)(2,1)} %copy.59), calls=%async_computation | async-start | bytes 1179648 | tf_op jit(solution)/shard_map/all_to_all | solution.py:512
  103.4 11.6 %project.1 = bf16[256,384]{1,0:T(8,128)(2,1)S(1)} custom-call(bf16[4096,896]{1,0:T(8,128)(2,1)} %all-gather.6.cloned.1.call-done.x_hbm, bf16[16,800,384]{2,1,0:T(8,128)(2,1)} %bitcast.31, f32[2,16,768]{2,1,0:T(8,128)S(1)} %slice.98.gb_ref, f32[2,4,1,128]{3,2,1,0:T(1,128)S(1)} %reshape.310.left_ref, f32[1,384]{1,0:T(1,128)S(1)} %broadcast_in_dim.108.pb_ref), custom_call_target="tpu_custom_call" | custom-call | flops 2516582400 | bytes 17825792 | tf_op jit(solution)/shard_map/project/pallas_call | solution.py:219
  115.0 11.0 %all_to_all.10 = bf16[8,32,384]{2,1,0:T(8,128)(2,1)S(1)} all-to-all(bf16[8,32,384]{2,1,0:T(8,128)(2,1)S(1)} %bitcast.29), channel_id=1, replica_groups=mesh['req'=8,'hid'=16] {'req'}, dimensions={0} | all-to-all | bytes 393216 | tf_op jit(solution)/shard_map/all_to_all | solution.py:521
  126.1 1.7 collective-permute-start.21
  129.1 1.7 collective-permute-start.23
  136.0 1.8 collective-permute-start.25
  139.7 2.4 collective-permute-start.18
  144.4 2.4 collective-permute-done.24.refs_6_
  147.0 2.7 %collective-permute-start.27 = (bf16[256,384]{1,0:T(8,128)(2,1)S(1)}, bf16[256,384]{1,0:T(8,128)(2,1)S(1)}, u32[]{:S(2)}, u32[]{:S(2)}) collective-permute-start(bf16[256,384]{1,0:T(8,128)(2,1)S(1)} %slice.102), channel_id=1, source_target_pairs={{1,0},{2,1},{3,2},{0,3},{5,4},{6,5},{7,6},{4,7},{9,8},{10,9},{11,1... | collective-permute-start | bytes 589832 | tf_op jit(solution)/shard_map/ppermute | solution.py:43
  150.1 2.5 collective-permute-start.20
  153.2 2.7 %collective-permute-done.19.refs_3_ = bf16[256,384]{1,0:T(8,128)(2,1)S(1)} collective-permute-done((bf16[256,384]{1,0:T(8,128)(2,1)S(1)}, bf16[256,384]{1,0:T(8,128)(2,1)S(1)}, u32[]{:S(2)}, u32[]{:S(2)}) %collective-permute-start.19) | collective-permute-done | bytes 196640 | tf_op jit(solution)/shard_map/ppermute | solution.py:43
  155.9 4.5 %qkv_tile.1 = (bf16[256,384]{1,0:T(8,128)(2,1)S(1)}, bf16[256,128]{1,0:T(8,128)(2,1)S(1)}) custom-call(s32[16]{0:T(128)S(1)} %fusion.22.src_ref, bf16[512,384]{1,0:T(8,128)(2,1)S(1)} %pad_maximum_fusion.2.refs_0_, bf16[512,384]{1,0:T(8,128)(2,1)S(1)} %collective-permute-done.17.refs_1_, bf16[512,384]{1,0:T(8,128)(2,1)S(1)} %collective-permute-done.18.refs_2_, ...), custom_call_target="tpu_custom_call" | custom-call | flops 1610612736 | bytes 12582912 | tf_op jit(solution)/shard_map/qkv_tile/pallas_call | solution.py:295
  160.6 3.0 %collective-permute-done.29.pi = bf16[256,128]{1,0:T(8,128)(2,1)S(1)} collective-permute-done((bf16[256,128]{1,0:T(8,128)(2,1)S(1)}, bf16[256,128]{1,0:T(8,128)(2,1)S(1)}, u32[]{:S(2)}, u32[]{:S(2)}) %collective-permute-start.29) | collective-permute-done | bytes 65568 | tf_op jit(solution)/shard_map/ppermute | solution.py:531
  163.7 6.6 %attend.1 = bf16[640,384]{1,0:T(8,128)(2,1)} custom-call(s32[1]{0:T(128)} %bitcast.7.low_ref, bf16[384,384]{1,0:T(8,128)(2,1)S(1)} %copy-done.3, bf16[256,384]{1,0:T(8,128)(2,1)S(1)} %get-tuple-element.23.qi, bf16[384,128]{1,0:T(8,128)(2,1)S(1)} %copy-done.5, bf16[384,128]{1,0:T(8,128)(2,1)S(1)} %collective-permute-done.28.pt, ...), custom_call_target="tpu_custom_call" | custom-call | flops 1073741824 | bytes 2097152 | tf_op jit(solution)/shard_map/attend/pallas_call | solution.py:357
  171.2 3.4 %convolution_add_fusion = f32[2,6144]{1,0:T(2,128)S(1)} fusion(bf16[384,6144]{1,0:T(8,128)(2,1)} %param.26, bf16[640,384]{1,0:T(8,128)(2,1)} %attend.1, f32[2,6144]{1,0:T(2,128)S(1)} %bitcast.35, pred[6144]{0:T(1024)(128)(4,1)S(1)} %broadcast_in_dim.119, s32[2]{0:T(128)S(1)} %fusion.15), kind=kOutput, calls=%fused_computation.1 | convolution fusion | flops 10446848 | bytes 5314568 | tf_op jit(solution)/shard_map/dot_general | solution.py:543
  175.2 2.2 collective-permute-start.32
  179.4 1.9 collective-permute-start.33
  187.2 21.1 %all-gather.1 = bf16[8,2,6144]{2,1,0:T(2,128)(2,1)S(1)} all-gather(bf16[1,2,6144]{2,1,0:T(2,128)(2,1)S(1)} %fusion.12), channel_id=1, replica_groups=mesh['req'=8,'hid'=16] {'req'}, dimensions={0}, use_global_device_ids=true | all-gather | bytes 221184 | tf_op jit(solution)/shard_map/all_gather | solution.py:551
  209.1 3.8 %convolution_reduce_fusion = f32[16]{0:T(128)S(1)} fusion(bf16[384,6144]{1,0:T(8,128)(2,1)} %param.28, f32[16,6144]{1,0:T(8,128)S(1)} %reshape.317, f32[6144]{0:T(1024)S(1)} %convert_element_type.50, f32[16]{0:T(128)S(1)} %get-tuple-element.37), kind=kOutput, calls=%fused_computation.6 | convolution fusion | flops 75798512 | bytes 5136512 | tf_op jit(solution)/shard_map/dot_general | solution.py:558
  212.9 3.3 %collective-permute-start.37 = (f32[16]{0:T(128)S(1)}, f32[16]{0:T(128)S(1)}, u32[]{:S(2)}, u32[]{:S(2)}) collective-permute-start(f32[16]{0:T(128)S(1)} %convolution_reduce_fusion), channel_id=1, source_target_pairs={{1,0},{2,1},{3,2},{0,3},{5,4},{6,5},{7,6},{4,7},{9,8},{10,9},{11,1... | collective-permute-start | bytes 200 | tf_op jit(solution)/shard_map/ppermute | solution.py:43
  217.5 2.7 %collective-permute-done.38 = f32[16]{0:T(128)S(1)} collective-permute-done((f32[16]{0:T(128)S(1)}, f32[16]{0:T(128)S(1)}, u32[]{:S(2)}, u32[]{:S(2)}) %collective-permute-start.38) | collective-permute-done | bytes 96 | tf_op jit(solution)/shard_map/ppermute | solution.py:43
  220.2 2.7 %collective-permute-start.40 = (f32[16]{0:T(128)S(1)}, f32[16]{0:T(128)S(1)}, u32[]{:S(2)}, u32[]{:S(2)}) collective-permute-start(f32[16]{0:T(128)S(1)} %maximum_maximum_fusion.1), channel_id=1, source_target_pairs={{4,0},{5,1},{6,2},{7,3},{8,4},{9,5},{10,6},{11,7},{12,8},{13,9},{1... | collective-permute-start | bytes 200 | tf_op jit(solution)/shard_map/ppermute | solution.py:43
  224.2 2.6 %collective-permute-done.41 = f32[16]{0:T(128)S(1)} collective-permute-done((f32[16]{0:T(128)S(1)}, f32[16]{0:T(128)S(1)}, u32[]{:S(2)}, u32[]{:S(2)}) %collective-permute-start.41) | collective-permute-done | bytes 96 | tf_op jit(solution)/shard_map/ppermute | solution.py:43
  226.8 15.8 %pmax.7 = f32[16]{0:T(128)} all-reduce(f32[16]{0:T(128)S(1)} %maximum_maximum_fusion), channel_id=1, replica_groups=mesh['req'=8,'hid'=16] {'req'}, use_global_device_ids=true, to_apply=%region_6.7 | all-reduce | flops 16 | bytes 128 | tf_op jit(solution)/shard_map/pmax | solution.py:565
  242.7 10.7 %finish.1 = bf16[2,480,384]{2,1,0:T(8,128)(2,1)} custom-call(bf16[2,480,384]{2,1,0:T(8,128)(2,1)S(1)} %copy-done, bf16[256,384]{1,0:T(8,128)(2,1)S(1)} %bitcast.28, bf16[10240,384]{1,0:T(8,128)(2,1)} %all-gather.8.cloned.1.call-done.a_hbm, bf16[8,16,48,384]{3,2,1,0:T(8,128)(2,1)} %bitcast.32, s32[2,480,1]{2,1,0:T(8,128)S(1)} %fusion.4.slot_ref), custom_call_target="tpu_custom_call" | custom-call | flops 3019898880 | bytes 14680064 | tf_op jit(solution)/shard_map/finish/pallas_call | solution.py:416
  (162 shorter events, 41.8 us)
Async XLA Ops:
  7.2 88.1 %all-gather.6.cloned.1.call-start = ((), (), s32[]{:S(2)}) async-start(), calls=%async_computation.2 | async-start | bytes 7798784 | tf_op jit(solution)/shard_map/all_gather | solution.py:493
  15.8 12.5 %collective-permute-start.7 = (bf16[192,384]{1,0:T(8,128)(2,1)S(1)}, bf16[192,384]{1,0:T(8,128)(2,1)}, u32[]{:S(2)}, u32[]{:S(2)}) collective-permute-start(bf16[192,384]{1,0:T(8,128)(2,1)S(1)} %get-tuple-element.30), channel_id=1, source_target_pairs={{12,0},{13,1},{14,2},{15,3},{0,4},{1,5},{2,6},{3,7},{4,8},{5,9},{6... | collective-permute-start | bytes 442376 | tf_op jit(solution)/shard_map/ppermute | solution.py:43
  17.9 19.5 %collective-permute-start.8 = (bf16[192,384]{1,0:T(8,128)(2,1)S(1)}, bf16[192,384]{1,0:T(8,128)(2,1)}, u32[]{:S(2)}, u32[]{:S(2)}) collective-permute-start(bf16[192,384]{1,0:T(8,128)(2,1)S(1)} %get-tuple-element.30), channel_id=1, source_target_pairs={{4,0},{5,1},{6,2},{7,3},{8,4},{9,5},{10,6},{11,7},{12,8},{13,9},{1... | collective-permute-start | bytes 442376 | tf_op jit(solution)/shard_map/ppermute | solution.py:43
  19.2 18.1 %collective-permute-start.9 = (bf16[192,384]{1,0:T(8,128)(2,1)S(1)}, bf16[192,384]{1,0:T(8,128)(2,1)}, u32[]{:S(2)}, u32[]{:S(2)}) collective-permute-start(bf16[192,384]{1,0:T(8,128)(2,1)S(1)} %get-tuple-element.30), channel_id=1, source_target_pairs={{8,0},{9,1},{10,2},{11,3},{12,4},{13,5},{14,6},{15,7},{0,8},{1,9},... | collective-permute-start | bytes 442376 | tf_op jit(solution)/shard_map/ppermute | solution.py:43
  20.9 20.4 %collective-permute-start = (bf16[192,384]{1,0:T(8,128)(2,1)S(1)}, bf16[192,384]{1,0:T(8,128)(2,1)}, u32[]{:S(2)}, u32[]{:S(2)}) collective-permute-start(bf16[192,384]{1,0:T(8,128)(2,1)S(1)} %get-tuple-element.31), channel_id=1, source_target_pairs={{3,0},{0,1},{1,2},{2,3},{7,4},{4,5},{5,6},{6,7},{11,8},{8,9},{9,10... | collective-permute-start | bytes 442376 | tf_op jit(solution)/shard_map/ppermute | solution.py:43
  22.5 18.7 %collective-permute-start.1 = (bf16[192,384]{1,0:T(8,128)(2,1)S(1)}, bf16[192,384]{1,0:T(8,128)(2,1)}, u32[]{:S(2)}, u32[]{:S(2)}) collective-permute-start(bf16[192,384]{1,0:T(8,128)(2,1)S(1)} %get-tuple-element.31), channel_id=1, source_target_pairs={{1,0},{2,1},{3,2},{0,3},{5,4},{6,5},{7,6},{4,7},{9,8},{10,9},{11,1... | collective-permute-start | bytes 442376 | tf_op jit(solution)/shard_map/ppermute | solution.py:43
  28.3 13.0 %collective-permute-start.2 = (bf16[192,384]{1,0:T(8,128)(2,1)S(1)}, bf16[192,384]{1,0:T(8,128)(2,1)}, u32[]{:S(2)}, u32[]{:S(2)}) collective-permute-start(bf16[192,384]{1,0:T(8,128)(2,1)S(1)} %get-tuple-element.31), channel_id=1, source_target_pairs={{2,0},{3,1},{0,2},{1,3},{6,4},{7,5},{4,6},{5,7},{10,8},{11,9},{8,1... | collective-permute-start | bytes 442376 | tf_op jit(solution)/shard_map/ppermute | solution.py:43
  38.5 13.7 %collective-permute-start.10 = (bf16[768,384]{1,0:T(8,128)(2,1)S(1)}, bf16[768,384]{1,0:T(8,128)(2,1)S(1)}, u32[]{:S(2)}, u32[]{:S(2)}) collective-permute-start(bf16[768,384]{1,0:T(8,128)(2,1)S(1)} %pad_maximum_fusion.1.refs_5_), channel_id=1, source_target_pairs={{3,0},{0,1},{1,2},{2,3},{7,4},{4,5},{5,6},{6,7},{11,8},{8,9},{9,10... | collective-permute-start | bytes 1769480 | tf_op jit(solution)/shard_map/ppermute | solution.py:43
  39.3 13.7 %collective-permute-start.11 = (bf16[768,384]{1,0:T(8,128)(2,1)S(1)}, bf16[768,384]{1,0:T(8,128)(2,1)S(1)}, u32[]{:S(2)}, u32[]{:S(2)}) collective-permute-start(bf16[768,384]{1,0:T(8,128)(2,1)S(1)} %pad_maximum_fusion.1.refs_5_), channel_id=1, source_target_pairs={{1,0},{2,1},{3,2},{0,3},{5,4},{6,5},{7,6},{4,7},{9,8},{10,9},{11,1... | collective-permute-start | bytes 1769480 | tf_op jit(solution)/shard_map/ppermute | solution.py:43
  42.4 15.6 %collective-permute-start.3 = (bf16[768,384]{1,0:T(8,128)(2,1)S(1)}, bf16[768,384]{1,0:T(8,128)(2,1)S(1)}, u32[]{:S(2)}, u32[]{:S(2)}) collective-permute-start(bf16[768,384]{1,0:T(8,128)(2,1)S(1)} %pad_maximum_fusion.refs_0_), channel_id=1, source_target_pairs={{12,0},{13,1},{14,2},{15,3},{0,4},{1,5},{2,6},{3,7},{4,8},{5,9},{6... | collective-permute-start | bytes 1769480 | tf_op jit(solution)/shard_map/ppermute | solution.py:43
  42.7 16.6 %collective-permute-start.4 = (bf16[768,384]{1,0:T(8,128)(2,1)S(1)}, bf16[768,384]{1,0:T(8,128)(2,1)S(1)}, u32[]{:S(2)}, u32[]{:S(2)}) collective-permute-start(bf16[768,384]{1,0:T(8,128)(2,1)S(1)} %pad_maximum_fusion.refs_0_), channel_id=1, source_target_pairs={{4,0},{5,1},{6,2},{7,3},{8,4},{9,5},{10,6},{11,7},{12,8},{13,9},{1... | collective-permute-start | bytes 1769480 | tf_op jit(solution)/shard_map/ppermute | solution.py:43
  52.3 14.9 %collective-permute-start.12 = (bf16[384,384]{1,0:T(8,128)(2,1)S(1)}, bf16[384,384]{1,0:T(8,128)(2,1)S(1)}, u32[]{:S(2)}, u32[]{:S(2)}) collective-permute-start(bf16[384,384]{1,0:T(8,128)(2,1)S(1)} %slice.92), channel_id=1, source_target_pairs={{3,0},{0,1},{1,2},{2,3},{7,4},{4,5},{5,6},{6,7},{11,8},{8,9},{9,10... | collective-permute-start | bytes 884744 | tf_op jit(solution)/shard_map/ppermute | solution.py:43
  53.0 14.9 %collective-permute-start.13 = (bf16[384,384]{1,0:T(8,128)(2,1)S(1)}, bf16[384,384]{1,0:T(8,128)(2,1)S(1)}, u32[]{:S(2)}, u32[]{:S(2)}) collective-permute-start(bf16[384,384]{1,0:T(8,128)(2,1)S(1)} %slice.93), channel_id=1, source_target_pairs={{1,0},{2,1},{3,2},{0,3},{5,4},{6,5},{7,6},{4,7},{9,8},{10,9},{11,1... | collective-permute-start | bytes 884744 | tf_op jit(solution)/shard_map/ppermute | solution.py:43
  58.0 15.6 %collective-permute-start.5 = (bf16[384,384]{1,0:T(8,128)(2,1)S(1)}, bf16[384,384]{1,0:T(8,128)(2,1)S(1)}, u32[]{:S(2)}, u32[]{:S(2)}) collective-permute-start(bf16[384,384]{1,0:T(8,128)(2,1)S(1)} %slice.89), channel_id=1, source_target_pairs={{12,0},{13,1},{14,2},{15,3},{0,4},{1,5},{2,6},{3,7},{4,8},{5,9},{6... | collective-permute-start | bytes 884744 | tf_op jit(solution)/shard_map/ppermute | solution.py:43
  59.3 16.0 %collective-permute-start.6 = (bf16[384,384]{1,0:T(8,128)(2,1)S(1)}, bf16[384,384]{1,0:T(8,128)(2,1)S(1)}, u32[]{:S(2)}, u32[]{:S(2)}) collective-permute-start(bf16[384,384]{1,0:T(8,128)(2,1)S(1)} %slice.90), channel_id=1, source_target_pairs={{4,0},{5,1},{6,2},{7,3},{8,4},{9,5},{10,6},{11,7},{12,8},{13,9},{1... | collective-permute-start | bytes 884744 | tf_op jit(solution)/shard_map/ppermute | solution.py:43
  63.4 40.0 %copy-start.17 = (f32[384]{0:T(512)S(1)}, f32[384]{0:T(512)}, u32[]{:S(2)}) copy-start(f32[384]{0:T(512)} %param.20) | copy-start | bytes 4612
  97.3 17.7 %all-to-all-start = ((bf16[16,48,384]{2,1,0:T(8,128)(2,1)}), bf16[16,48,384]{2,1,0:T(8,128)(2,1)S(1)}, u32[]{:S(2)}, u32[]{:S(2)}) async-start(bf16[16,48,384]{2,1,0:T(8,128)(2,1)} %copy.59), calls=%async_computation | async-start | bytes 1179648 | tf_op jit(solution)/shard_map/all_to_all | solution.py:512
  101.5 141.2 %all-gather.10.cloned.1.call-start = ((), (), s32[]{:S(2)}) async-start(), calls=%async_computation.4 | async-start | bytes 5308416 | tf_op jit(solution)/shard_map/all_gather | solution.py:527
  126.0 116.6 %all-gather.8.cloned.1.call-start = ((), (), s32[]{:S(2)}) async-start(), calls=%async_computation.3 | async-start | bytes 8355840 | tf_op jit(solution)/shard_map/all_gather | solution.py:537
  126.1 7.4 %collective-permute-start.21 = (bf16[128,384]{1,0:T(8,128)(2,1)S(1)}, bf16[128,384]{1,0:T(8,128)(2,1)S(1)}, u32[]{:S(2)}, u32[]{:S(2)}) collective-permute-start(bf16[128,384]{1,0:T(8,128)(2,1)S(1)} %get-tuple-element.32), channel_id=1, source_target_pairs={{12,0},{13,1},{14,2},{15,3},{0,4},{1,5},{2,6},{3,7},{4,8},{5,9},{6... | collective-permute-start | bytes 294920 | tf_op jit(solution)/shard_map/ppermute | solution.py:43
  127.8 7.1 %collective-permute-start.22 = (bf16[128,384]{1,0:T(8,128)(2,1)S(1)}, bf16[128,384]{1,0:T(8,128)(2,1)S(1)}, u32[]{:S(2)}, u32[]{:S(2)}) collective-permute-start(bf16[128,384]{1,0:T(8,128)(2,1)S(1)} %get-tuple-element.32), channel_id=1, source_target_pairs={{4,0},{5,1},{6,2},{7,3},{8,4},{9,5},{10,6},{11,7},{12,8},{13,9},{1... | collective-permute-start | bytes 294920 | tf_op jit(solution)/shard_map/ppermute | solution.py:43
  129.1 5.8 %collective-permute-start.23 = (bf16[128,384]{1,0:T(8,128)(2,1)S(1)}, bf16[128,384]{1,0:T(8,128)(2,1)S(1)}, u32[]{:S(2)}, u32[]{:S(2)}) collective-permute-start(bf16[128,384]{1,0:T(8,128)(2,1)S(1)} %get-tuple-element.32), channel_id=1, source_target_pairs={{8,0},{9,1},{10,2},{11,3},{12,4},{13,5},{14,6},{15,7},{0,8},{1,9},... | collective-permute-start | bytes 294920 | tf_op jit(solution)/shard_map/ppermute | solution.py:43
  130.8 7.0 %collective-permute-start.14 = (bf16[128,384]{1,0:T(8,128)(2,1)S(1)}, bf16[128,384]{1,0:T(8,128)(2,1)S(1)}, u32[]{:S(2)}, u32[]{:S(2)}) collective-permute-start(bf16[128,384]{1,0:T(8,128)(2,1)S(1)} %get-tuple-element.33), channel_id=1, source_target_pairs={{3,0},{0,1},{1,2},{2,3},{7,4},{4,5},{5,6},{6,7},{11,8},{8,9},{9,10... | collective-permute-start | bytes 294920 | tf_op jit(solution)/shard_map/ppermute | solution.py:43
  132.0 5.8 %collective-permute-start.15 = (bf16[128,384]{1,0:T(8,128)(2,1)S(1)}, bf16[128,384]{1,0:T(8,128)(2,1)S(1)}, u32[]{:S(2)}, u32[]{:S(2)}) collective-permute-start(bf16[128,384]{1,0:T(8,128)(2,1)S(1)} %get-tuple-element.33), channel_id=1, source_target_pairs={{1,0},{2,1},{3,2},{0,3},{5,4},{6,5},{7,6},{4,7},{9,8},{10,9},{11,1... | collective-permute-start | bytes 294920 | tf_op jit(solution)/shard_map/ppermute | solution.py:43
  133.5 5.8 %collective-permute-start.16 = (bf16[128,384]{1,0:T(8,128)(2,1)S(1)}, bf16[128,384]{1,0:T(8,128)(2,1)S(1)}, u32[]{:S(2)}, u32[]{:S(2)}) collective-permute-start(bf16[128,384]{1,0:T(8,128)(2,1)S(1)} %get-tuple-element.33), channel_id=1, source_target_pairs={{2,0},{3,1},{0,2},{1,3},{6,4},{7,5},{4,6},{5,7},{10,8},{11,9},{8,1... | collective-permute-start | bytes 294920 | tf_op jit(solution)/shard_map/ppermute | solution.py:43
  135.0 11.8 %collective-permute-start.24 = (bf16[512,384]{1,0:T(8,128)(2,1)S(1)}, bf16[512,384]{1,0:T(8,128)(2,1)S(1)}, u32[]{:S(2)}, u32[]{:S(2)}) collective-permute-start(bf16[512,384]{1,0:T(8,128)(2,1)S(1)} %pad_maximum_fusion.3.refs_5_), channel_id=1, source_target_pairs={{3,0},{0,1},{1,2},{2,3},{7,4},{4,5},{5,6},{6,7},{11,8},{8,9},{9,10... | collective-permute-start | bytes 1179656 | tf_op jit(solution)/shard_map/ppermute | solution.py:43
  136.0 10.9 %collective-permute-start.25 = (bf16[512,384]{1,0:T(8,128)(2,1)S(1)}, bf16[512,384]{1,0:T(8,128)(2,1)S(1)}, u32[]{:S(2)}, u32[]{:S(2)}) collective-permute-start(bf16[512,384]{1,0:T(8,128)(2,1)S(1)} %pad_maximum_fusion.3.refs_5_), channel_id=1, source_target_pairs={{1,0},{2,1},{3,2},{0,3},{5,4},{6,5},{7,6},{4,7},{9,8},{10,9},{11,1... | collective-permute-start | bytes 1179656 | tf_op jit(solution)/shard_map/ppermute | solution.py:43
  139.4 10.3 %collective-permute-start.17 = (bf16[512,384]{1,0:T(8,128)(2,1)S(1)}, bf16[512,384]{1,0:T(8,128)(2,1)S(1)}, u32[]{:S(2)}, u32[]{:S(2)}) collective-permute-start(bf16[512,384]{1,0:T(8,128)(2,1)S(1)} %pad_maximum_fusion.2.refs_0_), channel_id=1, source_target_pairs={{12,0},{13,1},{14,2},{15,3},{0,4},{1,5},{2,6},{3,7},{4,8},{5,9},{6... | collective-permute-start | bytes 1179656 | tf_op jit(solution)/shard_map/ppermute | solution.py:43
  139.7 10.3 %collective-permute-start.18 = (bf16[512,384]{1,0:T(8,128)(2,1)S(1)}, bf16[512,384]{1,0:T(8,128)(2,1)S(1)}, u32[]{:S(2)}, u32[]{:S(2)}) collective-permute-start(bf16[512,384]{1,0:T(8,128)(2,1)S(1)} %pad_maximum_fusion.2.refs_0_), channel_id=1, source_target_pairs={{4,0},{5,1},{6,2},{7,3},{8,4},{9,5},{10,6},{11,7},{12,8},{13,9},{1... | collective-permute-start | bytes 1179656 | tf_op jit(solution)/shard_map/ppermute | solution.py:43
  146.8 6.3 %collective-permute-start.26 = (bf16[256,384]{1,0:T(8,128)(2,1)S(1)}, bf16[256,384]{1,0:T(8,128)(2,1)S(1)}, u32[]{:S(2)}, u32[]{:S(2)}) collective-permute-start(bf16[256,384]{1,0:T(8,128)(2,1)S(1)} %slice.101), channel_id=1, source_target_pairs={{3,0},{0,1},{1,2},{2,3},{7,4},{4,5},{5,6},{6,7},{11,8},{8,9},{9,10... | collective-permute-start | bytes 589832 | tf_op jit(solution)/shard_map/ppermute | solution.py:43
  147.0 6.2 %collective-permute-start.27 = (bf16[256,384]{1,0:T(8,128)(2,1)S(1)}, bf16[256,384]{1,0:T(8,128)(2,1)S(1)}, u32[]{:S(2)}, u32[]{:S(2)}) collective-permute-start(bf16[256,384]{1,0:T(8,128)(2,1)S(1)} %slice.102), channel_id=1, source_target_pairs={{1,0},{2,1},{3,2},{0,3},{5,4},{6,5},{7,6},{4,7},{9,8},{10,9},{11,1... | collective-permute-start | bytes 589832 | tf_op jit(solution)/shard_map/ppermute | solution.py:43
  149.7 6.2 %collective-permute-start.19 = (bf16[256,384]{1,0:T(8,128)(2,1)S(1)}, bf16[256,384]{1,0:T(8,128)(2,1)S(1)}, u32[]{:S(2)}, u32[]{:S(2)}) collective-permute-start(bf16[256,384]{1,0:T(8,128)(2,1)S(1)} %slice.99), channel_id=1, source_target_pairs={{12,0},{13,1},{14,2},{15,3},{0,4},{1,5},{2,6},{3,7},{4,8},{5,9},{6... | collective-permute-start | bytes 589832 | tf_op jit(solution)/shard_map/ppermute | solution.py:43
  150.1 5.8 %collective-permute-start.20 = (bf16[256,384]{1,0:T(8,128)(2,1)S(1)}, bf16[256,384]{1,0:T(8,128)(2,1)S(1)}, u32[]{:S(2)}, u32[]{:S(2)}) collective-permute-start(bf16[256,384]{1,0:T(8,128)(2,1)S(1)} %slice.100), channel_id=1, source_target_pairs={{4,0},{5,1},{6,2},{7,3},{8,4},{9,5},{10,6},{11,7},{12,8},{13,9},{1... | collective-permute-start | bytes 589832 | tf_op jit(solution)/shard_map/ppermute | solution.py:43
  152.8 7.8 %collective-permute-start.28 = (bf16[384,128]{1,0:T(8,128)(2,1)S(1)}, bf16[384,128]{1,0:T(8,128)(2,1)S(1)}, u32[]{:S(2)}, u32[]{:S(2)}) collective-permute-start(bf16[384,128]{1,0:T(8,128)(2,1)S(1)} %copy-done.5), channel_id=1, source_target_pairs={{0,1},{1,0},{2,3},{3,2},{4,5},{5,4},{6,7},{7,6},{8,9},{9,8},{10,11... | collective-permute-start | bytes 294920 | tf_op jit(solution)/shard_map/ppermute | solution.py:524
  160.5 3.2 %collective-permute-start.29 = (bf16[256,128]{1,0:T(8,128)(2,1)S(1)}, bf16[256,128]{1,0:T(8,128)(2,1)S(1)}, u32[]{:S(2)}, u32[]{:S(2)}) collective-permute-start(bf16[256,128]{1,0:T(8,128)(2,1)S(1)} %get-tuple-element.25.oi), channel_id=1, source_target_pairs={{0,1},{1,0},{2,3},{3,2},{4,5},{5,4},{6,7},{7,6},{8,9},{9,8},{10,11... | collective-permute-start | bytes 196616 | tf_op jit(solution)/shard_map/ppermute | solution.py:531
  174.6 68.1 %copy-start = (bf16[2,480,384]{2,1,0:T(8,128)(2,1)S(1)}, bf16[2,480,384]{2,1,0:T(8,128)(2,1)}, u32[]{:S(2)}) copy-start(bf16[2,480,384]{2,1,0:T(8,128)(2,1)} %text_ref.1) | copy-start | bytes 2211844
  174.6 4.6 %collective-permute-start.30 = (f32[2,6144]{1,0:T(2,128)S(1)}, f32[2,6144]{1,0:T(2,128)S(1)}, u32[]{:S(2)}, u32[]{:S(2)}) collective-permute-start(f32[2,6144]{1,0:T(2,128)S(1)} %convolution_add_fusion), channel_id=1, source_target_pairs={{2,0},{3,1},{0,2},{1,3},{6,4},{7,5},{4,6},{5,7},{10,8},{11,9},{8,1... | collective-permute-start | bytes 147464 | tf_op jit(solution)/shard_map/ppermute | solution.py:43
  174.7 4.7 %collective-permute-start.31 = (f32[2,6144]{1,0:T(2,128)S(1)}, f32[2,6144]{1,0:T(2,128)S(1)}, u32[]{:S(2)}, u32[]{:S(2)}) collective-permute-start(f32[2,6144]{1,0:T(2,128)S(1)} %convolution_add_fusion), channel_id=1, source_target_pairs={{3,0},{0,1},{1,2},{2,3},{7,4},{4,5},{5,6},{6,7},{11,8},{8,9},{9,10... | collective-permute-start | bytes 147464 | tf_op jit(solution)/shard_map/ppermute | solution.py:43
  175.2 4.2 %collective-permute-start.32 = (f32[2,6144]{1,0:T(2,128)S(1)}, f32[2,6144]{1,0:T(2,128)S(1)}, u32[]{:S(2)}, u32[]{:S(2)}) collective-permute-start(f32[2,6144]{1,0:T(2,128)S(1)} %convolution_add_fusion), channel_id=1, source_target_pairs={{1,0},{2,1},{3,2},{0,3},{5,4},{6,5},{7,6},{4,7},{9,8},{10,9},{11,1... | collective-permute-start | bytes 147464 | tf_op jit(solution)/shard_map/ppermute | solution.py:43
  179.4 4.8 %collective-permute-start.33 = (f32[2,6144]{1,0:T(2,128)S(1)}, f32[2,6144]{1,0:T(2,128)S(1)}, u32[]{:S(2)}, u32[]{:S(2)}) collective-permute-start(f32[2,6144]{1,0:T(2,128)S(1)} %add_add_fusion), channel_id=1, source_target_pairs={{8,0},{9,1},{10,2},{11,3},{12,4},{13,5},{14,6},{15,7},{0,8},{1,9},... | collective-permute-start | bytes 147464 | tf_op jit(solution)/shard_map/ppermute | solution.py:43
  181.3 4.4 %collective-permute-start.34 = (f32[2,6144]{1,0:T(2,128)S(1)}, f32[2,6144]{1,0:T(2,128)S(1)}, u32[]{:S(2)}, u32[]{:S(2)}) collective-permute-start(f32[2,6144]{1,0:T(2,128)S(1)} %add_add_fusion), channel_id=1, source_target_pairs={{12,0},{13,1},{14,2},{15,3},{0,4},{1,5},{2,6},{3,7},{4,8},{5,9},{6... | collective-permute-start | bytes 147464 | tf_op jit(solution)/shard_map/ppermute | solution.py:43
  182.9 4.2 %collective-permute-start.35 = (f32[2,6144]{1,0:T(2,128)S(1)}, f32[2,6144]{1,0:T(2,128)S(1)}, u32[]{:S(2)}, u32[]{:S(2)}) collective-permute-start(f32[2,6144]{1,0:T(2,128)S(1)} %add_add_fusion), channel_id=1, source_target_pairs={{4,0},{5,1},{6,2},{7,3},{8,4},{9,5},{10,6},{11,7},{12,8},{13,9},{1... | collective-permute-start | bytes 147464 | tf_op jit(solution)/shard_map/ppermute | solution.py:43
  212.8 4.6 %collective-permute-start.36 = (f32[16]{0:T(128)S(1)}, f32[16]{0:T(128)S(1)}, u32[]{:S(2)}, u32[]{:S(2)}) collective-permute-start(f32[16]{0:T(128)S(1)} %convolution_reduce_fusion), channel_id=1, source_target_pairs={{3,0},{0,1},{1,2},{2,3},{7,4},{4,5},{5,6},{6,7},{11,8},{8,9},{9,10... | collective-permute-start | bytes 200 | tf_op jit(solution)/shard_map/ppermute | solution.py:43
  212.9 4.6 %collective-permute-start.37 = (f32[16]{0:T(128)S(1)}, f32[16]{0:T(128)S(1)}, u32[]{:S(2)}, u32[]{:S(2)}) collective-permute-start(f32[16]{0:T(128)S(1)} %convolution_reduce_fusion), channel_id=1, source_target_pairs={{1,0},{2,1},{3,2},{0,3},{5,4},{6,5},{7,6},{4,7},{9,8},{10,9},{11,1... | collective-permute-start | bytes 200 | tf_op jit(solution)/shard_map/ppermute | solution.py:43
  216.2 4.0 %collective-permute-start.38 = (f32[16]{0:T(128)S(1)}, f32[16]{0:T(128)S(1)}, u32[]{:S(2)}, u32[]{:S(2)}) collective-permute-start(f32[16]{0:T(128)S(1)} %convolution_reduce_fusion), channel_id=1, source_target_pairs={{2,0},{3,1},{0,2},{1,3},{6,4},{7,5},{4,6},{5,7},{10,8},{11,9},{8,1... | collective-permute-start | bytes 200 | tf_op jit(solution)/shard_map/ppermute | solution.py:43
  220.2 4.0 %collective-permute-start.39 = (f32[16]{0:T(128)S(1)}, f32[16]{0:T(128)S(1)}, u32[]{:S(2)}, u32[]{:S(2)}) collective-permute-start(f32[16]{0:T(128)S(1)} %maximum_maximum_fusion.1), channel_id=1, source_target_pairs={{12,0},{13,1},{14,2},{15,3},{0,4},{1,5},{2,6},{3,7},{4,8},{5,9},{6... | collective-permute-start | bytes 200 | tf_op jit(solution)/shard_map/ppermute | solution.py:43
  220.2 4.0 %collective-permute-start.40 = (f32[16]{0:T(128)S(1)}, f32[16]{0:T(128)S(1)}, u32[]{:S(2)}, u32[]{:S(2)}) collective-permute-start(f32[16]{0:T(128)S(1)} %maximum_maximum_fusion.1), channel_id=1, source_target_pairs={{4,0},{5,1},{6,2},{7,3},{8,4},{9,5},{10,6},{11,7},{12,8},{13,9},{1... | collective-permute-start | bytes 200 | tf_op jit(solution)/shard_map/ppermute | solution.py:43
  222.9 4.0 %collective-permute-start.41 = (f32[16]{0:T(128)S(1)}, f32[16]{0:T(128)S(1)}, u32[]{:S(2)}, u32[]{:S(2)}) collective-permute-start(f32[16]{0:T(128)S(1)} %maximum_maximum_fusion.1), channel_id=1, source_target_pairs={{8,0},{9,1},{10,2},{11,3},{12,4},{13,5},{14,6},{15,7},{0,8},{1,9},... | collective-permute-start | bytes 200 | tf_op jit(solution)/shard_map/ppermute | solution.py:43
  (16 other events, 301.4 us)
Sparse Core Ops, SparseCore 0:
  11.5 83.7 all-gather.5
  126.2 34.6 all-gather.9
  170.5 71.7 all-gather.7

commit v4 on v3

--- a/solution.py
+++ b/solution.py
@@ -147,6 +147,30 @@
     )(tile_order, place, merged)
 
 
+def cut_kernel(row_ref, w_hbm, o_hbm, sem):
+    strip = FEAT // N_REQ
+    rows = pl.ds(pl.multiple_of(row_ref[0], strip), strip)
+    copies = [
+        pltpu.make_async_copy(w_hbm.at[rows, pl.ds(k * FEAT, FEAT)], o_hbm.at[k], sem.at[k])
+        for k in range(N_HID)
+    ]
+    for c in copies:
+        c.start()
+    for c in copies:
+        c.wait()
+
+
+def cut(weight, row):
+    return pl.pallas_call(
+        cut_kernel,
+        out_shape=jax.ShapeDtypeStruct((N_HID, FEAT // N_REQ, FEAT), BF),
+        in_specs=[pl.BlockSpec(memory_space=pltpu.SMEM), pl.BlockSpec(memory_space=pl.ANY)],
+        out_specs=pl.BlockSpec(memory_space=pl.ANY),
+        scratch_shapes=[pltpu.SemaphoreType.DMA((N_HID,))],
+        name="cut",
+    )(row, in_hbm(weight))
+
+
 def project_kernel(
     x_hbm, w_hbm, gb_ref, left_ref, pb_ref, o_ref, tail, x, w, wl, acc, sem, x_sem, w_sem
 ):
@@ -214,8 +238,12 @@
     o_ref[...] = y.astype(BF)
 
 
-def project(gathered, weight, gain, bias, out_bias):
+def gain_and_bias(gain, bias):
     both = jnp.stack([gain, bias]).astype(F32).reshape(2, N_HID, MFEAT)
+    return both[:, :, :MAIN], both[:, :, MAIN:].reshape(2, RING, 1, 128)
+
+
+def project(gathered, weight, both, left, out_bias):
     return pl.pallas_call(
         project_kernel,
         out_shape=jax.ShapeDtypeStruct((TILE, FEAT), BF),
@@ -239,8 +267,8 @@
     )(
         in_hbm(gathered),
         in_hbm(weight.reshape(N_HID, MFEAT, FEAT)),
-        both[:, :, :MAIN],
-        both[:, :, MAIN:].reshape(2, RING, 1, 128),
+        both,
+        left,
         out_bias,
     )
 
@@ -503,18 +531,20 @@
     partner = [(i, i ^ 1) for i in range(N_HID)]
     text_blocks, text_where = gather_far(gather_near(text_rows))
     strip = FEAT // N_REQ
-    piece = lax.dynamic_slice_in_dim(out_weight, me * strip, strip, axis=0)
-    piece = piece.reshape(strip, N_HID, FEAT).transpose(1, 0, 2)
+    piece = cut(out_weight, (me * strip)[None].astype(jnp.int32))
+    both, left = gain_and_bias(ln_gain, ln_bias)
+    both, left, *text_blocks[8:] = lax.optimization_barrier((both, left, *text_blocks[8:]))
     q_text, kv_text = qkv(
         text_blocks, text_where, weight, cos[:TEXT], sin[:TEXT], sources, "qkv_text"
     )
-    gathered, piece, q_text, kv_text = lax.optimization_barrier((gathered, piece, q_text, kv_text))
+    piece, q_text = lax.optimization_barrier((piece, q_text))
+    gathered, q_text, kv_text = lax.optimization_barrier((gathered, q_text, kv_text))
     piece = lax.all_to_all(piece, "hid", split_axis=0, concat_axis=0, tiled=True)
     projected = project(
         gathered,
         proj_weight,
-        ln_gain,
-        ln_bias,
+        both,
+        left,
         proj_bias[None, :],
     )
     projected, piece = lax.optimization_barrier((projected, piece))

time: 261 us -> 264 us (1.011)
  Pallas kernels: 40.6 us -> 59.7 us
  waiting for transfers between devices: 51.4 us -> 33.3 us
  blocking collectives: 47.9 us -> 52.4 us
    pallas_call x0 -> x1, Pallas kernels: none -> 19.1 us  [cut(): pl.pallas_call(cut_kernel, out_shape=jax.ShapeDtypeStruct((N_HID, FEAT //...]
    all_gather x1, waiting for transfers between devices: 13.1 us -> 0.02 us  [shards(): lax.all_gather(pack(merged, tile_order, (hid % RING)[None]), 'hid', axis=...]
    ppermute x40, waiting for transfers between devices: 35.2 us -> 30.2 us  [shift(): return lax.ppermute(block, 'hid', route)]
    all_to_all x1, blocking collectives: 11 us -> 15.5 us  [shards(): lax.all_to_all(projected.reshape(N_REQ, TILE // N_REQ, FEAT), 'req', spli...]
    unnamed x41 -> x42, local copies, waits for them, and re-layouts: 7.99 us -> 6.95 us
  transfers between devices with their start and end apart: 46 -> 46, of which waited for: 20 -> 14; matrix products, arithmetic and copies ran while one was open for 14% -> 14% of each run, Pallas kernels for 11% -> 18%
where the time goes in v4:
time: 264 us; the launch traced here: 263 us
  starting transfers between devices  60.7 us (23%)
  Pallas kernels  59.7 us (23%)
  blocking collectives  52.4 us (20%)
  waiting for transfers between devices  33.3 us (13%)
  other arithmetic  19.6 us (7%)
  between operations  16.4 us (6%)
  local copies, waits for them, and re-layouts  11.9 us (5%)
  matrix products  9.21 us (3%)
    ppermute x40, starting transfers between devices, shift(): return lax.ppermute(block, 'hid', route)  55.9 us
    ppermute x40, waiting for transfers between devices, shift(): return lax.ppermute(block, 'hid', route)  30.2 us
    all_gather x1, blocking collectives, shards(): all_last = lax.all_gather(full_width, 'req', axis=0, tiled=True)  21.1 us
    pallas_call x1, Pallas kernels, cut(): pl.pallas_call(cut_kernel, out_shape=jax.ShapeDtypeStruct((N_HID, FEAT //...  19.1 us
    pmax x1, blocking collectives, shards(): logit_max = lax.pmax(top, 'req')  15.8 us
    all_to_all x1, blocking collectives, shards(): lax.all_to_all(projected.reshape(N_REQ, TILE // N_REQ, FEAT), 'req', spli...  15.5 us
    pallas_call x1, Pallas kernels, project(): pl.pallas_call(project_kernel, out_shape=jax.ShapeDtypeStruct((TILE, FEAT...  11.5 us
    pallas_call x1, Pallas kernels, finish(): pl.pallas_call(finish_kernel, out_shape=jax.ShapeDtypeStruct((REQ_GRP, LE...  10.7 us
  transfers between devices with their start and end apart: 46, of which 14 were waited for; matrix products, arithmetic and copies ran while one was open for 14% of the time, Pallas kernels for 18%

profile of v4, /device:TPU:1, one launch (start us, length us, event | category | flops | bytes accessed | tf_op | source)
XLA Modules:
  0.0 263.3 jit_solution(9058355849550094058)
XLA Ops:
  9.7 1.7 pack.1
  14.0 1.7 fusion.1
  15.8 2.1 collective-permute-start.7
  19.2 1.6 collective-permute-start.9
  20.9 1.6 collective-permute-start
  22.5 2.1 collective-permute-start.1
  24.7 1.8 copy.39
  26.5 1.8 copy.40
  29.7 7.7 %multiply_convert_fusion.refs_10_ = bf16[6144,512]{1,0:T(8,128)(2,1)} fusion(bf16[6144,64]{1,0:T(8,128)(2,1)S(1)} %copy.40, bf16[6144,64]{1,0:T(8,128)(2,1)S(1)} %copy.39, bf16[6144,384]{1,0:T(8,128)(2,1)} %param.23, f32[6144]{0:T(1024)S(1)} %convert_element_type.44), kind=kLoop, calls=%fused_computation | loop fusion | flops 25165824 | bytes 12607488 | tf_op jit(solution)/shard_map/convert_element_type | solution.py:530
  39.3 1.9 collective-permute-start.11
  42.7 2.4 collective-permute-start.4
  51.6 19.1 %cut.1 = bf16[16,48,384]{2,1,0:T(8,128)(2,1)} custom-call(s32[1]{0:T(128)} %bitcast.1.row_ref, bf16[384,6144]{1,0:T(8,128)(2,1)} %w_hbm.1), custom_call_target="tpu_custom_call" | custom-call | tf_op jit(solution)/shard_map/cut/pallas_call | solution.py:164
  72.2 2.7 %collective-permute-start.13 = (bf16[384,384]{1,0:T(8,128)(2,1)S(1)}, bf16[384,384]{1,0:T(8,128)(2,1)S(1)}, u32[]{:S(2)}, u32[]{:S(2)}) collective-permute-start(bf16[384,384]{1,0:T(8,128)(2,1)S(1)} %slice.94), channel_id=1, source_target_pairs={{1,0},{2,1},{3,2},{0,3},{5,4},{6,5},{7,6},{4,7},{9,8},{10,9},{11,1... | collective-permute-start | bytes 884744 | tf_op jit(solution)/shard_map/ppermute | solution.py:43
  75.0 2.9 %collective-permute-start.6 = (bf16[384,384]{1,0:T(8,128)(2,1)S(1)}, bf16[384,384]{1,0:T(8,128)(2,1)S(1)}, u32[]{:S(2)}, u32[]{:S(2)}) collective-permute-start(bf16[384,384]{1,0:T(8,128)(2,1)S(1)} %slice.90), channel_id=1, source_target_pairs={{4,0},{5,1},{6,2},{7,3},{8,4},{9,5},{10,6},{11,7},{12,8},{13,9},{1... | collective-permute-start | bytes 884744 | tf_op jit(solution)/shard_map/ppermute | solution.py:43
  78.2 9.2 %collective-permute-done.12.refs_8_ = bf16[384,384]{1,0:T(8,128)(2,1)S(1)} collective-permute-done((bf16[384,384]{1,0:T(8,128)(2,1)S(1)}, bf16[384,384]{1,0:T(8,128)(2,1)S(1)}, u32[]{:S(2)}, u32[]{:S(2)}) %collective-permute-start.12) | collective-permute-done | bytes 294944 | tf_op jit(solution)/shard_map/ppermute | solution.py:43
  87.4 2.7 %collective-permute-done.5.refs_3_ = bf16[384,384]{1,0:T(8,128)(2,1)S(1)} collective-permute-done((bf16[384,384]{1,0:T(8,128)(2,1)S(1)}, bf16[384,384]{1,0:T(8,128)(2,1)S(1)}, u32[]{:S(2)}, u32[]{:S(2)}) %collective-permute-start.5) | collective-permute-done | bytes 294944 | tf_op jit(solution)/shard_map/ppermute | solution.py:43
  90.1 5.5 %qkv_text.1 = (bf16[384,384]{1,0:T(8,128)(2,1)S(1)}, bf16[384,128]{1,0:T(8,128)(2,1)S(1)}) custom-call(s32[16]{0:T(128)S(1)} %fusion.22.src_ref, bf16[768,384]{1,0:T(8,128)(2,1)S(1)} %pad_maximum_fusion.refs_0_, bf16[768,384]{1,0:T(8,128)(2,1)S(1)} %collective-permute-done.3.refs_1_, bf16[768,384]{1,0:T(8,128)(2,1)S(1)} %collective-permute-done.4.refs_2_, ...), custom_call_target="tpu_custom_call" | custom-call | flops 2415919104 | bytes 12582912 | tf_op jit(solution)/shard_map/qkv_text/pallas_call | solution.py:323
  97.0 4.3 %all-to-all-start = ((bf16[16,48,384]{2,1,0:T(8,128)(2,1)}), bf16[16,48,384]{2,1,0:T(8,128)(2,1)S(1)}, u32[]{:S(2)}, u32[]{:S(2)}) async-start(bf16[16,48,384]{2,1,0:T(8,128)(2,1)} %cut.1), calls=%async_computation | async-start | bytes 1179648 | tf_op jit(solution)/shard_map/all_to_all | solution.py:542
  102.2 11.5 %project.1 = bf16[256,384]{1,0:T(8,128)(2,1)S(1)} custom-call(bf16[4096,896]{1,0:T(8,128)(2,1)} %all-gather.6.cloned.1.call-done.x_hbm, bf16[16,800,384]{2,1,0:T(8,128)(2,1)} %bitcast.28, f32[2,16,768]{2,1,0:T(8,128)S(1)} %copy-done.2, f32[2,4,1,128]{3,2,1,0:T(1,128)S(1)} %reshape.305.left_ref, f32[1,384]{1,0:T(1,128)S(1)} %broadcast_in_dim.112.pb_ref), custom_call_target="tpu_custom_call" | custom-call | flops 2516582400 | bytes 17825792 | tf_op jit(solution)/shard_map/project/pallas_call | solution.py:247
  113.8 15.5 %all_to_all.10 = bf16[8,32,384]{2,1,0:T(8,128)(2,1)S(1)} all-to-all(bf16[8,32,384]{2,1,0:T(8,128)(2,1)S(1)} %bitcast.26), channel_id=1, replica_groups=mesh['req'=8,'hid'=16] {'req'}, dimensions={0} | all-to-all | bytes 393216 | tf_op jit(solution)/shard_map/all_to_all | solution.py:551
  129.4 1.7 collective-permute-start.21
  132.4 1.7 collective-permute-start.23
  135.3 1.5 collective-permute-start.15
  136.8 1.5 collective-permute-start.16
  139.3 1.8 collective-permute-start.25
  141.1 1.5 collective-permute-done.16
  143.0 2.4 collective-permute-start.18
  147.7 2.4 collective-permute-done.24.refs_6_
  150.3 2.7 %collective-permute-start.27 = (bf16[256,384]{1,0:T(8,128)(2,1)S(1)}, bf16[256,384]{1,0:T(8,128)(2,1)S(1)}, u32[]{:S(2)}, u32[]{:S(2)}) collective-permute-start(bf16[256,384]{1,0:T(8,128)(2,1)S(1)} %slice.102), channel_id=1, source_target_pairs={{1,0},{2,1},{3,2},{0,3},{5,4},{6,5},{7,6},{4,7},{9,8},{10,9},{11,1... | collective-permute-start | bytes 589832 | tf_op jit(solution)/shard_map/ppermute | solution.py:43
  153.4 2.5 collective-permute-start.20
  156.5 2.7 %collective-permute-done.19.refs_3_ = bf16[256,384]{1,0:T(8,128)(2,1)S(1)} collective-permute-done((bf16[256,384]{1,0:T(8,128)(2,1)S(1)}, bf16[256,384]{1,0:T(8,128)(2,1)S(1)}, u32[]{:S(2)}, u32[]{:S(2)}) %collective-permute-start.19) | collective-permute-done | bytes 196640 | tf_op jit(solution)/shard_map/ppermute | solution.py:43
  159.2 4.5 %qkv_tile.1 = (bf16[256,384]{1,0:T(8,128)(2,1)S(1)}, bf16[256,128]{1,0:T(8,128)(2,1)S(1)}) custom-call(s32[16]{0:T(128)S(1)} %fusion.22.src_ref, bf16[512,384]{1,0:T(8,128)(2,1)S(1)} %pad_maximum_fusion.2.refs_0_, bf16[512,384]{1,0:T(8,128)(2,1)S(1)} %collective-permute-done.17.refs_1_, bf16[512,384]{1,0:T(8,128)(2,1)S(1)} %collective-permute-done.18.refs_2_, ...), custom_call_target="tpu_custom_call" | custom-call | flops 1610612736 | bytes 12582912 | tf_op jit(solution)/shard_map/qkv_tile/pallas_call | solution.py:323
  164.0 3.0 %collective-permute-done.29.pi = bf16[256,128]{1,0:T(8,128)(2,1)S(1)} collective-permute-done((bf16[256,128]{1,0:T(8,128)(2,1)S(1)}, bf16[256,128]{1,0:T(8,128)(2,1)S(1)}, u32[]{:S(2)}, u32[]{:S(2)}) %collective-permute-start.29) | collective-permute-done | bytes 65568 | tf_op jit(solution)/shard_map/ppermute | solution.py:561
  167.0 6.6 %attend.1 = bf16[640,384]{1,0:T(8,128)(2,1)} custom-call(s32[1]{0:T(128)} %bitcast.7.low_ref, bf16[384,384]{1,0:T(8,128)(2,1)S(1)} %copy-done.4, bf16[256,384]{1,0:T(8,128)(2,1)S(1)} %get-tuple-element.33.qi, bf16[384,128]{1,0:T(8,128)(2,1)S(1)} %copy-done.6, bf16[384,128]{1,0:T(8,128)(2,1)S(1)} %collective-permute-done.28.pt, ...), custom_call_target="tpu_custom_call" | custom-call | flops 1073741824 | bytes 2097152 | tf_op jit(solution)/shard_map/attend/pallas_call | solution.py:385
  174.5 3.4 %convolution_add_fusion = f32[2,6144]{1,0:T(2,128)S(1)} fusion(bf16[384,6144]{1,0:T(8,128)(2,1)} %w_hbm.1, bf16[640,384]{1,0:T(8,128)(2,1)} %attend.1, f32[2,6144]{1,0:T(2,128)S(1)} %bitcast.30, pred[6144]{0:T(1024)(128)(4,1)S(1)} %broadcast_in_dim.123, s32[2]{0:T(128)S(1)} %fusion.15), kind=kOutput, calls=%fused_computation.1 | convolution fusion | flops 10446848 | bytes 5314568 | tf_op jit(solution)/shard_map/dot_general | solution.py:573
  178.5 2.2 collective-permute-start.32
  180.9 1.6 collective-permute-done.30
  182.7 1.9 collective-permute-start.33
  184.6 1.6 collective-permute-start.34
  189.0 1.5 collective-permute-done.35
  190.5 21.1 %all-gather.1 = bf16[8,2,6144]{2,1,0:T(2,128)(2,1)S(1)} all-gather(bf16[1,2,6144]{2,1,0:T(2,128)(2,1)S(1)} %fusion.12), channel_id=1, replica_groups=mesh['req'=8,'hid'=16] {'req'}, dimensions={0}, use_global_device_ids=true | all-gather | bytes 221184 | tf_op jit(solution)/shard_map/all_gather | solution.py:581
  212.3 3.8 %convolution_reduce_fusion = f32[16]{0:T(128)S(1)} fusion(bf16[384,6144]{1,0:T(8,128)(2,1)} %param.28, f32[16,6144]{1,0:T(8,128)S(1)} %reshape.313, f32[6144]{0:T(1024)S(1)} %convert_element_type.50, f32[16]{0:T(128)S(1)} %get-tuple-element.47), kind=kOutput, calls=%fused_computation.6 | convolution fusion | flops 75798512 | bytes 5136512 | tf_op jit(solution)/shard_map/dot_general | solution.py:588
  216.2 3.3 %collective-permute-start.37 = (f32[16]{0:T(128)S(1)}, f32[16]{0:T(128)S(1)}, u32[]{:S(2)}, u32[]{:S(2)}) collective-permute-start(f32[16]{0:T(128)S(1)} %convolution_reduce_fusion), channel_id=1, source_target_pairs={{1,0},{2,1},{3,2},{0,3},{5,4},{6,5},{7,6},{4,7},{9,8},{10,9},{11,1... | collective-permute-start | bytes 200 | tf_op jit(solution)/shard_map/ppermute | solution.py:43
  220.8 2.7 %collective-permute-done.38 = f32[16]{0:T(128)S(1)} collective-permute-done((f32[16]{0:T(128)S(1)}, f32[16]{0:T(128)S(1)}, u32[]{:S(2)}, u32[]{:S(2)}) %collective-permute-start.38) | collective-permute-done | bytes 96 | tf_op jit(solution)/shard_map/ppermute | solution.py:43
  223.5 2.7 %collective-permute-start.40 = (f32[16]{0:T(128)S(1)}, f32[16]{0:T(128)S(1)}, u32[]{:S(2)}, u32[]{:S(2)}) collective-permute-start(f32[16]{0:T(128)S(1)} %maximum_maximum_fusion.1), channel_id=1, source_target_pairs={{4,0},{5,1},{6,2},{7,3},{8,4},{9,5},{10,6},{11,7},{12,8},{13,9},{1... | collective-permute-start | bytes 200 | tf_op jit(solution)/shard_map/ppermute | solution.py:43
  227.5 2.6 %collective-permute-done.41 = f32[16]{0:T(128)S(1)} collective-permute-done((f32[16]{0:T(128)S(1)}, f32[16]{0:T(128)S(1)}, u32[]{:S(2)}, u32[]{:S(2)}) %collective-permute-start.41) | collective-permute-done | bytes 96 | tf_op jit(solution)/shard_map/ppermute | solution.py:43
  230.1 15.8 %pmax.7 = f32[16]{0:T(128)} all-reduce(f32[16]{0:T(128)S(1)} %maximum_maximum_fusion), channel_id=1, replica_groups=mesh['req'=8,'hid'=16] {'req'}, use_global_device_ids=true, to_apply=%region_6.7 | all-reduce | flops 16 | bytes 128 | tf_op jit(solution)/shard_map/pmax | solution.py:595
  246.0 10.7 %finish.1 = bf16[2,480,384]{2,1,0:T(8,128)(2,1)} custom-call(bf16[2,480,384]{2,1,0:T(8,128)(2,1)S(1)} %copy-done, bf16[256,384]{1,0:T(8,128)(2,1)S(1)} %bitcast.25, bf16[10240,384]{1,0:T(8,128)(2,1)} %all-gather.8.cloned.1.call-done.a_hbm, bf16[8,16,48,384]{3,2,1,0:T(8,128)(2,1)} %bitcast.29, s32[2,480,1]{2,1,0:T(8,128)S(1)} %fusion.4.slot_ref), custom_call_target="tpu_custom_call" | custom-call | flops 3019898880 | bytes 14680064 | tf_op jit(solution)/shard_map/finish/pallas_call | solution.py:444
  (162 shorter events, 35.4 us)
Async XLA Ops:
  7.2 94.2 %all-gather.6.cloned.1.call-start = ((), (), s32[]{:S(2)}) async-start(), calls=%async_computation.2 | async-start | bytes 7798784 | tf_op jit(solution)/shard_map/all_gather | solution.py:521
  15.8 12.5 %collective-permute-start.7 = (bf16[192,384]{1,0:T(8,128)(2,1)S(1)}, bf16[192,384]{1,0:T(8,128)(2,1)}, u32[]{:S(2)}, u32[]{:S(2)}) collective-permute-start(bf16[192,384]{1,0:T(8,128)(2,1)S(1)} %get-tuple-element.40), channel_id=1, source_target_pairs={{12,0},{13,1},{14,2},{15,3},{0,4},{1,5},{2,6},{3,7},{4,8},{5,9},{6... | collective-permute-start | bytes 442376 | tf_op jit(solution)/shard_map/ppermute | solution.py:43
  17.9 19.5 %collective-permute-start.8 = (bf16[192,384]{1,0:T(8,128)(2,1)S(1)}, bf16[192,384]{1,0:T(8,128)(2,1)}, u32[]{:S(2)}, u32[]{:S(2)}) collective-permute-start(bf16[192,384]{1,0:T(8,128)(2,1)S(1)} %get-tuple-element.40), channel_id=1, source_target_pairs={{4,0},{5,1},{6,2},{7,3},{8,4},{9,5},{10,6},{11,7},{12,8},{13,9},{1... | collective-permute-start | bytes 442376 | tf_op jit(solution)/shard_map/ppermute | solution.py:43
  19.2 18.1 %collective-permute-start.9 = (bf16[192,384]{1,0:T(8,128)(2,1)S(1)}, bf16[192,384]{1,0:T(8,128)(2,1)}, u32[]{:S(2)}, u32[]{:S(2)}) collective-permute-start(bf16[192,384]{1,0:T(8,128)(2,1)S(1)} %get-tuple-element.40), channel_id=1, source_target_pairs={{8,0},{9,1},{10,2},{11,3},{12,4},{13,5},{14,6},{15,7},{0,8},{1,9},... | collective-permute-start | bytes 442376 | tf_op jit(solution)/shard_map/ppermute | solution.py:43
  20.9 20.4 %collective-permute-start = (bf16[192,384]{1,0:T(8,128)(2,1)S(1)}, bf16[192,384]{1,0:T(8,128)(2,1)}, u32[]{:S(2)}, u32[]{:S(2)}) collective-permute-start(bf16[192,384]{1,0:T(8,128)(2,1)S(1)} %get-tuple-element.41), channel_id=1, source_target_pairs={{3,0},{0,1},{1,2},{2,3},{7,4},{4,5},{5,6},{6,7},{11,8},{8,9},{9,10... | collective-permute-start | bytes 442376 | tf_op jit(solution)/shard_map/ppermute | solution.py:43
  22.5 18.7 %collective-permute-start.1 = (bf16[192,384]{1,0:T(8,128)(2,1)S(1)}, bf16[192,384]{1,0:T(8,128)(2,1)}, u32[]{:S(2)}, u32[]{:S(2)}) collective-permute-start(bf16[192,384]{1,0:T(8,128)(2,1)S(1)} %get-tuple-element.41), channel_id=1, source_target_pairs={{1,0},{2,1},{3,2},{0,3},{5,4},{6,5},{7,6},{4,7},{9,8},{10,9},{11,1... | collective-permute-start | bytes 442376 | tf_op jit(solution)/shard_map/ppermute | solution.py:43
  28.3 13.0 %collective-permute-start.2 = (bf16[192,384]{1,0:T(8,128)(2,1)S(1)}, bf16[192,384]{1,0:T(8,128)(2,1)}, u32[]{:S(2)}, u32[]{:S(2)}) collective-permute-start(bf16[192,384]{1,0:T(8,128)(2,1)S(1)} %get-tuple-element.41), channel_id=1, source_target_pairs={{2,0},{3,1},{0,2},{1,3},{6,4},{7,5},{4,6},{5,7},{10,8},{11,9},{8,1... | collective-permute-start | bytes 442376 | tf_op jit(solution)/shard_map/ppermute | solution.py:43
  38.5 33.5 %collective-permute-start.10 = (bf16[768,384]{1,0:T(8,128)(2,1)S(1)}, bf16[768,384]{1,0:T(8,128)(2,1)S(1)}, u32[]{:S(2)}, u32[]{:S(2)}) collective-permute-start(bf16[768,384]{1,0:T(8,128)(2,1)S(1)} %pad_maximum_fusion.1.refs_5_), channel_id=1, source_target_pairs={{3,0},{0,1},{1,2},{2,3},{7,4},{4,5},{5,6},{6,7},{11,8},{8,9},{9,10... | collective-permute-start | bytes 1769480 | tf_op jit(solution)/shard_map/ppermute | solution.py:43
  39.3 32.8 %collective-permute-start.11 = (bf16[768,384]{1,0:T(8,128)(2,1)S(1)}, bf16[768,384]{1,0:T(8,128)(2,1)S(1)}, u32[]{:S(2)}, u32[]{:S(2)}) collective-permute-start(bf16[768,384]{1,0:T(8,128)(2,1)S(1)} %pad_maximum_fusion.1.refs_5_), channel_id=1, source_target_pairs={{1,0},{2,1},{3,2},{0,3},{5,4},{6,5},{7,6},{4,7},{9,8},{10,9},{11,1... | collective-permute-start | bytes 1769480 | tf_op jit(solution)/shard_map/ppermute | solution.py:43
  42.4 32.5 %collective-permute-start.3 = (bf16[768,384]{1,0:T(8,128)(2,1)S(1)}, bf16[768,384]{1,0:T(8,128)(2,1)S(1)}, u32[]{:S(2)}, u32[]{:S(2)}) collective-permute-start(bf16[768,384]{1,0:T(8,128)(2,1)S(1)} %pad_maximum_fusion.refs_0_), channel_id=1, source_target_pairs={{12,0},{13,1},{14,2},{15,3},{0,4},{1,5},{2,6},{3,7},{4,8},{5,9},{6... | collective-permute-start | bytes 1769480 | tf_op jit(solution)/shard_map/ppermute | solution.py:43
  42.7 32.3 %collective-permute-start.4 = (bf16[768,384]{1,0:T(8,128)(2,1)S(1)}, bf16[768,384]{1,0:T(8,128)(2,1)S(1)}, u32[]{:S(2)}, u32[]{:S(2)}) collective-permute-start(bf16[768,384]{1,0:T(8,128)(2,1)S(1)} %pad_maximum_fusion.refs_0_), channel_id=1, source_target_pairs={{4,0},{5,1},{6,2},{7,3},{8,4},{9,5},{10,6},{11,7},{12,8},{13,9},{1... | collective-permute-start | bytes 1769480 | tf_op jit(solution)/shard_map/ppermute | solution.py:43
  72.0 15.4 %collective-permute-start.12 = (bf16[384,384]{1,0:T(8,128)(2,1)S(1)}, bf16[384,384]{1,0:T(8,128)(2,1)S(1)}, u32[]{:S(2)}, u32[]{:S(2)}) collective-permute-start(bf16[384,384]{1,0:T(8,128)(2,1)S(1)} %slice.93), channel_id=1, source_target_pairs={{3,0},{0,1},{1,2},{2,3},{7,4},{4,5},{5,6},{6,7},{11,8},{8,9},{9,10... | collective-permute-start | bytes 884744 | tf_op jit(solution)/shard_map/ppermute | solution.py:43
  72.2 15.3 %collective-permute-start.13 = (bf16[384,384]{1,0:T(8,128)(2,1)S(1)}, bf16[384,384]{1,0:T(8,128)(2,1)S(1)}, u32[]{:S(2)}, u32[]{:S(2)}) collective-permute-start(bf16[384,384]{1,0:T(8,128)(2,1)S(1)} %slice.94), channel_id=1, source_target_pairs={{1,0},{2,1},{3,2},{0,3},{5,4},{6,5},{7,6},{4,7},{9,8},{10,9},{11,1... | collective-permute-start | bytes 884744 | tf_op jit(solution)/shard_map/ppermute | solution.py:43
  74.9 15.2 %collective-permute-start.5 = (bf16[384,384]{1,0:T(8,128)(2,1)S(1)}, bf16[384,384]{1,0:T(8,128)(2,1)S(1)}, u32[]{:S(2)}, u32[]{:S(2)}) collective-permute-start(bf16[384,384]{1,0:T(8,128)(2,1)S(1)} %slice.89), channel_id=1, source_target_pairs={{12,0},{13,1},{14,2},{15,3},{0,4},{1,5},{2,6},{3,7},{4,8},{5,9},{6... | collective-permute-start | bytes 884744 | tf_op jit(solution)/shard_map/ppermute | solution.py:43
  75.0 15.1 %collective-permute-start.6 = (bf16[384,384]{1,0:T(8,128)(2,1)S(1)}, bf16[384,384]{1,0:T(8,128)(2,1)S(1)}, u32[]{:S(2)}, u32[]{:S(2)}) collective-permute-start(bf16[384,384]{1,0:T(8,128)(2,1)S(1)} %slice.90), channel_id=1, source_target_pairs={{4,0},{5,1},{6,2},{7,3},{8,4},{9,5},{10,6},{11,7},{12,8},{13,9},{1... | collective-permute-start | bytes 884744 | tf_op jit(solution)/shard_map/ppermute | solution.py:43
  97.0 16.8 %all-to-all-start = ((bf16[16,48,384]{2,1,0:T(8,128)(2,1)}), bf16[16,48,384]{2,1,0:T(8,128)(2,1)S(1)}, u32[]{:S(2)}, u32[]{:S(2)}) async-start(bf16[16,48,384]{2,1,0:T(8,128)(2,1)} %cut.1), calls=%async_computation | async-start | bytes 1179648 | tf_op jit(solution)/shard_map/all_to_all | solution.py:542
  101.2 144.7 %all-gather.10.cloned.1.call-start = ((), (), s32[]{:S(2)}) async-start(), calls=%async_computation.4 | async-start | bytes 5308416 | tf_op jit(solution)/shard_map/all_gather | solution.py:557
  102.2 43.2 %copy-start.10 = (f32[640,64]{1,0:T(8,128)S(1)}, f32[640,64]{1,0:T(8,128)}, u32[]{:S(2)}) copy-start(f32[640,64]{1,0:T(8,128)} %copy-done.9) | copy-start | bytes 491524
  129.3 116.6 %all-gather.8.cloned.1.call-start = ((), (), s32[]{:S(2)}) async-start(), calls=%async_computation.3 | async-start | bytes 8355840 | tf_op jit(solution)/shard_map/all_gather | solution.py:567
  129.4 7.4 %collective-permute-start.21 = (bf16[128,384]{1,0:T(8,128)(2,1)S(1)}, bf16[128,384]{1,0:T(8,128)(2,1)S(1)}, u32[]{:S(2)}, u32[]{:S(2)}) collective-permute-start(bf16[128,384]{1,0:T(8,128)(2,1)S(1)} %get-tuple-element.42), channel_id=1, source_target_pairs={{12,0},{13,1},{14,2},{15,3},{0,4},{1,5},{2,6},{3,7},{4,8},{5,9},{6... | collective-permute-start | bytes 294920 | tf_op jit(solution)/shard_map/ppermute | solution.py:43
  131.1 7.1 %collective-permute-start.22 = (bf16[128,384]{1,0:T(8,128)(2,1)S(1)}, bf16[128,384]{1,0:T(8,128)(2,1)S(1)}, u32[]{:S(2)}, u32[]{:S(2)}) collective-permute-start(bf16[128,384]{1,0:T(8,128)(2,1)S(1)} %get-tuple-element.42), channel_id=1, source_target_pairs={{4,0},{5,1},{6,2},{7,3},{8,4},{9,5},{10,6},{11,7},{12,8},{13,9},{1... | collective-permute-start | bytes 294920 | tf_op jit(solution)/shard_map/ppermute | solution.py:43
  132.4 5.8 %collective-permute-start.23 = (bf16[128,384]{1,0:T(8,128)(2,1)S(1)}, bf16[128,384]{1,0:T(8,128)(2,1)S(1)}, u32[]{:S(2)}, u32[]{:S(2)}) collective-permute-start(bf16[128,384]{1,0:T(8,128)(2,1)S(1)} %get-tuple-element.42), channel_id=1, source_target_pairs={{8,0},{9,1},{10,2},{11,3},{12,4},{13,5},{14,6},{15,7},{0,8},{1,9},... | collective-permute-start | bytes 294920 | tf_op jit(solution)/shard_map/ppermute | solution.py:43
  134.1 7.0 %collective-permute-start.14 = (bf16[128,384]{1,0:T(8,128)(2,1)S(1)}, bf16[128,384]{1,0:T(8,128)(2,1)S(1)}, u32[]{:S(2)}, u32[]{:S(2)}) collective-permute-start(bf16[128,384]{1,0:T(8,128)(2,1)S(1)} %get-tuple-element.43), channel_id=1, source_target_pairs={{3,0},{0,1},{1,2},{2,3},{7,4},{4,5},{5,6},{6,7},{11,8},{8,9},{9,10... | collective-permute-start | bytes 294920 | tf_op jit(solution)/shard_map/ppermute | solution.py:43
  135.3 5.8 %collective-permute-start.15 = (bf16[128,384]{1,0:T(8,128)(2,1)S(1)}, bf16[128,384]{1,0:T(8,128)(2,1)S(1)}, u32[]{:S(2)}, u32[]{:S(2)}) collective-permute-start(bf16[128,384]{1,0:T(8,128)(2,1)S(1)} %get-tuple-element.43), channel_id=1, source_target_pairs={{1,0},{2,1},{3,2},{0,3},{5,4},{6,5},{7,6},{4,7},{9,8},{10,9},{11,1... | collective-permute-start | bytes 294920 | tf_op jit(solution)/shard_map/ppermute | solution.py:43
  136.8 5.8 %collective-permute-start.16 = (bf16[128,384]{1,0:T(8,128)(2,1)S(1)}, bf16[128,384]{1,0:T(8,128)(2,1)S(1)}, u32[]{:S(2)}, u32[]{:S(2)}) collective-permute-start(bf16[128,384]{1,0:T(8,128)(2,1)S(1)} %get-tuple-element.43), channel_id=1, source_target_pairs={{2,0},{3,1},{0,2},{1,3},{6,4},{7,5},{4,6},{5,7},{10,8},{11,9},{8,1... | collective-permute-start | bytes 294920 | tf_op jit(solution)/shard_map/ppermute | solution.py:43
  138.3 11.8 %collective-permute-start.24 = (bf16[512,384]{1,0:T(8,128)(2,1)S(1)}, bf16[512,384]{1,0:T(8,128)(2,1)S(1)}, u32[]{:S(2)}, u32[]{:S(2)}) collective-permute-start(bf16[512,384]{1,0:T(8,128)(2,1)S(1)} %pad_maximum_fusion.3.refs_5_), channel_id=1, source_target_pairs={{3,0},{0,1},{1,2},{2,3},{7,4},{4,5},{5,6},{6,7},{11,8},{8,9},{9,10... | collective-permute-start | bytes 1179656 | tf_op jit(solution)/shard_map/ppermute | solution.py:43
  139.3 11.0 %collective-permute-start.25 = (bf16[512,384]{1,0:T(8,128)(2,1)S(1)}, bf16[512,384]{1,0:T(8,128)(2,1)S(1)}, u32[]{:S(2)}, u32[]{:S(2)}) collective-permute-start(bf16[512,384]{1,0:T(8,128)(2,1)S(1)} %pad_maximum_fusion.3.refs_5_), channel_id=1, source_target_pairs={{1,0},{2,1},{3,2},{0,3},{5,4},{6,5},{7,6},{4,7},{9,8},{10,9},{11,1... | collective-permute-start | bytes 1179656 | tf_op jit(solution)/shard_map/ppermute | solution.py:43
  142.7 10.4 %collective-permute-start.17 = (bf16[512,384]{1,0:T(8,128)(2,1)S(1)}, bf16[512,384]{1,0:T(8,128)(2,1)S(1)}, u32[]{:S(2)}, u32[]{:S(2)}) collective-permute-start(bf16[512,384]{1,0:T(8,128)(2,1)S(1)} %pad_maximum_fusion.2.refs_0_), channel_id=1, source_target_pairs={{12,0},{13,1},{14,2},{15,3},{0,4},{1,5},{2,6},{3,7},{4,8},{5,9},{6... | collective-permute-start | bytes 1179656 | tf_op jit(solution)/shard_map/ppermute | solution.py:43
  143.0 10.3 %collective-permute-start.18 = (bf16[512,384]{1,0:T(8,128)(2,1)S(1)}, bf16[512,384]{1,0:T(8,128)(2,1)S(1)}, u32[]{:S(2)}, u32[]{:S(2)}) collective-permute-start(bf16[512,384]{1,0:T(8,128)(2,1)S(1)} %pad_maximum_fusion.2.refs_0_), channel_id=1, source_target_pairs={{4,0},{5,1},{6,2},{7,3},{8,4},{9,5},{10,6},{11,7},{12,8},{13,9},{1... | collective-permute-start | bytes 1179656 | tf_op jit(solution)/shard_map/ppermute | solution.py:43
  150.2 6.3 %collective-permute-start.26 = (bf16[256,384]{1,0:T(8,128)(2,1)S(1)}, bf16[256,384]{1,0:T(8,128)(2,1)S(1)}, u32[]{:S(2)}, u32[]{:S(2)}) collective-permute-start(bf16[256,384]{1,0:T(8,128)(2,1)S(1)} %slice.101), channel_id=1, source_target_pairs={{3,0},{0,1},{1,2},{2,3},{7,4},{4,5},{5,6},{6,7},{11,8},{8,9},{9,10... | collective-permute-start | bytes 589832 | tf_op jit(solution)/shard_map/ppermute | solution.py:43
  150.3 6.2 %collective-permute-start.27 = (bf16[256,384]{1,0:T(8,128)(2,1)S(1)}, bf16[256,384]{1,0:T(8,128)(2,1)S(1)}, u32[]{:S(2)}, u32[]{:S(2)}) collective-permute-start(bf16[256,384]{1,0:T(8,128)(2,1)S(1)} %slice.102), channel_id=1, source_target_pairs={{1,0},{2,1},{3,2},{0,3},{5,4},{6,5},{7,6},{4,7},{9,8},{10,9},{11,1... | collective-permute-start | bytes 589832 | tf_op jit(solution)/shard_map/ppermute | solution.py:43
  153.0 6.2 %collective-permute-start.19 = (bf16[256,384]{1,0:T(8,128)(2,1)S(1)}, bf16[256,384]{1,0:T(8,128)(2,1)S(1)}, u32[]{:S(2)}, u32[]{:S(2)}) collective-permute-start(bf16[256,384]{1,0:T(8,128)(2,1)S(1)} %slice.99), channel_id=1, source_target_pairs={{12,0},{13,1},{14,2},{15,3},{0,4},{1,5},{2,6},{3,7},{4,8},{5,9},{6... | collective-permute-start | bytes 589832 | tf_op jit(solution)/shard_map/ppermute | solution.py:43
  153.4 5.9 %collective-permute-start.20 = (bf16[256,384]{1,0:T(8,128)(2,1)S(1)}, bf16[256,384]{1,0:T(8,128)(2,1)S(1)}, u32[]{:S(2)}, u32[]{:S(2)}) collective-permute-start(bf16[256,384]{1,0:T(8,128)(2,1)S(1)} %slice.100), channel_id=1, source_target_pairs={{4,0},{5,1},{6,2},{7,3},{8,4},{9,5},{10,6},{11,7},{12,8},{13,9},{1... | collective-permute-start | bytes 589832 | tf_op jit(solution)/shard_map/ppermute | solution.py:43
  156.2 7.8 %collective-permute-start.28 = (bf16[384,128]{1,0:T(8,128)(2,1)S(1)}, bf16[384,128]{1,0:T(8,128)(2,1)S(1)}, u32[]{:S(2)}, u32[]{:S(2)}) collective-permute-start(bf16[384,128]{1,0:T(8,128)(2,1)S(1)} %copy-done.6), channel_id=1, source_target_pairs={{0,1},{1,0},{2,3},{3,2},{4,5},{5,4},{6,7},{7,6},{8,9},{9,8},{10,11... | collective-permute-start | bytes 294920 | tf_op jit(solution)/shard_map/ppermute | solution.py:554
  163.8 3.2 %collective-permute-start.29 = (bf16[256,128]{1,0:T(8,128)(2,1)S(1)}, bf16[256,128]{1,0:T(8,128)(2,1)S(1)}, u32[]{:S(2)}, u32[]{:S(2)}) collective-permute-start(bf16[256,128]{1,0:T(8,128)(2,1)S(1)} %get-tuple-element.35.oi), channel_id=1, source_target_pairs={{0,1},{1,0},{2,3},{3,2},{4,5},{5,4},{6,7},{7,6},{8,9},{9,8},{10,11... | collective-permute-start | bytes 196616 | tf_op jit(solution)/shard_map/ppermute | solution.py:561
  177.9 68.1 %copy-start = (bf16[2,480,384]{2,1,0:T(8,128)(2,1)S(1)}, bf16[2,480,384]{2,1,0:T(8,128)(2,1)}, u32[]{:S(2)}) copy-start(bf16[2,480,384]{2,1,0:T(8,128)(2,1)} %text_ref.1) | copy-start | bytes 2211844
  177.9 4.6 %collective-permute-start.30 = (f32[2,6144]{1,0:T(2,128)S(1)}, f32[2,6144]{1,0:T(2,128)S(1)}, u32[]{:S(2)}, u32[]{:S(2)}) collective-permute-start(f32[2,6144]{1,0:T(2,128)S(1)} %convolution_add_fusion), channel_id=1, source_target_pairs={{2,0},{3,1},{0,2},{1,3},{6,4},{7,5},{4,6},{5,7},{10,8},{11,9},{8,1... | collective-permute-start | bytes 147464 | tf_op jit(solution)/shard_map/ppermute | solution.py:43
  178.0 4.7 %collective-permute-start.31 = (f32[2,6144]{1,0:T(2,128)S(1)}, f32[2,6144]{1,0:T(2,128)S(1)}, u32[]{:S(2)}, u32[]{:S(2)}) collective-permute-start(f32[2,6144]{1,0:T(2,128)S(1)} %convolution_add_fusion), channel_id=1, source_target_pairs={{3,0},{0,1},{1,2},{2,3},{7,4},{4,5},{5,6},{6,7},{11,8},{8,9},{9,10... | collective-permute-start | bytes 147464 | tf_op jit(solution)/shard_map/ppermute | solution.py:43
  178.5 4.2 %collective-permute-start.32 = (f32[2,6144]{1,0:T(2,128)S(1)}, f32[2,6144]{1,0:T(2,128)S(1)}, u32[]{:S(2)}, u32[]{:S(2)}) collective-permute-start(f32[2,6144]{1,0:T(2,128)S(1)} %convolution_add_fusion), channel_id=1, source_target_pairs={{1,0},{2,1},{3,2},{0,3},{5,4},{6,5},{7,6},{4,7},{9,8},{10,9},{11,1... | collective-permute-start | bytes 147464 | tf_op jit(solution)/shard_map/ppermute | solution.py:43
  182.7 4.8 %collective-permute-start.33 = (f32[2,6144]{1,0:T(2,128)S(1)}, f32[2,6144]{1,0:T(2,128)S(1)}, u32[]{:S(2)}, u32[]{:S(2)}) collective-permute-start(f32[2,6144]{1,0:T(2,128)S(1)} %add_add_fusion), channel_id=1, source_target_pairs={{8,0},{9,1},{10,2},{11,3},{12,4},{13,5},{14,6},{15,7},{0,8},{1,9},... | collective-permute-start | bytes 147464 | tf_op jit(solution)/shard_map/ppermute | solution.py:43
  184.6 4.4 %collective-permute-start.34 = (f32[2,6144]{1,0:T(2,128)S(1)}, f32[2,6144]{1,0:T(2,128)S(1)}, u32[]{:S(2)}, u32[]{:S(2)}) collective-permute-start(f32[2,6144]{1,0:T(2,128)S(1)} %add_add_fusion), channel_id=1, source_target_pairs={{12,0},{13,1},{14,2},{15,3},{0,4},{1,5},{2,6},{3,7},{4,8},{5,9},{6... | collective-permute-start | bytes 147464 | tf_op jit(solution)/shard_map/ppermute | solution.py:43
  186.2 4.2 %collective-permute-start.35 = (f32[2,6144]{1,0:T(2,128)S(1)}, f32[2,6144]{1,0:T(2,128)S(1)}, u32[]{:S(2)}, u32[]{:S(2)}) collective-permute-start(f32[2,6144]{1,0:T(2,128)S(1)} %add_add_fusion), channel_id=1, source_target_pairs={{4,0},{5,1},{6,2},{7,3},{8,4},{9,5},{10,6},{11,7},{12,8},{13,9},{1... | collective-permute-start | bytes 147464 | tf_op jit(solution)/shard_map/ppermute | solution.py:43
  216.1 4.6 %collective-permute-start.36 = (f32[16]{0:T(128)S(1)}, f32[16]{0:T(128)S(1)}, u32[]{:S(2)}, u32[]{:S(2)}) collective-permute-start(f32[16]{0:T(128)S(1)} %convolution_reduce_fusion), channel_id=1, source_target_pairs={{3,0},{0,1},{1,2},{2,3},{7,4},{4,5},{5,6},{6,7},{11,8},{8,9},{9,10... | collective-permute-start | bytes 200 | tf_op jit(solution)/shard_map/ppermute | solution.py:43
  216.2 4.6 %collective-permute-start.37 = (f32[16]{0:T(128)S(1)}, f32[16]{0:T(128)S(1)}, u32[]{:S(2)}, u32[]{:S(2)}) collective-permute-start(f32[16]{0:T(128)S(1)} %convolution_reduce_fusion), channel_id=1, source_target_pairs={{1,0},{2,1},{3,2},{0,3},{5,4},{6,5},{7,6},{4,7},{9,8},{10,9},{11,1... | collective-permute-start | bytes 200 | tf_op jit(solution)/shard_map/ppermute | solution.py:43
  219.5 4.0 %collective-permute-start.38 = (f32[16]{0:T(128)S(1)}, f32[16]{0:T(128)S(1)}, u32[]{:S(2)}, u32[]{:S(2)}) collective-permute-start(f32[16]{0:T(128)S(1)} %convolution_reduce_fusion), channel_id=1, source_target_pairs={{2,0},{3,1},{0,2},{1,3},{6,4},{7,5},{4,6},{5,7},{10,8},{11,9},{8,1... | collective-permute-start | bytes 200 | tf_op jit(solution)/shard_map/ppermute | solution.py:43
  223.5 4.0 %collective-permute-start.39 = (f32[16]{0:T(128)S(1)}, f32[16]{0:T(128)S(1)}, u32[]{:S(2)}, u32[]{:S(2)}) collective-permute-start(f32[16]{0:T(128)S(1)} %maximum_maximum_fusion.1), channel_id=1, source_target_pairs={{12,0},{13,1},{14,2},{15,3},{0,4},{1,5},{2,6},{3,7},{4,8},{5,9},{6... | collective-permute-start | bytes 200 | tf_op jit(solution)/shard_map/ppermute | solution.py:43
  223.5 4.0 %collective-permute-start.40 = (f32[16]{0:T(128)S(1)}, f32[16]{0:T(128)S(1)}, u32[]{:S(2)}, u32[]{:S(2)}) collective-permute-start(f32[16]{0:T(128)S(1)} %maximum_maximum_fusion.1), channel_id=1, source_target_pairs={{4,0},{5,1},{6,2},{7,3},{8,4},{9,5},{10,6},{11,7},{12,8},{13,9},{1... | collective-permute-start | bytes 200 | tf_op jit(solution)/shard_map/ppermute | solution.py:43
  226.2 4.0 %collective-permute-start.41 = (f32[16]{0:T(128)S(1)}, f32[16]{0:T(128)S(1)}, u32[]{:S(2)}, u32[]{:S(2)}) collective-permute-start(f32[16]{0:T(128)S(1)} %maximum_maximum_fusion.1), channel_id=1, source_target_pairs={{8,0},{9,1},{10,2},{11,3},{12,4},{13,5},{14,6},{15,7},{0,8},{1,9},... | collective-permute-start | bytes 200 | tf_op jit(solution)/shard_map/ppermute | solution.py:43
  (17 other events, 296.2 us)
Sparse Core Ops, SparseCore 0:
  11.5 83.7 all-gather.5
  129.5 34.6 all-gather.9
  173.8 71.6 all-gather.7

commit v5 on v4

--- a/solution.py
+++ b/solution.py
@@ -147,11 +147,11 @@
     )(tile_order, place, merged)
 
 
-def cut_kernel(row_ref, w_hbm, o_hbm, sem):
+def cut_kernel(row_ref, w_hbm, o_ref, sem):
     strip = FEAT // N_REQ
     rows = pl.ds(pl.multiple_of(row_ref[0], strip), strip)
     copies = [
-        pltpu.make_async_copy(w_hbm.at[rows, pl.ds(k * FEAT, FEAT)], o_hbm.at[k], sem.at[k])
+        pltpu.make_async_copy(w_hbm.at[rows, pl.ds(k * FEAT, FEAT)], o_ref.at[k], sem.at[k])
         for k in range(N_HID)
     ]
     for c in copies:
@@ -165,7 +165,7 @@
         cut_kernel,
         out_shape=jax.ShapeDtypeStruct((N_HID, FEAT // N_REQ, FEAT), BF),
         in_specs=[pl.BlockSpec(memory_space=pltpu.SMEM), pl.BlockSpec(memory_space=pl.ANY)],
-        out_specs=pl.BlockSpec(memory_space=pl.ANY),
+        out_specs=vmem(),
         scratch_shapes=[pltpu.SemaphoreType.DMA((N_HID,))],
         name="cut",
     )(row, in_hbm(weight))

time: 264 us -> 258 us (0.977)
  Pallas kernels: 59.7 us -> 42.6 us
  waiting for transfers between devices: 33.3 us -> 46 us
  blocking collectives: 52.4 us -> 48.5 us
    pallas_call x1, Pallas kernels: 19.1 us -> 2 us  [cut(): pl.pallas_call(cut_kernel, out_shape=jax.ShapeDtypeStruct((N_HID, FEAT //...]
    all_gather x1, waiting for transfers between devices: 0.02 us -> 11.2 us  [shards(): lax.all_gather(pack(merged, tile_order, (hid % RING)[None]), 'hid', axis=...]
    all_to_all x1, blocking collectives: 15.5 us -> 11.6 us  [shards(): lax.all_to_all(projected.reshape(N_REQ, TILE // N_REQ, FEAT), 'req', spli...]
  transfers between devices with their start and end apart: 46 -> 46, of which waited for: 14 -> 18; matrix products, arithmetic and copies ran while one was open for 14% -> 14% of each run, Pallas kernels for 18% -> 12%
where the time goes in v5:
time: 258 us; the launch traced here: 256 us
  starting transfers between devices  62.2 us (24%)
  blocking collectives  48.5 us (19%)
  waiting for transfers between devices  46 us (18%)
  Pallas kernels  42.6 us (17%)
  other arithmetic  19.6 us (8%)
  between operations  16.4 us (6%)
  local copies, waits for them, and re-layouts  11.9 us (5%)
  matrix products  9.21 us (4%)
    ppermute x40, starting transfers between devices, shift(): return lax.ppermute(block, 'hid', route)  56.8 us
    ppermute x40, waiting for transfers between devices, shift(): return lax.ppermute(block, 'hid', route)  31.7 us
    all_gather x1, blocking collectives, shards(): all_last = lax.all_gather(full_width, 'req', axis=0, tiled=True)  21.1 us
    pmax x1, blocking collectives, shards(): logit_max = lax.pmax(top, 'req')  15.8 us
    pallas_call x1, Pallas kernels, project(): pl.pallas_call(project_kernel, out_shape=jax.ShapeDtypeStruct((TILE, FEAT...  11.6 us
    all_to_all x1, blocking collectives, shards(): lax.all_to_all(projected.reshape(N_REQ, TILE // N_REQ, FEAT), 'req', spli...  11.6 us
    all_gather x1, waiting for transfers between devices, shards(): lax.all_gather(pack(merged, tile_order, (hid % RING)[None]), 'hid', axis=...  11.2 us
    pallas_call x1, Pallas kernels, finish(): pl.pallas_call(finish_kernel, out_shape=jax.ShapeDtypeStruct((REQ_GRP, LE...  10.7 us
  transfers between devices with their start and end apart: 46, of which 18 were waited for; matrix products, arithmetic and copies ran while one was open for 14% of the time, Pallas kernels for 12%

profile of v5, /device:TPU:1, one launch (start us, length us, event | category | flops | bytes accessed | tf_op | source)
XLA Modules:
  0.0 256.4 jit_solution(4300596668076773339)
XLA Ops:
  9.7 1.7 pack.1
  14.0 1.7 fusion.1
  15.8 2.1 collective-permute-start.7
  19.2 1.6 collective-permute-start.9
  20.9 1.6 collective-permute-start
  22.5 2.1 collective-permute-start.1
  24.7 1.8 copy.39
  26.5 1.8 copy.40
  29.7 7.7 %multiply_convert_fusion.refs_10_ = bf16[6144,512]{1,0:T(8,128)(2,1)} fusion(bf16[6144,64]{1,0:T(8,128)(2,1)S(1)} %copy.40, bf16[6144,64]{1,0:T(8,128)(2,1)S(1)} %copy.39, bf16[6144,384]{1,0:T(8,128)(2,1)} %param.23, f32[6144]{0:T(1024)S(1)} %convert_element_type.44), kind=kLoop, calls=%fused_computation | loop fusion | flops 25165824 | bytes 12607488 | tf_op jit(solution)/shard_map/convert_element_type | solution.py:530
  39.3 1.9 collective-permute-start.11
  42.7 2.4 collective-permute-start.4
  51.6 2.0 cut.1
  55.0 2.7 %collective-permute-start.13 = (bf16[384,384]{1,0:T(8,128)(2,1)S(1)}, bf16[384,384]{1,0:T(8,128)(2,1)S(1)}, u32[]{:S(2)}, u32[]{:S(2)}) collective-permute-start(bf16[384,384]{1,0:T(8,128)(2,1)S(1)} %slice.94), channel_id=1, source_target_pairs={{1,0},{2,1},{3,2},{0,3},{5,4},{6,5},{7,6},{4,7},{9,8},{10,9},{11,1... | collective-permute-start | bytes 884744 | tf_op jit(solution)/shard_map/ppermute | solution.py:43
  59.3 3.8 %collective-permute-start.6 = (bf16[384,384]{1,0:T(8,128)(2,1)S(1)}, bf16[384,384]{1,0:T(8,128)(2,1)S(1)}, u32[]{:S(2)}, u32[]{:S(2)}) collective-permute-start(bf16[384,384]{1,0:T(8,128)(2,1)S(1)} %slice.90), channel_id=1, source_target_pairs={{4,0},{5,1},{6,2},{7,3},{8,4},{9,5},{10,6},{11,7},{12,8},{13,9},{1... | collective-permute-start | bytes 884744 | tf_op jit(solution)/shard_map/ppermute | solution.py:43
  63.4 6.5 %collective-permute-done.12.refs_8_ = bf16[384,384]{1,0:T(8,128)(2,1)S(1)} collective-permute-done((bf16[384,384]{1,0:T(8,128)(2,1)S(1)}, bf16[384,384]{1,0:T(8,128)(2,1)S(1)}, u32[]{:S(2)}, u32[]{:S(2)}) %collective-permute-start.12) | collective-permute-done | bytes 294944 | tf_op jit(solution)/shard_map/ppermute | solution.py:43
  69.9 3.7 %collective-permute-done.5.refs_3_ = bf16[384,384]{1,0:T(8,128)(2,1)S(1)} collective-permute-done((bf16[384,384]{1,0:T(8,128)(2,1)S(1)}, bf16[384,384]{1,0:T(8,128)(2,1)S(1)}, u32[]{:S(2)}, u32[]{:S(2)}) %collective-permute-start.5) | collective-permute-done | bytes 294944 | tf_op jit(solution)/shard_map/ppermute | solution.py:43
  73.6 1.7 collective-permute-done.6.refs_4_
  75.4 5.5 %qkv_text.1 = (bf16[384,384]{1,0:T(8,128)(2,1)S(1)}, bf16[384,128]{1,0:T(8,128)(2,1)S(1)}) custom-call(s32[16]{0:T(128)S(1)} %fusion.22.src_ref, bf16[768,384]{1,0:T(8,128)(2,1)S(1)} %pad_maximum_fusion.refs_0_, bf16[768,384]{1,0:T(8,128)(2,1)S(1)} %collective-permute-done.3.refs_1_, bf16[768,384]{1,0:T(8,128)(2,1)S(1)} %collective-permute-done.4.refs_2_, ...), custom_call_target="tpu_custom_call" | custom-call | flops 2415919104 | bytes 12582912 | tf_op jit(solution)/shard_map/qkv_text/pallas_call | solution.py:323
  82.2 4.9 %all-to-all-start = ((bf16[16,48,384]{2,1,0:T(8,128)(2,1)}), bf16[16,48,384]{2,1,0:T(8,128)(2,1)S(1)}, u32[]{:S(2)}, u32[]{:S(2)}) async-start(bf16[16,48,384]{2,1,0:T(8,128)(2,1)} %cut.1), calls=%async_computation | async-start | bytes 1179648 | tf_op jit(solution)/shard_map/all_to_all | solution.py:542
  87.2 11.2 %all-gather.6.cloned.1.call-done.x_hbm = bf16[4096,896]{1,0:T(8,128)(2,1)} async-done(((bf16[256,896]{1,0:T(8,128)(2,1)}), bf16[4096,896]{1,0:T(8,128)(2,1)}) %all-gather.6.cloned.1.call-update) | async-done | bytes 7340048 | tf_op jit(solution)/shard_map/all_gather | solution.py:521
  99.3 11.6 %project.1 = bf16[256,384]{1,0:T(8,128)(2,1)S(1)} custom-call(bf16[4096,896]{1,0:T(8,128)(2,1)} %all-gather.6.cloned.1.call-done.x_hbm, bf16[16,800,384]{2,1,0:T(8,128)(2,1)} %bitcast.28, f32[2,16,768]{2,1,0:T(8,128)S(1)} %copy-done.2, f32[2,4,1,128]{3,2,1,0:T(1,128)S(1)} %reshape.305.left_ref, f32[1,384]{1,0:T(1,128)S(1)} %broadcast_in_dim.112.pb_ref), custom_call_target="tpu_custom_call" | custom-call | flops 2516582400 | bytes 17825792 | tf_op jit(solution)/shard_map/project/pallas_call | solution.py:247
  110.9 11.6 %all_to_all.10 = bf16[8,32,384]{2,1,0:T(8,128)(2,1)S(1)} all-to-all(bf16[8,32,384]{2,1,0:T(8,128)(2,1)S(1)} %bitcast.26), channel_id=1, replica_groups=mesh['req'=8,'hid'=16] {'req'}, dimensions={0} | all-to-all | bytes 393216 | tf_op jit(solution)/shard_map/all_to_all | solution.py:551
  122.6 1.7 collective-permute-start.21
  125.6 1.7 collective-permute-start.23
  128.5 1.5 collective-permute-start.15
  132.5 1.8 collective-permute-start.25
  134.2 1.6 collective-permute-done.16
  136.2 2.4 collective-permute-start.18
  140.9 2.4 collective-permute-done.24.refs_6_
  143.5 2.7 %collective-permute-start.27 = (bf16[256,384]{1,0:T(8,128)(2,1)S(1)}, bf16[256,384]{1,0:T(8,128)(2,1)S(1)}, u32[]{:S(2)}, u32[]{:S(2)}) collective-permute-start(bf16[256,384]{1,0:T(8,128)(2,1)S(1)} %slice.102), channel_id=1, source_target_pairs={{1,0},{2,1},{3,2},{0,3},{5,4},{6,5},{7,6},{4,7},{9,8},{10,9},{11,1... | collective-permute-start | bytes 589832 | tf_op jit(solution)/shard_map/ppermute | solution.py:43
  146.6 2.5 collective-permute-start.20
  149.7 2.7 %collective-permute-done.19.refs_3_ = bf16[256,384]{1,0:T(8,128)(2,1)S(1)} collective-permute-done((bf16[256,384]{1,0:T(8,128)(2,1)S(1)}, bf16[256,384]{1,0:T(8,128)(2,1)S(1)}, u32[]{:S(2)}, u32[]{:S(2)}) %collective-permute-start.19) | collective-permute-done | bytes 196640 | tf_op jit(solution)/shard_map/ppermute | solution.py:43
  152.4 4.5 %qkv_tile.1 = (bf16[256,384]{1,0:T(8,128)(2,1)S(1)}, bf16[256,128]{1,0:T(8,128)(2,1)S(1)}) custom-call(s32[16]{0:T(128)S(1)} %fusion.22.src_ref, bf16[512,384]{1,0:T(8,128)(2,1)S(1)} %pad_maximum_fusion.2.refs_0_, bf16[512,384]{1,0:T(8,128)(2,1)S(1)} %collective-permute-done.17.refs_1_, bf16[512,384]{1,0:T(8,128)(2,1)S(1)} %collective-permute-done.18.refs_2_, ...), custom_call_target="tpu_custom_call" | custom-call | flops 1610612736 | bytes 12582912 | tf_op jit(solution)/shard_map/qkv_tile/pallas_call | solution.py:323
  157.1 3.0 %collective-permute-done.29.pi = bf16[256,128]{1,0:T(8,128)(2,1)S(1)} collective-permute-done((bf16[256,128]{1,0:T(8,128)(2,1)S(1)}, bf16[256,128]{1,0:T(8,128)(2,1)S(1)}, u32[]{:S(2)}, u32[]{:S(2)}) %collective-permute-start.29) | collective-permute-done | bytes 65568 | tf_op jit(solution)/shard_map/ppermute | solution.py:561
  160.2 6.6 %attend.1 = bf16[640,384]{1,0:T(8,128)(2,1)} custom-call(s32[1]{0:T(128)} %bitcast.7.low_ref, bf16[384,384]{1,0:T(8,128)(2,1)S(1)} %copy-done.4, bf16[256,384]{1,0:T(8,128)(2,1)S(1)} %get-tuple-element.33.qi, bf16[384,128]{1,0:T(8,128)(2,1)S(1)} %copy-done.6, bf16[384,128]{1,0:T(8,128)(2,1)S(1)} %collective-permute-done.28.pt, ...), custom_call_target="tpu_custom_call" | custom-call | flops 1073741824 | bytes 2097152 | tf_op jit(solution)/shard_map/attend/pallas_call | solution.py:385
  167.6 3.4 %convolution_add_fusion = f32[2,6144]{1,0:T(2,128)S(1)} fusion(bf16[384,6144]{1,0:T(8,128)(2,1)} %w_hbm.1, bf16[640,384]{1,0:T(8,128)(2,1)} %attend.1, f32[2,6144]{1,0:T(2,128)S(1)} %bitcast.30, pred[6144]{0:T(1024)(128)(4,1)S(1)} %broadcast_in_dim.123, s32[2]{0:T(128)S(1)} %fusion.15), kind=kOutput, calls=%fused_computation.1 | convolution fusion | flops 10446848 | bytes 5314568 | tf_op jit(solution)/shard_map/dot_general | solution.py:573
  171.7 2.2 collective-permute-start.32
  174.1 1.6 collective-permute-done.30
  175.9 1.8 collective-permute-start.33
  177.8 1.6 collective-permute-start.34
  183.7 21.1 %all-gather.1 = bf16[8,2,6144]{2,1,0:T(2,128)(2,1)S(1)} all-gather(bf16[1,2,6144]{2,1,0:T(2,128)(2,1)S(1)} %fusion.12), channel_id=1, replica_groups=mesh['req'=8,'hid'=16] {'req'}, dimensions={0}, use_global_device_ids=true | all-gather | bytes 221184 | tf_op jit(solution)/shard_map/all_gather | solution.py:581
  205.5 3.8 %convolution_reduce_fusion = f32[16]{0:T(128)S(1)} fusion(bf16[384,6144]{1,0:T(8,128)(2,1)} %param.28, f32[16,6144]{1,0:T(8,128)S(1)} %reshape.313, f32[6144]{0:T(1024)S(1)} %convert_element_type.50, f32[16]{0:T(128)S(1)} %get-tuple-element.47), kind=kOutput, calls=%fused_computation.6 | convolution fusion | flops 75798512 | bytes 5136512 | tf_op jit(solution)/shard_map/dot_general | solution.py:588
  209.4 3.3 %collective-permute-start.37 = (f32[16]{0:T(128)S(1)}, f32[16]{0:T(128)S(1)}, u32[]{:S(2)}, u32[]{:S(2)}) collective-permute-start(f32[16]{0:T(128)S(1)} %convolution_reduce_fusion), channel_id=1, source_target_pairs={{1,0},{2,1},{3,2},{0,3},{5,4},{6,5},{7,6},{4,7},{9,8},{10,9},{11,1... | collective-permute-start | bytes 200 | tf_op jit(solution)/shard_map/ppermute | solution.py:43
  213.9 2.7 %collective-permute-done.38 = f32[16]{0:T(128)S(1)} collective-permute-done((f32[16]{0:T(128)S(1)}, f32[16]{0:T(128)S(1)}, u32[]{:S(2)}, u32[]{:S(2)}) %collective-permute-start.38) | collective-permute-done | bytes 96 | tf_op jit(solution)/shard_map/ppermute | solution.py:43
  216.7 2.7 %collective-permute-start.40 = (f32[16]{0:T(128)S(1)}, f32[16]{0:T(128)S(1)}, u32[]{:S(2)}, u32[]{:S(2)}) collective-permute-start(f32[16]{0:T(128)S(1)} %maximum_maximum_fusion.1), channel_id=1, source_target_pairs={{4,0},{5,1},{6,2},{7,3},{8,4},{9,5},{10,6},{11,7},{12,8},{13,9},{1... | collective-permute-start | bytes 200 | tf_op jit(solution)/shard_map/ppermute | solution.py:43
  220.7 2.6 %collective-permute-done.41 = f32[16]{0:T(128)S(1)} collective-permute-done((f32[16]{0:T(128)S(1)}, f32[16]{0:T(128)S(1)}, u32[]{:S(2)}, u32[]{:S(2)}) %collective-permute-start.41) | collective-permute-done | bytes 96 | tf_op jit(solution)/shard_map/ppermute | solution.py:43
  223.3 15.8 %pmax.7 = f32[16]{0:T(128)} all-reduce(f32[16]{0:T(128)S(1)} %maximum_maximum_fusion), channel_id=1, replica_groups=mesh['req'=8,'hid'=16] {'req'}, use_global_device_ids=true, to_apply=%region_6.7 | all-reduce | flops 16 | bytes 128 | tf_op jit(solution)/shard_map/pmax | solution.py:595
  239.1 10.7 %finish.1 = bf16[2,480,384]{2,1,0:T(8,128)(2,1)} custom-call(bf16[2,480,384]{2,1,0:T(8,128)(2,1)S(1)} %copy-done, bf16[256,384]{1,0:T(8,128)(2,1)S(1)} %bitcast.25, bf16[10240,384]{1,0:T(8,128)(2,1)} %all-gather.8.cloned.1.call-done.a_hbm, bf16[8,16,48,384]{3,2,1,0:T(8,128)(2,1)} %bitcast.29, s32[2,480,1]{2,1,0:T(8,128)S(1)} %fusion.4.slot_ref), custom_call_target="tpu_custom_call" | custom-call | flops 3019898880 | bytes 14680064 | tf_op jit(solution)/shard_map/finish/pallas_call | solution.py:444
  (162 shorter events, 39.8 us)
Async XLA Ops:
  7.2 91.3 %all-gather.6.cloned.1.call-start = ((), (), s32[]{:S(2)}) async-start(), calls=%async_computation.2 | async-start | bytes 7798784 | tf_op jit(solution)/shard_map/all_gather | solution.py:521
  15.8 12.5 %collective-permute-start.7 = (bf16[192,384]{1,0:T(8,128)(2,1)S(1)}, bf16[192,384]{1,0:T(8,128)(2,1)}, u32[]{:S(2)}, u32[]{:S(2)}) collective-permute-start(bf16[192,384]{1,0:T(8,128)(2,1)S(1)} %get-tuple-element.40), channel_id=1, source_target_pairs={{12,0},{13,1},{14,2},{15,3},{0,4},{1,5},{2,6},{3,7},{4,8},{5,9},{6... | collective-permute-start | bytes 442376 | tf_op jit(solution)/shard_map/ppermute | solution.py:43
  17.9 19.5 %collective-permute-start.8 = (bf16[192,384]{1,0:T(8,128)(2,1)S(1)}, bf16[192,384]{1,0:T(8,128)(2,1)}, u32[]{:S(2)}, u32[]{:S(2)}) collective-permute-start(bf16[192,384]{1,0:T(8,128)(2,1)S(1)} %get-tuple-element.40), channel_id=1, source_target_pairs={{4,0},{5,1},{6,2},{7,3},{8,4},{9,5},{10,6},{11,7},{12,8},{13,9},{1... | collective-permute-start | bytes 442376 | tf_op jit(solution)/shard_map/ppermute | solution.py:43
  19.2 18.1 %collective-permute-start.9 = (bf16[192,384]{1,0:T(8,128)(2,1)S(1)}, bf16[192,384]{1,0:T(8,128)(2,1)}, u32[]{:S(2)}, u32[]{:S(2)}) collective-permute-start(bf16[192,384]{1,0:T(8,128)(2,1)S(1)} %get-tuple-element.40), channel_id=1, source_target_pairs={{8,0},{9,1},{10,2},{11,3},{12,4},{13,5},{14,6},{15,7},{0,8},{1,9},... | collective-permute-start | bytes 442376 | tf_op jit(solution)/shard_map/ppermute | solution.py:43
  20.9 20.4 %collective-permute-start = (bf16[192,384]{1,0:T(8,128)(2,1)S(1)}, bf16[192,384]{1,0:T(8,128)(2,1)}, u32[]{:S(2)}, u32[]{:S(2)}) collective-permute-start(bf16[192,384]{1,0:T(8,128)(2,1)S(1)} %get-tuple-element.41), channel_id=1, source_target_pairs={{3,0},{0,1},{1,2},{2,3},{7,4},{4,5},{5,6},{6,7},{11,8},{8,9},{9,10... | collective-permute-start | bytes 442376 | tf_op jit(solution)/shard_map/ppermute | solution.py:43
  22.5 18.7 %collective-permute-start.1 = (bf16[192,384]{1,0:T(8,128)(2,1)S(1)}, bf16[192,384]{1,0:T(8,128)(2,1)}, u32[]{:S(2)}, u32[]{:S(2)}) collective-permute-start(bf16[192,384]{1,0:T(8,128)(2,1)S(1)} %get-tuple-element.41), channel_id=1, source_target_pairs={{1,0},{2,1},{3,2},{0,3},{5,4},{6,5},{7,6},{4,7},{9,8},{10,9},{11,1... | collective-permute-start | bytes 442376 | tf_op jit(solution)/shard_map/ppermute | solution.py:43
  28.3 13.0 %collective-permute-start.2 = (bf16[192,384]{1,0:T(8,128)(2,1)S(1)}, bf16[192,384]{1,0:T(8,128)(2,1)}, u32[]{:S(2)}, u32[]{:S(2)}) collective-permute-start(bf16[192,384]{1,0:T(8,128)(2,1)S(1)} %get-tuple-element.41), channel_id=1, source_target_pairs={{2,0},{3,1},{0,2},{1,3},{6,4},{7,5},{4,6},{5,7},{10,8},{11,9},{8,1... | collective-permute-start | bytes 442376 | tf_op jit(solution)/shard_map/ppermute | solution.py:43
  38.5 16.3 %collective-permute-start.10 = (bf16[768,384]{1,0:T(8,128)(2,1)S(1)}, bf16[768,384]{1,0:T(8,128)(2,1)S(1)}, u32[]{:S(2)}, u32[]{:S(2)}) collective-permute-start(bf16[768,384]{1,0:T(8,128)(2,1)S(1)} %pad_maximum_fusion.1.refs_5_), channel_id=1, source_target_pairs={{3,0},{0,1},{1,2},{2,3},{7,4},{4,5},{5,6},{6,7},{11,8},{8,9},{9,10... | collective-permute-start | bytes 1769480 | tf_op jit(solution)/shard_map/ppermute | solution.py:43
  39.3 15.7 %collective-permute-start.11 = (bf16[768,384]{1,0:T(8,128)(2,1)S(1)}, bf16[768,384]{1,0:T(8,128)(2,1)S(1)}, u32[]{:S(2)}, u32[]{:S(2)}) collective-permute-start(bf16[768,384]{1,0:T(8,128)(2,1)S(1)} %pad_maximum_fusion.1.refs_5_), channel_id=1, source_target_pairs={{1,0},{2,1},{3,2},{0,3},{5,4},{6,5},{7,6},{4,7},{9,8},{10,9},{11,1... | collective-permute-start | bytes 1769480 | tf_op jit(solution)/shard_map/ppermute | solution.py:43
  42.4 15.6 %collective-permute-start.3 = (bf16[768,384]{1,0:T(8,128)(2,1)S(1)}, bf16[768,384]{1,0:T(8,128)(2,1)S(1)}, u32[]{:S(2)}, u32[]{:S(2)}) collective-permute-start(bf16[768,384]{1,0:T(8,128)(2,1)S(1)} %pad_maximum_fusion.refs_0_), channel_id=1, source_target_pairs={{12,0},{13,1},{14,2},{15,3},{0,4},{1,5},{2,6},{3,7},{4,8},{5,9},{6... | collective-permute-start | bytes 1769480 | tf_op jit(solution)/shard_map/ppermute | solution.py:43
  42.7 16.6 %collective-permute-start.4 = (bf16[768,384]{1,0:T(8,128)(2,1)S(1)}, bf16[768,384]{1,0:T(8,128)(2,1)S(1)}, u32[]{:S(2)}, u32[]{:S(2)}) collective-permute-start(bf16[768,384]{1,0:T(8,128)(2,1)S(1)} %pad_maximum_fusion.refs_0_), channel_id=1, source_target_pairs={{4,0},{5,1},{6,2},{7,3},{8,4},{9,5},{10,6},{11,7},{12,8},{13,9},{1... | collective-permute-start | bytes 1769480 | tf_op jit(solution)/shard_map/ppermute | solution.py:43
  54.9 15.0 %collective-permute-start.12 = (bf16[384,384]{1,0:T(8,128)(2,1)S(1)}, bf16[384,384]{1,0:T(8,128)(2,1)S(1)}, u32[]{:S(2)}, u32[]{:S(2)}) collective-permute-start(bf16[384,384]{1,0:T(8,128)(2,1)S(1)} %slice.93), channel_id=1, source_target_pairs={{3,0},{0,1},{1,2},{2,3},{7,4},{4,5},{5,6},{6,7},{11,8},{8,9},{9,10... | collective-permute-start | bytes 884744 | tf_op jit(solution)/shard_map/ppermute | solution.py:43
  55.0 14.9 %collective-permute-start.13 = (bf16[384,384]{1,0:T(8,128)(2,1)S(1)}, bf16[384,384]{1,0:T(8,128)(2,1)S(1)}, u32[]{:S(2)}, u32[]{:S(2)}) collective-permute-start(bf16[384,384]{1,0:T(8,128)(2,1)S(1)} %slice.94), channel_id=1, source_target_pairs={{1,0},{2,1},{3,2},{0,3},{5,4},{6,5},{7,6},{4,7},{9,8},{10,9},{11,1... | collective-permute-start | bytes 884744 | tf_op jit(solution)/shard_map/ppermute | solution.py:43
  58.0 15.6 %collective-permute-start.5 = (bf16[384,384]{1,0:T(8,128)(2,1)S(1)}, bf16[384,384]{1,0:T(8,128)(2,1)S(1)}, u32[]{:S(2)}, u32[]{:S(2)}) collective-permute-start(bf16[384,384]{1,0:T(8,128)(2,1)S(1)} %slice.89), channel_id=1, source_target_pairs={{12,0},{13,1},{14,2},{15,3},{0,4},{1,5},{2,6},{3,7},{4,8},{5,9},{6... | collective-permute-start | bytes 884744 | tf_op jit(solution)/shard_map/ppermute | solution.py:43
  59.3 16.0 %collective-permute-start.6 = (bf16[384,384]{1,0:T(8,128)(2,1)S(1)}, bf16[384,384]{1,0:T(8,128)(2,1)S(1)}, u32[]{:S(2)}, u32[]{:S(2)}) collective-permute-start(bf16[384,384]{1,0:T(8,128)(2,1)S(1)} %slice.90), channel_id=1, source_target_pairs={{4,0},{5,1},{6,2},{7,3},{8,4},{9,5},{10,6},{11,7},{12,8},{13,9},{1... | collective-permute-start | bytes 884744 | tf_op jit(solution)/shard_map/ppermute | solution.py:43
  82.2 28.7 %all-to-all-start = ((bf16[16,48,384]{2,1,0:T(8,128)(2,1)}), bf16[16,48,384]{2,1,0:T(8,128)(2,1)S(1)}, u32[]{:S(2)}, u32[]{:S(2)}) async-start(bf16[16,48,384]{2,1,0:T(8,128)(2,1)} %cut.1), calls=%async_computation | async-start | bytes 1179648 | tf_op jit(solution)/shard_map/all_to_all | solution.py:542
  87.1 152.0 %all-gather.10.cloned.1.call-start = ((), (), s32[]{:S(2)}) async-start(), calls=%async_computation.4 | async-start | bytes 5308416 | tf_op jit(solution)/shard_map/all_gather | solution.py:557
  99.3 39.3 %copy-start.10 = (f32[640,64]{1,0:T(8,128)S(1)}, f32[640,64]{1,0:T(8,128)}, u32[]{:S(2)}) copy-start(f32[640,64]{1,0:T(8,128)} %copy-done.9) | copy-start | bytes 491524
  122.5 116.6 %all-gather.8.cloned.1.call-start = ((), (), s32[]{:S(2)}) async-start(), calls=%async_computation.3 | async-start | bytes 8355840 | tf_op jit(solution)/shard_map/all_gather | solution.py:567
  122.6 7.4 %collective-permute-start.21 = (bf16[128,384]{1,0:T(8,128)(2,1)S(1)}, bf16[128,384]{1,0:T(8,128)(2,1)S(1)}, u32[]{:S(2)}, u32[]{:S(2)}) collective-permute-start(bf16[128,384]{1,0:T(8,128)(2,1)S(1)} %get-tuple-element.42), channel_id=1, source_target_pairs={{12,0},{13,1},{14,2},{15,3},{0,4},{1,5},{2,6},{3,7},{4,8},{5,9},{6... | collective-permute-start | bytes 294920 | tf_op jit(solution)/shard_map/ppermute | solution.py:43
  124.3 7.1 %collective-permute-start.22 = (bf16[128,384]{1,0:T(8,128)(2,1)S(1)}, bf16[128,384]{1,0:T(8,128)(2,1)S(1)}, u32[]{:S(2)}, u32[]{:S(2)}) collective-permute-start(bf16[128,384]{1,0:T(8,128)(2,1)S(1)} %get-tuple-element.42), channel_id=1, source_target_pairs={{4,0},{5,1},{6,2},{7,3},{8,4},{9,5},{10,6},{11,7},{12,8},{13,9},{1... | collective-permute-start | bytes 294920 | tf_op jit(solution)/shard_map/ppermute | solution.py:43
  125.6 5.8 %collective-permute-start.23 = (bf16[128,384]{1,0:T(8,128)(2,1)S(1)}, bf16[128,384]{1,0:T(8,128)(2,1)S(1)}, u32[]{:S(2)}, u32[]{:S(2)}) collective-permute-start(bf16[128,384]{1,0:T(8,128)(2,1)S(1)} %get-tuple-element.42), channel_id=1, source_target_pairs={{8,0},{9,1},{10,2},{11,3},{12,4},{13,5},{14,6},{15,7},{0,8},{1,9},... | collective-permute-start | bytes 294920 | tf_op jit(solution)/shard_map/ppermute | solution.py:43
  127.3 7.0 %collective-permute-start.14 = (bf16[128,384]{1,0:T(8,128)(2,1)S(1)}, bf16[128,384]{1,0:T(8,128)(2,1)S(1)}, u32[]{:S(2)}, u32[]{:S(2)}) collective-permute-start(bf16[128,384]{1,0:T(8,128)(2,1)S(1)} %get-tuple-element.43), channel_id=1, source_target_pairs={{3,0},{0,1},{1,2},{2,3},{7,4},{4,5},{5,6},{6,7},{11,8},{8,9},{9,10... | collective-permute-start | bytes 294920 | tf_op jit(solution)/shard_map/ppermute | solution.py:43
  128.5 5.8 %collective-permute-start.15 = (bf16[128,384]{1,0:T(8,128)(2,1)S(1)}, bf16[128,384]{1,0:T(8,128)(2,1)S(1)}, u32[]{:S(2)}, u32[]{:S(2)}) collective-permute-start(bf16[128,384]{1,0:T(8,128)(2,1)S(1)} %get-tuple-element.43), channel_id=1, source_target_pairs={{1,0},{2,1},{3,2},{0,3},{5,4},{6,5},{7,6},{4,7},{9,8},{10,9},{11,1... | collective-permute-start | bytes 294920 | tf_op jit(solution)/shard_map/ppermute | solution.py:43
  130.0 5.8 %collective-permute-start.16 = (bf16[128,384]{1,0:T(8,128)(2,1)S(1)}, bf16[128,384]{1,0:T(8,128)(2,1)S(1)}, u32[]{:S(2)}, u32[]{:S(2)}) collective-permute-start(bf16[128,384]{1,0:T(8,128)(2,1)S(1)} %get-tuple-element.43), channel_id=1, source_target_pairs={{2,0},{3,1},{0,2},{1,3},{6,4},{7,5},{4,6},{5,7},{10,8},{11,9},{8,1... | collective-permute-start | bytes 294920 | tf_op jit(solution)/shard_map/ppermute | solution.py:43
  131.5 11.8 %collective-permute-start.24 = (bf16[512,384]{1,0:T(8,128)(2,1)S(1)}, bf16[512,384]{1,0:T(8,128)(2,1)S(1)}, u32[]{:S(2)}, u32[]{:S(2)}) collective-permute-start(bf16[512,384]{1,0:T(8,128)(2,1)S(1)} %pad_maximum_fusion.3.refs_5_), channel_id=1, source_target_pairs={{3,0},{0,1},{1,2},{2,3},{7,4},{4,5},{5,6},{6,7},{11,8},{8,9},{9,10... | collective-permute-start | bytes 1179656 | tf_op jit(solution)/shard_map/ppermute | solution.py:43
  132.5 11.0 %collective-permute-start.25 = (bf16[512,384]{1,0:T(8,128)(2,1)S(1)}, bf16[512,384]{1,0:T(8,128)(2,1)S(1)}, u32[]{:S(2)}, u32[]{:S(2)}) collective-permute-start(bf16[512,384]{1,0:T(8,128)(2,1)S(1)} %pad_maximum_fusion.3.refs_5_), channel_id=1, source_target_pairs={{1,0},{2,1},{3,2},{0,3},{5,4},{6,5},{7,6},{4,7},{9,8},{10,9},{11,1... | collective-permute-start | bytes 1179656 | tf_op jit(solution)/shard_map/ppermute | solution.py:43
  135.8 10.3 %collective-permute-start.17 = (bf16[512,384]{1,0:T(8,128)(2,1)S(1)}, bf16[512,384]{1,0:T(8,128)(2,1)S(1)}, u32[]{:S(2)}, u32[]{:S(2)}) collective-permute-start(bf16[512,384]{1,0:T(8,128)(2,1)S(1)} %pad_maximum_fusion.2.refs_0_), channel_id=1, source_target_pairs={{12,0},{13,1},{14,2},{15,3},{0,4},{1,5},{2,6},{3,7},{4,8},{5,9},{6... | collective-permute-start | bytes 1179656 | tf_op jit(solution)/shard_map/ppermute | solution.py:43
  136.2 10.3 %collective-permute-start.18 = (bf16[512,384]{1,0:T(8,128)(2,1)S(1)}, bf16[512,384]{1,0:T(8,128)(2,1)S(1)}, u32[]{:S(2)}, u32[]{:S(2)}) collective-permute-start(bf16[512,384]{1,0:T(8,128)(2,1)S(1)} %pad_maximum_fusion.2.refs_0_), channel_id=1, source_target_pairs={{4,0},{5,1},{6,2},{7,3},{8,4},{9,5},{10,6},{11,7},{12,8},{13,9},{1... | collective-permute-start | bytes 1179656 | tf_op jit(solution)/shard_map/ppermute | solution.py:43
  143.3 6.3 %collective-permute-start.26 = (bf16[256,384]{1,0:T(8,128)(2,1)S(1)}, bf16[256,384]{1,0:T(8,128)(2,1)S(1)}, u32[]{:S(2)}, u32[]{:S(2)}) collective-permute-start(bf16[256,384]{1,0:T(8,128)(2,1)S(1)} %slice.101), channel_id=1, source_target_pairs={{3,0},{0,1},{1,2},{2,3},{7,4},{4,5},{5,6},{6,7},{11,8},{8,9},{9,10... | collective-permute-start | bytes 589832 | tf_op jit(solution)/shard_map/ppermute | solution.py:43
  143.5 6.2 %collective-permute-start.27 = (bf16[256,384]{1,0:T(8,128)(2,1)S(1)}, bf16[256,384]{1,0:T(8,128)(2,1)S(1)}, u32[]{:S(2)}, u32[]{:S(2)}) collective-permute-start(bf16[256,384]{1,0:T(8,128)(2,1)S(1)} %slice.102), channel_id=1, source_target_pairs={{1,0},{2,1},{3,2},{0,3},{5,4},{6,5},{7,6},{4,7},{9,8},{10,9},{11,1... | collective-permute-start | bytes 589832 | tf_op jit(solution)/shard_map/ppermute | solution.py:43
  146.2 6.2 %collective-permute-start.19 = (bf16[256,384]{1,0:T(8,128)(2,1)S(1)}, bf16[256,384]{1,0:T(8,128)(2,1)S(1)}, u32[]{:S(2)}, u32[]{:S(2)}) collective-permute-start(bf16[256,384]{1,0:T(8,128)(2,1)S(1)} %slice.99), channel_id=1, source_target_pairs={{12,0},{13,1},{14,2},{15,3},{0,4},{1,5},{2,6},{3,7},{4,8},{5,9},{6... | collective-permute-start | bytes 589832 | tf_op jit(solution)/shard_map/ppermute | solution.py:43
  146.6 5.9 %collective-permute-start.20 = (bf16[256,384]{1,0:T(8,128)(2,1)S(1)}, bf16[256,384]{1,0:T(8,128)(2,1)S(1)}, u32[]{:S(2)}, u32[]{:S(2)}) collective-permute-start(bf16[256,384]{1,0:T(8,128)(2,1)S(1)} %slice.100), channel_id=1, source_target_pairs={{4,0},{5,1},{6,2},{7,3},{8,4},{9,5},{10,6},{11,7},{12,8},{13,9},{1... | collective-permute-start | bytes 589832 | tf_op jit(solution)/shard_map/ppermute | solution.py:43
  149.3 7.8 %collective-permute-start.28 = (bf16[384,128]{1,0:T(8,128)(2,1)S(1)}, bf16[384,128]{1,0:T(8,128)(2,1)S(1)}, u32[]{:S(2)}, u32[]{:S(2)}) collective-permute-start(bf16[384,128]{1,0:T(8,128)(2,1)S(1)} %copy-done.6), channel_id=1, source_target_pairs={{0,1},{1,0},{2,3},{3,2},{4,5},{5,4},{6,7},{7,6},{8,9},{9,8},{10,11... | collective-permute-start | bytes 294920 | tf_op jit(solution)/shard_map/ppermute | solution.py:554
  157.0 3.2 %collective-permute-start.29 = (bf16[256,128]{1,0:T(8,128)(2,1)S(1)}, bf16[256,128]{1,0:T(8,128)(2,1)S(1)}, u32[]{:S(2)}, u32[]{:S(2)}) collective-permute-start(bf16[256,128]{1,0:T(8,128)(2,1)S(1)} %get-tuple-element.35.oi), channel_id=1, source_target_pairs={{0,1},{1,0},{2,3},{3,2},{4,5},{5,4},{6,7},{7,6},{8,9},{9,8},{10,11... | collective-permute-start | bytes 196616 | tf_op jit(solution)/shard_map/ppermute | solution.py:561
  171.1 68.1 %copy-start = (bf16[2,480,384]{2,1,0:T(8,128)(2,1)S(1)}, bf16[2,480,384]{2,1,0:T(8,128)(2,1)}, u32[]{:S(2)}) copy-start(bf16[2,480,384]{2,1,0:T(8,128)(2,1)} %text_ref.1) | copy-start | bytes 2211844
  171.1 4.6 %collective-permute-start.30 = (f32[2,6144]{1,0:T(2,128)S(1)}, f32[2,6144]{1,0:T(2,128)S(1)}, u32[]{:S(2)}, u32[]{:S(2)}) collective-permute-start(f32[2,6144]{1,0:T(2,128)S(1)} %convolution_add_fusion), channel_id=1, source_target_pairs={{2,0},{3,1},{0,2},{1,3},{6,4},{7,5},{4,6},{5,7},{10,8},{11,9},{8,1... | collective-permute-start | bytes 147464 | tf_op jit(solution)/shard_map/ppermute | solution.py:43
  171.2 4.7 %collective-permute-start.31 = (f32[2,6144]{1,0:T(2,128)S(1)}, f32[2,6144]{1,0:T(2,128)S(1)}, u32[]{:S(2)}, u32[]{:S(2)}) collective-permute-start(f32[2,6144]{1,0:T(2,128)S(1)} %convolution_add_fusion), channel_id=1, source_target_pairs={{3,0},{0,1},{1,2},{2,3},{7,4},{4,5},{5,6},{6,7},{11,8},{8,9},{9,10... | collective-permute-start | bytes 147464 | tf_op jit(solution)/shard_map/ppermute | solution.py:43
  171.7 4.2 %collective-permute-start.32 = (f32[2,6144]{1,0:T(2,128)S(1)}, f32[2,6144]{1,0:T(2,128)S(1)}, u32[]{:S(2)}, u32[]{:S(2)}) collective-permute-start(f32[2,6144]{1,0:T(2,128)S(1)} %convolution_add_fusion), channel_id=1, source_target_pairs={{1,0},{2,1},{3,2},{0,3},{5,4},{6,5},{7,6},{4,7},{9,8},{10,9},{11,1... | collective-permute-start | bytes 147464 | tf_op jit(solution)/shard_map/ppermute | solution.py:43
  175.9 4.8 %collective-permute-start.33 = (f32[2,6144]{1,0:T(2,128)S(1)}, f32[2,6144]{1,0:T(2,128)S(1)}, u32[]{:S(2)}, u32[]{:S(2)}) collective-permute-start(f32[2,6144]{1,0:T(2,128)S(1)} %add_add_fusion), channel_id=1, source_target_pairs={{8,0},{9,1},{10,2},{11,3},{12,4},{13,5},{14,6},{15,7},{0,8},{1,9},... | collective-permute-start | bytes 147464 | tf_op jit(solution)/shard_map/ppermute | solution.py:43
  177.8 4.4 %collective-permute-start.34 = (f32[2,6144]{1,0:T(2,128)S(1)}, f32[2,6144]{1,0:T(2,128)S(1)}, u32[]{:S(2)}, u32[]{:S(2)}) collective-permute-start(f32[2,6144]{1,0:T(2,128)S(1)} %add_add_fusion), channel_id=1, source_target_pairs={{12,0},{13,1},{14,2},{15,3},{0,4},{1,5},{2,6},{3,7},{4,8},{5,9},{6... | collective-permute-start | bytes 147464 | tf_op jit(solution)/shard_map/ppermute | solution.py:43
  179.4 4.2 %collective-permute-start.35 = (f32[2,6144]{1,0:T(2,128)S(1)}, f32[2,6144]{1,0:T(2,128)S(1)}, u32[]{:S(2)}, u32[]{:S(2)}) collective-permute-start(f32[2,6144]{1,0:T(2,128)S(1)} %add_add_fusion), channel_id=1, source_target_pairs={{4,0},{5,1},{6,2},{7,3},{8,4},{9,5},{10,6},{11,7},{12,8},{13,9},{1... | collective-permute-start | bytes 147464 | tf_op jit(solution)/shard_map/ppermute | solution.py:43
  209.3 4.6 %collective-permute-start.36 = (f32[16]{0:T(128)S(1)}, f32[16]{0:T(128)S(1)}, u32[]{:S(2)}, u32[]{:S(2)}) collective-permute-start(f32[16]{0:T(128)S(1)} %convolution_reduce_fusion), channel_id=1, source_target_pairs={{3,0},{0,1},{1,2},{2,3},{7,4},{4,5},{5,6},{6,7},{11,8},{8,9},{9,10... | collective-permute-start | bytes 200 | tf_op jit(solution)/shard_map/ppermute | solution.py:43
  209.4 4.6 %collective-permute-start.37 = (f32[16]{0:T(128)S(1)}, f32[16]{0:T(128)S(1)}, u32[]{:S(2)}, u32[]{:S(2)}) collective-permute-start(f32[16]{0:T(128)S(1)} %convolution_reduce_fusion), channel_id=1, source_target_pairs={{1,0},{2,1},{3,2},{0,3},{5,4},{6,5},{7,6},{4,7},{9,8},{10,9},{11,1... | collective-permute-start | bytes 200 | tf_op jit(solution)/shard_map/ppermute | solution.py:43
  212.7 4.0 %collective-permute-start.38 = (f32[16]{0:T(128)S(1)}, f32[16]{0:T(128)S(1)}, u32[]{:S(2)}, u32[]{:S(2)}) collective-permute-start(f32[16]{0:T(128)S(1)} %convolution_reduce_fusion), channel_id=1, source_target_pairs={{2,0},{3,1},{0,2},{1,3},{6,4},{7,5},{4,6},{5,7},{10,8},{11,9},{8,1... | collective-permute-start | bytes 200 | tf_op jit(solution)/shard_map/ppermute | solution.py:43
  216.7 4.0 %collective-permute-start.39 = (f32[16]{0:T(128)S(1)}, f32[16]{0:T(128)S(1)}, u32[]{:S(2)}, u32[]{:S(2)}) collective-permute-start(f32[16]{0:T(128)S(1)} %maximum_maximum_fusion.1), channel_id=1, source_target_pairs={{12,0},{13,1},{14,2},{15,3},{0,4},{1,5},{2,6},{3,7},{4,8},{5,9},{6... | collective-permute-start | bytes 200 | tf_op jit(solution)/shard_map/ppermute | solution.py:43
  216.7 4.0 %collective-permute-start.40 = (f32[16]{0:T(128)S(1)}, f32[16]{0:T(128)S(1)}, u32[]{:S(2)}, u32[]{:S(2)}) collective-permute-start(f32[16]{0:T(128)S(1)} %maximum_maximum_fusion.1), channel_id=1, source_target_pairs={{4,0},{5,1},{6,2},{7,3},{8,4},{9,5},{10,6},{11,7},{12,8},{13,9},{1... | collective-permute-start | bytes 200 | tf_op jit(solution)/shard_map/ppermute | solution.py:43
  219.3 4.0 %collective-permute-start.41 = (f32[16]{0:T(128)S(1)}, f32[16]{0:T(128)S(1)}, u32[]{:S(2)}, u32[]{:S(2)}) collective-permute-start(f32[16]{0:T(128)S(1)} %maximum_maximum_fusion.1), channel_id=1, source_target_pairs={{8,0},{9,1},{10,2},{11,3},{12,4},{13,5},{14,6},{15,7},{0,8},{1,9},... | collective-permute-start | bytes 200 | tf_op jit(solution)/shard_map/ppermute | solution.py:43
  (17 other events, 286.6 us)
Sparse Core Ops, SparseCore 0:
  11.5 86.8 all-gather.5
  122.6 34.6 all-gather.9
  167.0 71.6 all-gather.7
